TPU v7x, 128 devices: a whole 4x4x4 slice. The times are simulated.
128 devices in a mesh: depth: 4 (over x), panel: 32 (over y, z, core).
Axes of the slice: x: 4, y: 4, z: 4, core: 2. Of those that a mesh axis runs over, the one named last changes fastest.
Arguments:
- diag_blocks: float32 [4, 1024, 1024], P('depth', 'panel'), as said below
- coupling: float32 [4, 1024, 1024], P('depth', 'panel'), may hold values from -0.078125 to 0.078125
- sources: float32 [4, 1024, 256], P('depth', 'panel'), may hold values from -6 to 6
- requests: int32 [4, 128], P('depth', 'panel'), may hold values from 0 to 1023, as said below
Outputs:
- panels: float32 [4, 1024, 256], P('depth', 'panel')
- picked: float32 [4, 128, 256], P('depth', 'panel')
Inputs may be any that keep to these rules, and one draw needn't show every extreme that they name: `requests`: row numbers within their block; both 0 and 1023 occur. `diag_blocks`: every diagonal block is exactly symmetric with a positive diagonal.
All inputs are finite; a program needn't handle non-finite values.
Results may differ from a plain program's by a relative error of at most 0.0001.
Values sent between devices are 32-bit elements; how exact they have to be, the bound alone decides.
No kernel may reach another device: no remote copies, remote signals or barrier semaphores. Data moves between devices by JAX's collectives and lax.ppermute only.
A program may use at most 64 MiB of HBM per device.

v0:
```python
import functools

import jax
import jax.numpy as jnp
from jax import lax
from jax.experimental import pallas as pl
from jax.experimental.pallas import tpu as pltpu
from jax.sharding import PartitionSpec as P


ITERS = 2
F32, BF16 = jnp.float32, jnp.bfloat16
LANES = 128
SENT_GROUPS = 5

AXES = ((1, 3, 2), (4, 12, 8))
SIBLINGS = [(p, p ^ 1) for p in range(32)]


def from_partner(block, phase, number):
    pairs = [
        (yz * 2 + core, (yz ^ AXES[core ^ phase][number]) * 2 + core)
        for yz in range(16)
        for core in range(2)
    ]
    return lax.ppermute(block, "panel", pairs)


def join_kernel(first, second, both):
    rows = first.shape[0]
    both[:rows] = first[...]
    both[rows:] = second[...]


def joined(first, second):
    return call(join_kernel, vmem((first.shape[0] * 2, first.shape[1])), first, second)


PIECES = (("A", None), ("B", None), ("A", 0), ("A", 1), ("B", 0), ("B", 1), ("A", 2), ("B", 2))


def offset_of(core, piece, unit):
    half, line = piece
    near = AXES[core]
    offset = ((0, near[0]) if half == "A" else (near[1], near[2]))[unit]
    return offset ^ (0 if line is None else AXES[1 - core][line])


def gathered(own):
    near = from_partner(own, 0, 0)
    other = from_partner(own, 0, 1)
    far = from_partner(own, 0, 2)
    a = joined(own, near)
    a1, a0 = from_partner(a, 1, 1), from_partner(a, 1, 0)
    b = joined(other, far)
    b0, b1 = from_partner(b, 1, 0), from_partner(b, 1, 1)
    a2, b2 = from_partner(a1, 1, 0), from_partner(b0, 1, 1)
    pieces = [a, b, a0, a1, b0, b1, a2, b2]
    return pieces + [lax.ppermute(piece, "panel", SIBLINGS) for piece in pieces]


def split(x):
    high = x.astype(BF16)
    return high, (x - high.astype(F32)).astype(BF16)


def product(x, high_ref, low_ref, transposed=False):
    rows = x.shape[0]
    both = jnp.concatenate(split(x), 0)
    dims = (((1,), (1 if transposed else 0,)), ((), ()))
    first = lax.dot_general(both, high_ref[...], dims, preferred_element_type=F32)
    second = lax.dot_general(both, low_ref[...], dims, preferred_element_type=F32)
    total = first + second
    return total[:rows] + total[rows:]


def jacobi(right_hand, diag, d_high, d_low):
    iterate = right_hand / diag
    for _ in range(ITERS):
        image = product(iterate, d_high, d_low)
        iterate = iterate + (right_hand - image) / diag
    return iterate


def pack_kernel(asked, diag_rows, coupling_rows, source_rows, packed, requests, sems):
    few = requests.shape[1]
    fetch = pltpu.make_async_copy(asked, requests, sems.at[2 + SENT_GROUPS])
    fetch.start()
    count, size = diag_rows.shape
    cols = source_rows.shape[1]
    sent = [(coupling_rows, size), (source_rows, cols)]
    group = lax.div(lax.axis_index("panel") * count, LANES)
    for k in range(SENT_GROUPS):
        start = lax.rem(group + k, size // LANES) * LANES
        sent.append((diag_rows.at[:, pl.ds(pl.multiple_of(start, LANES), LANES)], LANES))
    copies = []
    at = 0
    for number, (rows, width) in enumerate(sent):
        copies.append(
            pltpu.make_async_copy(rows, packed.at[:, at : at + width], sems.at[number])
        )
        copies[-1].start()
        at += width
    fetch.wait()
    row = lax.broadcasted_iota(jnp.int32, (count, LANES), 0)
    lane = lax.broadcasted_iota(jnp.int32, (count, LANES), 1)
    slots = jnp.zeros((count, LANES), F32)
    for k in range(few):
        here = (row == 0) & (lane == lax.axis_index("panel") * few + k)
        slots = jnp.where(here, requests[0, k].astype(F32), slots)
    packed[:, at:] = slots
    for copy in copies:
        copy.wait()


def first_kernel(*refs, size, cols):
    pieces = refs[:16]
    d_high, d_low, c_high, c_low, source, diag, wanted, side = refs[16:]
    me = lax.axis_index("panel")
    core = lax.rem(me, 2)
    place = lax.div(me, 2)
    unit_rows = size // 32
    step = 16
    groups = size // LANES

    def move(piece, start, to):
        def body(i, _):
            rows = pl.ds(pl.multiple_of(to + i * step, step), step)
            held = piece.at[pl.ds(pl.multiple_of(start + i * step, step), step)]
            c_high[rows, :], c_low[rows, :] = split(held[:, 0:size])
            side[rows, 0:cols] = held[:, size : size + cols]
            for k in range(SENT_GROUPS):
                at = lax.rem(lax.div(to, LANES) + k, groups) * LANES
                where = pl.ds(pl.multiple_of(at, LANES), LANES)
                own = size + cols + k * LANES
                d_high[rows, where], d_low[rows, where] = split(held[:, own : own + LANES])
            side[rows, cols:] = held[:, size + cols + SENT_GROUPS * LANES :]
            return 0

        lax.fori_loop(0, unit_rows // step, body, 0)

    for number in range(16):
        sibling = number // 8
        for unit in range(2):
            piece = PIECES[number % 8]
            offset = jnp.where(
                core == sibling, offset_of(0, piece, unit), offset_of(1, piece, unit)
            )
            owner = lax.bitwise_xor(place, offset) * 2 + lax.bitwise_xor(core, sibling)
            move(pieces[number], unit * unit_rows, owner * unit_rows)

    for group in range(groups):
        for k in range(1, groups - SENT_GROUPS + 1):
            rows = slice(group * LANES, (group + 1) * LANES)
            where = (group + k) % groups * LANES
            where = slice(where, where + LANES)
            block = d_high[rows, where].astype(F32) + d_low[rows, where].astype(F32)
            d_high[where, rows], d_low[where, rows] = split(block.T)

    pick = lax.broadcasted_iota(jnp.int32, (8, cols), 1) == (
        lax.broadcasted_iota(jnp.int32, (8, cols), 0) + me * 8
    )
    own = lax.dot_general(
        pick.astype(F32),
        side[:, 0:cols],
        (((1,), (1,)), ((), ())),
        precision=lax.Precision.HIGHEST,
        preferred_element_type=F32,
    )
    source[...] = own
    eye = lax.broadcasted_iota(jnp.int32, (LANES, LANES), 0) == lax.broadcasted_iota(
        jnp.int32, (LANES, LANES), 1
    )
    for start in range(0, size, LANES):
        tiles = slice(start, start + LANES)
        tile = d_high[tiles, tiles].astype(F32) + d_low[tiles, tiles].astype(F32)
        line = jnp.sum(jnp.where(eye, tile, 0.0), axis=0, keepdims=True)
        diag[:, start : start + LANES] = jnp.broadcast_to(line, (8, LANES))
    line = jnp.sum(side[:, cols : cols + LANES], axis=0, keepdims=True)
    wanted[...] = jnp.broadcast_to(line, (8, LANES))


def hop(block, here, there):
    other = [k for k in range(4) if k not in (here, there)]
    route = [(here, there), (there, here), tuple(other), tuple(other[::-1])]
    return lax.ppermute(block, "depth", route)


def taken(plane, planes, refs):
    total = jnp.zeros_like(refs[0])
    for meant, ref in zip(planes, refs):
        total = jnp.where(plane == meant, ref[...], total)
    return total


def forward_kernel(stage, d_high, d_low, c_high, c_low, source, diag, *refs):
    @pl.when(lax.axis_index("depth") == stage)
    def _():
        right_hand = source[...] - refs[0][...] if stage else source[...]
        forward = jacobi(right_hand, diag[...], d_high, d_low)
        refs[-1][...] = product(forward, c_high, c_low)


def turn_kernel(count, d_high, d_low, source, diag, *refs):
    right_hand = source[...] - taken(lax.axis_index("depth"), range(1, count + 1), refs[:count])
    refs[count][...] = right_hand

    @pl.when(lax.axis_index("depth") == count)
    def _():
        refs[count + 1][...] = jacobi(right_hand, diag[...], d_high, d_low)


def backward_kernel(plane, d_high, d_low, c_high, c_low, right_hand, diag, ahead, panel):
    @pl.when(lax.axis_index("depth") == plane)
    def _():
        rest = right_hand[...] - product(ahead[...], c_high, c_low, True)
        panel[...] = jacobi(rest, diag[...], d_high, d_low)


def last_kernel(count, d_high, d_low, c_high, c_low, right_hand, diag, wanted, *refs):
    ahead = taken(lax.axis_index("depth"), range(count - 1, -1, -1), refs[:count])
    rest = right_hand[...] - product(ahead, c_high, c_low, True)
    panel = jacobi(rest, diag[...], d_high, d_low)
    size = panel.shape[1]
    high = panel.astype(BF16)
    rest = panel - high.astype(F32)
    middle = rest.astype(BF16)
    low = (rest - middle.astype(F32)).astype(BF16)
    line = wanted[0:1, :].astype(jnp.int32)
    chosen = (lax.broadcasted_iota(jnp.int32, (size, LANES), 0) == line).astype(BF16)
    parts = [jnp.dot(part, chosen, preferred_element_type=F32) for part in (high, middle, low)]
    picked = parts[0] + parts[1] + parts[2]
    send = refs[count]
    blocks = send.shape[0]
    own, few = size // blocks, LANES // blocks
    filler = jnp.zeros((8, LANES - own - few), F32)
    for block in range(blocks):
        send[block] = jnp.concatenate(
            [
                panel[:, block * own : (block + 1) * own],
                picked[:, block * few : (block + 1) * few],
                filler,
            ],
            1,
        )


def unpack_kernel(got, panels, picked):
    turned = got[...].T
    own = panels.shape[0]
    panels[...] = turned[:own]
    picked[...] = turned[own : own + picked.shape[0]]


def vmem(shape, dtype=F32):
    return pltpu.VMEM(shape, dtype)


def call(kernel, out_shape, *args, scratch=(), limit=8):
    args = [pltpu.with_memory_space_constraint(arg, pltpu.VMEM) for arg in args]
    space = pl.BlockSpec(memory_space=pltpu.VMEM)
    return pl.pallas_call(
        kernel,
        out_shape=out_shape,
        in_specs=[space] * len(args),
        out_specs=jax.tree.map(lambda _: space, out_shape),
        scratch_shapes=scratch,
        compiler_params=pltpu.CompilerParams(vmem_limit_bytes=limit * 1024 * 1024),
    )(*args)


def per_device(diag_blocks, coupling, sources, requests):
    rows, size, cols = diag_blocks.shape[1], diag_blocks.shape[2], sources.shape[2]
    few = requests.shape[1]
    width = size + cols + (SENT_GROUPS + 1) * LANES
    far = pl.BlockSpec(memory_space=pltpu.HBM)
    operands = (requests, diag_blocks[0], coupling[0], sources[0])
    packed = pl.pallas_call(
        pack_kernel,
        out_shape=vmem((rows, width)),
        in_specs=[far] * 4,
        out_specs=pl.BlockSpec(memory_space=pltpu.VMEM),
        scratch_shapes=[pltpu.SMEM(requests.shape, jnp.int32), pltpu.SemaphoreType.DMA((3 + SENT_GROUPS,))],
        compiler_params=pltpu.CompilerParams(vmem_limit_bytes=8 * 1024 * 1024),
    )(*[pltpu.with_memory_space_constraint(x, pltpu.HBM) for x in operands])
    pieces = gathered(packed)

    vec = vmem((8, size))
    mat = vmem((size, size), BF16)
    d_high, d_low, c_high, c_low, source, diag, wanted = call(
        functools.partial(first_kernel, size=size, cols=cols),
        (mat, mat, mat, mat, vec, vec, vmem((8, LANES))),
        *pieces,
        scratch=[pltpu.VMEM((size, cols + LANES), F32)],
    )
    mats = (d_high, d_low, c_high, c_low)

    last = 3
    lefts = []
    for k in range(last):
        carried = call(
            functools.partial(forward_kernel, k),
            vec, *mats, source, diag, *lefts[-1:],
        )
        lefts.append(hop(carried, k, k + 1))
    right_hand, panel = call(
        functools.partial(turn_kernel, last),
        (vec, vec), d_high, d_low, source, diag, *lefts,
    )
    aheads = []
    for k in range(last - 1, -1, -1):
        aheads.append(hop(panel, k + 1, k))
        if k > 0:
            panel = call(
                functools.partial(backward_kernel, k),
                vec, *mats, right_hand, diag, aheads[-1],
            )
    send = call(
        functools.partial(last_kernel, last),
        vmem((size // rows, 8, LANES)),
        *mats, right_hand, diag, wanted, *aheads,
    )
    got = lax.all_to_all(send, "panel", 0, 0, tiled=True).reshape(cols, LANES)
    panels, picked = call(
        unpack_kernel,
        (jax.ShapeDtypeStruct((rows, cols), F32), jax.ShapeDtypeStruct((few, cols), F32)),
        got,
    )
    return panels[None], picked[None]


def solution(mesh):
    placed = (
        P("depth", "panel", None),
        P("depth", "panel", None),
        P("depth", "panel", None),
        P("depth", "panel"),
    )
    return jax.shard_map(
        per_device,
        mesh=mesh,
        in_specs=placed,
        out_specs=(P("depth", "panel", None), P("depth", "panel", None)),
        check_vma=False,
    )
```

profile of v0, /device:TPU:1, one launch (start us, length us, event | category | flops | bytes accessed | tf_op | source)
XLA Modules:
  0.0 90.8 jit_solution(5300164302754983693)
XLA Ops:
  1.6 2.2 %collective-permute-start = (f32[32,2048]{1,0:T(8,128)S(1)}, f32[32,2048]{1,0:T(8,128)S(1)}, u32[]{:S(2)}, u32[]{:S(2)}) collective-permute-start(f32[32,2048]{1,0:T(8,128)S(1)} %shard_map.59.first), channel_id=1, source_target_pairs={{0,2},{1,9},{2,0},{3,11},{4,6},{5,13},{6,4},{7,15},{8,10},{9,1},{1... | collective-permute-start | bytes 786440 | tf_op jit(solution)/shard_map/ppermute | solution.py:26
  3.8 2.6 %collective-permute-start.2 = (f32[32,2048]{1,0:T(8,128)S(1)}, f32[32,2048]{1,0:T(8,128)S(1)}, u32[]{:S(2)}, u32[]{:S(2)}) collective-permute-start(f32[32,2048]{1,0:T(8,128)S(1)} %shard_map.59.first), channel_id=1, source_target_pairs={{0,4},{1,17},{2,6},{3,19},{4,0},{5,21},{6,2},{7,23},{8,12},{9,25},... | collective-permute-start | bytes 786440 | tf_op jit(solution)/shard_map/ppermute | solution.py:26
  7.9 1.7 %collective-permute-start.9 = (f32[64,2048]{1,0:T(8,128)S(1)}, f32[64,2048]{1,0:T(8,128)S(1)}, u32[]{:S(2)}, u32[]{:S(2)}) collective-permute-start(f32[64,2048]{1,0:T(8,128)S(1)} %shard_map.60.refs_0_), channel_id=1, source_target_pairs={{0,1},{1,0},{2,3},{3,2},{4,5},{5,4},{6,7},{7,6},{8,9},{9,8},{10,11... | collective-permute-start | bytes 1572872 | tf_op jit(solution)/shard_map/ppermute | solution.py:59
  9.6 3.9 %collective-permute-start.4 = (f32[64,2048]{1,0:T(8,128)S(1)}, f32[64,2048]{1,0:T(8,128)S(1)}, u32[]{:S(2)}, u32[]{:S(2)}) collective-permute-start(f32[64,2048]{1,0:T(8,128)S(1)} %shard_map.60.refs_0_), channel_id=1, source_target_pairs={{0,24},{1,7},{2,26},{3,5},{4,28},{5,3},{6,30},{7,1},{8,16},{9,15},... | collective-permute-start | bytes 1572872 | tf_op jit(solution)/shard_map/ppermute | solution.py:26
  13.5 4.4 %collective-permute-done.1.first = f32[32,2048]{1,0:T(8,128)S(1)} collective-permute-done((f32[32,2048]{1,0:T(8,128)S(1)}, f32[32,2048]{1,0:T(8,128)S(1)}, u32[]{:S(2)}, u32[]{:S(2)}) %collective-permute-start.1) | collective-permute-done | bytes 262176 | tf_op jit(solution)/shard_map/ppermute | solution.py:26
  19.5 3.5 %collective-permute-start.10 = (f32[64,2048]{1,0:T(8,128)S(1)}, f32[64,2048]{1,0:T(8,128)S(1)}, u32[]{:S(2)}, u32[]{:S(2)}) collective-permute-start(f32[64,2048]{1,0:T(8,128)S(1)} %shard_map.61.refs_1_), channel_id=1, source_target_pairs={{0,1},{1,0},{2,3},{3,2},{4,5},{5,4},{6,7},{7,6},{8,9},{9,8},{10,11... | collective-permute-start | bytes 1572872 | tf_op jit(solution)/shard_map/ppermute | solution.py:59
  23.6 1.7 %collective-permute-start.12 = (f32[64,2048]{1,0:T(8,128)S(1)}, f32[64,2048]{1,0:T(8,128)S(1)}, u32[]{:S(2)}, u32[]{:S(2)}) collective-permute-start(f32[64,2048]{1,0:T(8,128)S(1)} %collective-permute-done.4.refs_3_), channel_id=1, source_target_pairs={{0,1},{1,0},{2,3},{3,2},{4,5},{5,4},{6,7},{7,6},{8,9},{9,8},{10,11... | collective-permute-start | bytes 1572872 | tf_op jit(solution)/shard_map/ppermute | solution.py:59
  25.3 2.1 %collective-permute-done.5.refs_4_ = f32[64,2048]{1,0:T(8,128)S(1)} collective-permute-done((f32[64,2048]{1,0:T(8,128)S(1)}, f32[64,2048]{1,0:T(8,128)S(1)}, u32[]{:S(2)}, u32[]{:S(2)}) %collective-permute-start.5) | collective-permute-done | bytes 524320 | tf_op jit(solution)/shard_map/ppermute | solution.py:26
  27.4 2.6 %collective-permute-start.8 = (f32[64,2048]{1,0:T(8,128)S(1)}, f32[64,2048]{1,0:T(8,128)S(1)}, u32[]{:S(2)}, u32[]{:S(2)}) collective-permute-start(f32[64,2048]{1,0:T(8,128)S(1)} %collective-permute-done.5.refs_4_), channel_id=1, source_target_pairs={{0,24},{1,7},{2,26},{3,5},{4,28},{5,3},{6,30},{7,1},{8,16},{9,15},... | collective-permute-start | bytes 1572872 | tf_op jit(solution)/shard_map/ppermute | solution.py:26
  30.0 3.7 %collective-permute-start.13 = (f32[64,2048]{1,0:T(8,128)S(1)}, f32[64,2048]{1,0:T(8,128)S(1)}, u32[]{:S(2)}, u32[]{:S(2)}) collective-permute-start(f32[64,2048]{1,0:T(8,128)S(1)} %collective-permute-done.5.refs_4_), channel_id=1, source_target_pairs={{0,1},{1,0},{2,3},{3,2},{4,5},{5,4},{6,7},{7,6},{8,9},{9,8},{10,11... | collective-permute-start | bytes 1572872 | tf_op jit(solution)/shard_map/ppermute | solution.py:59
  34.2 2.1 %collective-permute-start.15 = (f32[64,2048]{1,0:T(8,128)S(1)}, f32[64,2048]{1,0:T(8,128)S(1)}, u32[]{:S(2)}, u32[]{:S(2)}) collective-permute-start(f32[64,2048]{1,0:T(8,128)S(1)} %collective-permute-done.7.refs_6_), channel_id=1, source_target_pairs={{0,1},{1,0},{2,3},{3,2},{4,5},{5,4},{6,7},{7,6},{8,9},{9,8},{10,11... | collective-permute-start | bytes 1572872 | tf_op jit(solution)/shard_map/ppermute | solution.py:59
  36.3 1.9 %collective-permute-done.8.refs_7_ = f32[64,2048]{1,0:T(8,128)S(1)} collective-permute-done((f32[64,2048]{1,0:T(8,128)S(1)}, f32[64,2048]{1,0:T(8,128)S(1)}, u32[]{:S(2)}, u32[]{:S(2)}) %collective-permute-start.8) | collective-permute-done | bytes 524320 | tf_op jit(solution)/shard_map/ppermute | solution.py:26
  38.2 2.8 %collective-permute-start.16 = (f32[64,2048]{1,0:T(8,128)S(1)}, f32[64,2048]{1,0:T(8,128)S(1)}, u32[]{:S(2)}, u32[]{:S(2)}) collective-permute-start(f32[64,2048]{1,0:T(8,128)S(1)} %collective-permute-done.8.refs_7_), channel_id=1, source_target_pairs={{0,1},{1,0},{2,3},{3,2},{4,5},{5,4},{6,7},{7,6},{8,9},{9,8},{10,11... | collective-permute-start | bytes 1572872 | tf_op jit(solution)/shard_map/ppermute | solution.py:59
  42.6 2.9 %shard_map.62 = (bf16[1024,1024]{1,0:T(8,128)(2,1)S(1)}, bf16[1024,1024]{1,0:T(8,128)(2,1)S(1)}, bf16[1024,1024]{1,0:T(8,128)(2,1)S(1)}, bf16[1024,1024]{1,0:T(8...) custom-call(f32[64,2048]{1,0:T(8,128)S(1)} %shard_map.60.refs_0_, ...), custom_call_target="tpu_custom_call" | custom-call | tf_op jit(solution)/shard_map/pallas_call | solution.py:262
  45.5 1.8 %shard_map.63 = f32[8,1024]{1,0:T(8,128)S(1)} custom-call(bf16[1024,1024]{1,0:T(8,128)(2,1)S(1)} %get-tuple-element.13.d_high, bf16[1024,1024]{1,0:T(8,128)(2,1)S(1)} %get-tuple-element.14.d_low, bf16[1024,1024]{1,0:T(8,128)(2,1)S(1)} %get-tuple-element.15.c_high, bf16[1024,1024]{1,0:T(8,128)(2,1)S(1)} %get-tuple-element.16.c_low, ...), custom_call_target="tpu_custom_call" | custom-call | tf_op jit(solution)/shard_map/pallas_call | solution.py:262
  47.3 2.8 %collective-permute-done.17.refs_0_ = f32[8,1024]{1,0:T(8,128)S(1)} collective-permute-done((f32[8,1024]{1,0:T(8,128)S(1)}, f32[8,1024]{1,0:T(8,128)S(1)}, u32[]{:S(2)}, u32[]{:S(2)}) %collective-permute-start.17) | collective-permute-done | bytes 32800 | tf_op jit(solution)/shard_map/ppermute | solution.py:186
  50.9 3.2 %collective-permute-done.18.refs_0_.refs_1_ = f32[8,1024]{1,0:T(8,128)S(1)} collective-permute-done((f32[8,1024]{1,0:T(8,128)S(1)}, f32[8,1024]{1,0:T(8,128)S(1)}, u32[]{:S(2)}, u32[]{:S(2)}) %collective-permute-start.18) | collective-permute-done | bytes 32800 | tf_op jit(solution)/shard_map/ppermute | solution.py:186
  54.7 2.2 %collective-permute-done.19.refs_2_ = f32[8,1024]{1,0:T(8,128)S(1)} collective-permute-done((f32[8,1024]{1,0:T(8,128)S(1)}, f32[8,1024]{1,0:T(8,128)S(1)}, u32[]{:S(2)}, u32[]{:S(2)}) %collective-permute-start.19) | collective-permute-done | bytes 32800 | tf_op jit(solution)/shard_map/ppermute | solution.py:186
  57.5 2.5 %collective-permute-done.20.ahead.refs_0_ = f32[8,1024]{1,0:T(8,128)S(1)} collective-permute-done((f32[8,1024]{1,0:T(8,128)S(1)}, f32[8,1024]{1,0:T(8,128)S(1)}, u32[]{:S(2)}, u32[]{:S(2)}) %collective-permute-start.20) | collective-permute-done | bytes 32800 | tf_op jit(solution)/shard_map/ppermute | solution.py:186
  60.1 2.3 %collective-permute-start.21 = (f32[8,1024]{1,0:T(8,128)S(1)}, f32[8,1024]{1,0:T(8,128)S(1)}, u32[]{:S(2)}, u32[]{:S(2)}) collective-permute-start(f32[8,1024]{1,0:T(8,128)S(1)} %shard_map.67), channel_id=1, source_target_pairs={{64,32},{32,64},{0,96},{96,0},{65,33},{33,65},{1,97},{97,1},{66,34... | collective-permute-start | bytes 98312 | tf_op jit(solution)/shard_map/ppermute | solution.py:186
  62.4 1.7 %collective-permute-done.21.ahead.refs_1_ = f32[8,1024]{1,0:T(8,128)S(1)} collective-permute-done((f32[8,1024]{1,0:T(8,128)S(1)}, f32[8,1024]{1,0:T(8,128)S(1)}, u32[]{:S(2)}, u32[]{:S(2)}) %collective-permute-start.21) | collective-permute-done | bytes 32800 | tf_op jit(solution)/shard_map/ppermute | solution.py:186
  64.1 4.1 %collective-permute-start.22 = (f32[8,1024]{1,0:T(8,128)S(1)}, f32[8,1024]{1,0:T(8,128)S(1)}, u32[]{:S(2)}, u32[]{:S(2)}) collective-permute-start(f32[8,1024]{1,0:T(8,128)S(1)} %shard_map.68), channel_id=1, source_target_pairs={{32,0},{0,32},{64,96},{96,64},{33,1},{1,33},{65,97},{97,65},{34,2}... | collective-permute-start | bytes 98312 | tf_op jit(solution)/shard_map/ppermute | solution.py:186
  69.5 2.6 %shard_map.69 = f32[32,8,128]{2,1,0:T(8,128)S(1)} custom-call(bf16[1024,1024]{1,0:T(8,128)(2,1)S(1)} %get-tuple-element.13.d_high, bf16[1024,1024]{1,0:T(8,128)(2,1)S(1)} %get-tuple-element.14.d_low, bf16[1024,1024]{1,0:T(8,128)(2,1)S(1)} %get-tuple-element.15.c_high, bf16[1024,1024]{1,0:T(8,128)(2,1)S(1)} %get-tuple-element.16.c_low, ...), custom_call_target="tpu_custom_call" | custom-call | tf_op jit(solution)/shard_map/pallas_call | solution.py:262
  72.1 18.0 %all_to_all.5 = f32[32,8,128]{2,1,0:T(8,128)S(1)} all-to-all(f32[32,8,128]{2,1,0:T(8,128)S(1)} %shard_map.69), channel_id=1, replica_groups=mesh['depth'=4,'panel'=32] {'panel'}, dimensions={0} | all-to-all | bytes 262144 | tf_op jit(solution)/shard_map/all_to_all | solution.py:323
  (35 shorter events, 10.8 us)
Async XLA Ops:
  1.6 6.3 %collective-permute-start = (f32[32,2048]{1,0:T(8,128)S(1)}, f32[32,2048]{1,0:T(8,128)S(1)}, u32[]{:S(2)}, u32[]{:S(2)}) collective-permute-start(f32[32,2048]{1,0:T(8,128)S(1)} %shard_map.59.first), channel_id=1, source_target_pairs={{0,2},{1,9},{2,0},{3,11},{4,6},{5,13},{6,4},{7,15},{8,10},{9,1},{1... | collective-permute-start | bytes 786440 | tf_op jit(solution)/shard_map/ppermute | solution.py:26
  3.8 9.6 %collective-permute-start.2 = (f32[32,2048]{1,0:T(8,128)S(1)}, f32[32,2048]{1,0:T(8,128)S(1)}, u32[]{:S(2)}, u32[]{:S(2)}) collective-permute-start(f32[32,2048]{1,0:T(8,128)S(1)} %shard_map.59.first), channel_id=1, source_target_pairs={{0,4},{1,17},{2,6},{3,19},{4,0},{5,21},{6,2},{7,23},{8,12},{9,25},... | collective-permute-start | bytes 786440 | tf_op jit(solution)/shard_map/ppermute | solution.py:26
  6.4 11.5 %collective-permute-start.1 = (f32[32,2048]{1,0:T(8,128)S(1)}, f32[32,2048]{1,0:T(8,128)S(1)}, u32[]{:S(2)}, u32[]{:S(2)}) collective-permute-start(f32[32,2048]{1,0:T(8,128)S(1)} %shard_map.59.first), channel_id=1, source_target_pairs={{0,6},{1,25},{2,4},{3,27},{4,2},{5,29},{6,0},{7,31},{8,14},{9,17},... | collective-permute-start | bytes 786440 | tf_op jit(solution)/shard_map/ppermute | solution.py:26
  7.9 15.2 %collective-permute-start.9 = (f32[64,2048]{1,0:T(8,128)S(1)}, f32[64,2048]{1,0:T(8,128)S(1)}, u32[]{:S(2)}, u32[]{:S(2)}) collective-permute-start(f32[64,2048]{1,0:T(8,128)S(1)} %shard_map.60.refs_0_), channel_id=1, source_target_pairs={{0,1},{1,0},{2,3},{3,2},{4,5},{5,4},{6,7},{7,6},{8,9},{9,8},{10,11... | collective-permute-start | bytes 1572872 | tf_op jit(solution)/shard_map/ppermute | solution.py:59
  9.6 14.0 %collective-permute-start.4 = (f32[64,2048]{1,0:T(8,128)S(1)}, f32[64,2048]{1,0:T(8,128)S(1)}, u32[]{:S(2)}, u32[]{:S(2)}) collective-permute-start(f32[64,2048]{1,0:T(8,128)S(1)} %shard_map.60.refs_0_), channel_id=1, source_target_pairs={{0,24},{1,7},{2,26},{3,5},{4,28},{5,3},{6,30},{7,1},{8,16},{9,15},... | collective-permute-start | bytes 1572872 | tf_op jit(solution)/shard_map/ppermute | solution.py:26
  13.4 11.8 %collective-permute-start.3 = (f32[64,2048]{1,0:T(8,128)S(1)}, f32[64,2048]{1,0:T(8,128)S(1)}, u32[]{:S(2)}, u32[]{:S(2)}) collective-permute-start(f32[64,2048]{1,0:T(8,128)S(1)} %shard_map.60.refs_0_), channel_id=1, source_target_pairs={{0,8},{1,3},{2,10},{3,1},{4,12},{5,7},{6,14},{7,5},{8,0},{9,11},{1... | collective-permute-start | bytes 1572872 | tf_op jit(solution)/shard_map/ppermute | solution.py:26
  17.9 9.5 %collective-permute-start.5 = (f32[64,2048]{1,0:T(8,128)S(1)}, f32[64,2048]{1,0:T(8,128)S(1)}, u32[]{:S(2)}, u32[]{:S(2)}) collective-permute-start(f32[64,2048]{1,0:T(8,128)S(1)} %shard_map.61.refs_1_), channel_id=1, source_target_pairs={{0,8},{1,3},{2,10},{3,1},{4,12},{5,7},{6,14},{7,5},{8,0},{9,11},{1... | collective-permute-start | bytes 1572872 | tf_op jit(solution)/shard_map/ppermute | solution.py:26
  19.5 10.4 %collective-permute-start.10 = (f32[64,2048]{1,0:T(8,128)S(1)}, f32[64,2048]{1,0:T(8,128)S(1)}, u32[]{:S(2)}, u32[]{:S(2)}) collective-permute-start(f32[64,2048]{1,0:T(8,128)S(1)} %shard_map.61.refs_1_), channel_id=1, source_target_pairs={{0,1},{1,0},{2,3},{3,2},{4,5},{5,4},{6,7},{7,6},{8,9},{9,8},{10,11... | collective-permute-start | bytes 1572872 | tf_op jit(solution)/shard_map/ppermute | solution.py:59
  23.1 10.6 %collective-permute-start.6 = (f32[64,2048]{1,0:T(8,128)S(1)}, f32[64,2048]{1,0:T(8,128)S(1)}, u32[]{:S(2)}, u32[]{:S(2)}) collective-permute-start(f32[64,2048]{1,0:T(8,128)S(1)} %shard_map.61.refs_1_), channel_id=1, source_target_pairs={{0,24},{1,7},{2,26},{3,5},{4,28},{5,3},{6,30},{7,1},{8,16},{9,15},... | collective-permute-start | bytes 1572872 | tf_op jit(solution)/shard_map/ppermute | solution.py:26
  23.6 10.2 %collective-permute-start.12 = (f32[64,2048]{1,0:T(8,128)S(1)}, f32[64,2048]{1,0:T(8,128)S(1)}, u32[]{:S(2)}, u32[]{:S(2)}) collective-permute-start(f32[64,2048]{1,0:T(8,128)S(1)} %collective-permute-done.4.refs_3_), channel_id=1, source_target_pairs={{0,1},{1,0},{2,3},{3,2},{4,5},{5,4},{6,7},{7,6},{8,9},{9,8},{10,11... | collective-permute-start | bytes 1572872 | tf_op jit(solution)/shard_map/ppermute | solution.py:59
  25.3 8.9 %collective-permute-start.7 = (f32[64,2048]{1,0:T(8,128)S(1)}, f32[64,2048]{1,0:T(8,128)S(1)}, u32[]{:S(2)}, u32[]{:S(2)}) collective-permute-start(f32[64,2048]{1,0:T(8,128)S(1)} %collective-permute-done.4.refs_3_), channel_id=1, source_target_pairs={{0,8},{1,3},{2,10},{3,1},{4,12},{5,7},{6,14},{7,5},{8,0},{9,11},{1... | collective-permute-start | bytes 1572872 | tf_op jit(solution)/shard_map/ppermute | solution.py:26
  27.4 10.8 %collective-permute-start.8 = (f32[64,2048]{1,0:T(8,128)S(1)}, f32[64,2048]{1,0:T(8,128)S(1)}, u32[]{:S(2)}, u32[]{:S(2)}) collective-permute-start(f32[64,2048]{1,0:T(8,128)S(1)} %collective-permute-done.5.refs_4_), channel_id=1, source_target_pairs={{0,24},{1,7},{2,26},{3,5},{4,28},{5,3},{6,30},{7,1},{8,16},{9,15},... | collective-permute-start | bytes 1572872 | tf_op jit(solution)/shard_map/ppermute | solution.py:26
  30.0 11.1 %collective-permute-start.13 = (f32[64,2048]{1,0:T(8,128)S(1)}, f32[64,2048]{1,0:T(8,128)S(1)}, u32[]{:S(2)}, u32[]{:S(2)}) collective-permute-start(f32[64,2048]{1,0:T(8,128)S(1)} %collective-permute-done.5.refs_4_), channel_id=1, source_target_pairs={{0,1},{1,0},{2,3},{3,2},{4,5},{5,4},{6,7},{7,6},{8,9},{9,8},{10,11... | collective-permute-start | bytes 1572872 | tf_op jit(solution)/shard_map/ppermute | solution.py:59
  33.7 7.4 %collective-permute-start.11 = (f32[64,2048]{1,0:T(8,128)S(1)}, f32[64,2048]{1,0:T(8,128)S(1)}, u32[]{:S(2)}, u32[]{:S(2)}) collective-permute-start(f32[64,2048]{1,0:T(8,128)S(1)} %collective-permute-done.3.refs_2_), channel_id=1, source_target_pairs={{0,1},{1,0},{2,3},{3,2},{4,5},{5,4},{6,7},{7,6},{8,9},{9,8},{10,11... | collective-permute-start | bytes 1572872 | tf_op jit(solution)/shard_map/ppermute | solution.py:59
  33.8 7.3 %collective-permute-start.14 = (f32[64,2048]{1,0:T(8,128)S(1)}, f32[64,2048]{1,0:T(8,128)S(1)}, u32[]{:S(2)}, u32[]{:S(2)}) collective-permute-start(f32[64,2048]{1,0:T(8,128)S(1)} %collective-permute-done.6.refs_5_), channel_id=1, source_target_pairs={{0,1},{1,0},{2,3},{3,2},{4,5},{5,4},{6,7},{7,6},{8,9},{9,8},{10,11... | collective-permute-start | bytes 1572872 | tf_op jit(solution)/shard_map/ppermute | solution.py:59
  34.2 6.9 %collective-permute-start.15 = (f32[64,2048]{1,0:T(8,128)S(1)}, f32[64,2048]{1,0:T(8,128)S(1)}, u32[]{:S(2)}, u32[]{:S(2)}) collective-permute-start(f32[64,2048]{1,0:T(8,128)S(1)} %collective-permute-done.7.refs_6_), channel_id=1, source_target_pairs={{0,1},{1,0},{2,3},{3,2},{4,5},{5,4},{6,7},{7,6},{8,9},{9,8},{10,11... | collective-permute-start | bytes 1572872 | tf_op jit(solution)/shard_map/ppermute | solution.py:59
  38.2 4.4 %collective-permute-start.16 = (f32[64,2048]{1,0:T(8,128)S(1)}, f32[64,2048]{1,0:T(8,128)S(1)}, u32[]{:S(2)}, u32[]{:S(2)}) collective-permute-start(f32[64,2048]{1,0:T(8,128)S(1)} %collective-permute-done.8.refs_7_), channel_id=1, source_target_pairs={{0,1},{1,0},{2,3},{3,2},{4,5},{5,4},{6,7},{7,6},{8,9},{9,8},{10,11... | collective-permute-start | bytes 1572872 | tf_op jit(solution)/shard_map/ppermute | solution.py:59
  47.3 2.8 %collective-permute-start.17 = (f32[8,1024]{1,0:T(8,128)S(1)}, f32[8,1024]{1,0:T(8,128)S(1)}, u32[]{:S(2)}, u32[]{:S(2)}) collective-permute-start(f32[8,1024]{1,0:T(8,128)S(1)} %shard_map.63), channel_id=1, source_target_pairs={{0,32},{32,0},{64,96},{96,64},{1,33},{33,1},{65,97},{97,65},{2,34}... | collective-permute-start | bytes 98312 | tf_op jit(solution)/shard_map/ppermute | solution.py:186
  50.1 4.0 %collective-permute-start.18 = (f32[8,1024]{1,0:T(8,128)S(1)}, f32[8,1024]{1,0:T(8,128)S(1)}, u32[]{:S(2)}, u32[]{:S(2)}) collective-permute-start(f32[8,1024]{1,0:T(8,128)S(1)} %shard_map.64), channel_id=1, source_target_pairs={{32,64},{64,32},{0,96},{96,0},{33,65},{65,33},{1,97},{97,1},{34,66... | collective-permute-start | bytes 98312 | tf_op jit(solution)/shard_map/ppermute | solution.py:186
  54.1 2.8 %collective-permute-start.19 = (f32[8,1024]{1,0:T(8,128)S(1)}, f32[8,1024]{1,0:T(8,128)S(1)}, u32[]{:S(2)}, u32[]{:S(2)}) collective-permute-start(f32[8,1024]{1,0:T(8,128)S(1)} %shard_map.65), channel_id=1, source_target_pairs={{64,96},{96,64},{0,32},{32,0},{65,97},{97,65},{1,33},{33,1},{66,98... | collective-permute-start | bytes 98312 | tf_op jit(solution)/shard_map/ppermute | solution.py:186
  56.9 3.2 %collective-permute-start.20 = (f32[8,1024]{1,0:T(8,128)S(1)}, f32[8,1024]{1,0:T(8,128)S(1)}, u32[]{:S(2)}, u32[]{:S(2)}) collective-permute-start(f32[8,1024]{1,0:T(8,128)S(1)} %get-tuple-element.21), channel_id=1, source_target_pairs={{96,64},{64,96},{0,32},{32,0},{97,65},{65,97},{1,33},{33,1},{98,66... | collective-permute-start | bytes 98312 | tf_op jit(solution)/shard_map/ppermute | solution.py:186
  60.1 4.0 %collective-permute-start.21 = (f32[8,1024]{1,0:T(8,128)S(1)}, f32[8,1024]{1,0:T(8,128)S(1)}, u32[]{:S(2)}, u32[]{:S(2)}) collective-permute-start(f32[8,1024]{1,0:T(8,128)S(1)} %shard_map.67), channel_id=1, source_target_pairs={{64,32},{32,64},{0,96},{96,0},{65,33},{33,65},{1,97},{97,1},{66,34... | collective-permute-start | bytes 98312 | tf_op jit(solution)/shard_map/ppermute | solution.py:186
  64.1 5.4 %collective-permute-start.22 = (f32[8,1024]{1,0:T(8,128)S(1)}, f32[8,1024]{1,0:T(8,128)S(1)}, u32[]{:S(2)}, u32[]{:S(2)}) collective-permute-start(f32[8,1024]{1,0:T(8,128)S(1)} %shard_map.68), channel_id=1, source_target_pairs={{32,0},{0,32},{64,96},{96,64},{33,1},{1,33},{65,97},{97,65},{34,2}... | collective-permute-start | bytes 98312 | tf_op jit(solution)/shard_map/ppermute | solution.py:186
where the time goes:
time: 91 us; the launch traced here: 90.8 us
  starting transfers between devices  37.3 us (41%)
  waiting for transfers between devices  25.7 us (28%)
  blocking collectives  18 us (20%)
  Pallas kernels  9.12 us (10%)
    all_to_all x1, blocking collectives, per_device(): got = lax.all_to_all(send, 'panel', 0, 0, tiled=True).reshape(cols, LANES)  18 us
    ppermute x8, starting transfers between devices, gathered(): return pieces + [lax.ppermute(piece, 'panel', SIBLINGS) for piece in pieces]  16 us
    ppermute x6, waiting for transfers between devices, hop(): return lax.ppermute(block, 'depth', route)  13.7 us
    ppermute x9, starting transfers between devices, from_partner(): return lax.ppermute(block, 'panel', pairs)  12.9 us
    ppermute x9, waiting for transfers between devices, from_partner(): return lax.ppermute(block, 'panel', pairs)  10.5 us
    ppermute x6, starting transfers between devices, hop(): return lax.ppermute(block, 'depth', route)  8.4 us
    pallas_call x11, Pallas kernels, call(): pl.pallas_call(kernel, out_shape=out_shape, in_specs=[space] * len(args),...  8.14 us
  transfers between devices with their start and end apart: 23, of which 12 were waited for; matrix products, arithmetic and copies ran while one was open for 0% of the time, Pallas kernels for 0%

commit v1 on v0

--- a/solution.py
+++ b/solution.py
@@ -64,10 +64,10 @@
     return high, (x - high.astype(F32)).astype(BF16)
 
 
-def product(x, high_ref, low_ref, transposed=False):
+def product(x, high_ref, low_ref):
     rows = x.shape[0]
     both = jnp.concatenate(split(x), 0)
-    dims = (((1,), (1 if transposed else 0,)), ((), ()))
+    dims = (((1,), (0,)), ((), ()))
     first = lax.dot_general(both, high_ref[...], dims, preferred_element_type=F32)
     second = lax.dot_general(both, low_ref[...], dims, preferred_element_type=F32)
     total = first + second
@@ -113,12 +113,11 @@
         copy.wait()
 
 
-def first_kernel(*refs, size, cols):
-    pieces = refs[:16]
-    d_high, d_low, c_high, c_low, source, diag, wanted, side = refs[16:]
-    me = lax.axis_index("panel")
-    core = lax.rem(me, 2)
-    place = lax.div(me, 2)
+def move_pieces(numbers, pieces, d_high, d_low, c_high, c_low, side):
+    size = d_high.shape[0]
+    cols = side.shape[1] - LANES
+    core = lax.rem(lax.axis_index("panel"), 2)
+    place = lax.div(lax.axis_index("panel"), 2)
     unit_rows = size // 32
     step = 16
     groups = size // LANES
@@ -139,7 +138,7 @@
 
         lax.fori_loop(0, unit_rows // step, body, 0)
 
-    for number in range(16):
+    for number, held in zip(numbers, pieces):
         sibling = number // 8
         for unit in range(2):
             piece = PIECES[number % 8]
@@ -147,7 +146,26 @@
                 core == sibling, offset_of(0, piece, unit), offset_of(1, piece, unit)
             )
             owner = lax.bitwise_xor(place, offset) * 2 + lax.bitwise_xor(core, sibling)
-            move(pieces[number], unit * unit_rows, owner * unit_rows)
+            move(held, unit * unit_rows, owner * unit_rows)
+
+
+EARLY = (0, 1, 2, 3, 4, 5, 8, 9, 10, 11)
+LATE = tuple(number for number in range(16) if number not in EARLY)
+
+
+def early_kernel(*refs):
+    count = len(EARLY)
+    move_pieces(EARLY, refs[:count], *refs[count:])
+
+
+def late_kernel(*refs):
+    count = len(LATE)
+    side = refs[count + 4]
+    d_high, d_low, c_high, c_low, source, diag, wanted = refs[count + 5 :]
+    size = d_high.shape[0]
+    groups = size // LANES
+    cols = side.shape[1] - LANES
+    move_pieces(LATE, refs[:count], d_high, d_low, c_high, c_low, side)
 
     for group in range(groups):
         for k in range(1, groups - SENT_GROUPS + 1):
@@ -158,7 +176,7 @@
             d_high[where, rows], d_low[where, rows] = split(block.T)
 
     pick = lax.broadcasted_iota(jnp.int32, (8, cols), 1) == (
-        lax.broadcasted_iota(jnp.int32, (8, cols), 0) + me * 8
+        lax.broadcasted_iota(jnp.int32, (8, cols), 0) + lax.axis_index("panel") * 8
     )
     own = lax.dot_general(
         pick.astype(F32),
@@ -201,6 +219,16 @@
         refs[-1][...] = product(forward, c_high, c_low)
 
 
+def transpose_kernel(last, high, low, high_turned, low_turned):
+    @pl.when(lax.axis_index("depth") != last)
+    def _():
+        for ref, turned in ((high, high_turned), (low, low_turned)):
+            for row in range(0, ref.shape[0], LANES):
+                for col in range(0, ref.shape[1], LANES):
+                    block = ref[row : row + LANES, col : col + LANES].astype(F32)
+                    turned[col : col + LANES, row : row + LANES] = block.T.astype(BF16)
+
+
 def turn_kernel(count, d_high, d_low, source, diag, *refs):
     right_hand = source[...] - taken(lax.axis_index("depth"), range(1, count + 1), refs[:count])
     refs[count][...] = right_hand
@@ -213,14 +241,14 @@
 def backward_kernel(plane, d_high, d_low, c_high, c_low, right_hand, diag, ahead, panel):
     @pl.when(lax.axis_index("depth") == plane)
     def _():
-        rest = right_hand[...] - product(ahead[...], c_high, c_low, True)
+        rest = right_hand[...] - product(ahead[...], c_high, c_low)
         panel[...] = jacobi(rest, diag[...], d_high, d_low)
 
 
 def last_kernel(count, d_high, d_low, c_high, c_low, right_hand, diag, wanted, *refs):
     ahead = taken(lax.axis_index("depth"), range(count - 1, -1, -1), refs[:count])
-    rest = right_hand[...] - product(ahead, c_high, c_low, True)
-    panel = jacobi(rest, diag[...], d_high, d_low)
+    coupled = jnp.where(lax.axis_index("depth") == count, 0.0, product(ahead, c_high, c_low))
+    panel = jacobi(right_hand[...] - coupled, diag[...], d_high, d_low)
     size = panel.shape[1]
     high = panel.astype(BF16)
     rest = panel - high.astype(F32)
@@ -256,7 +284,7 @@
     return pltpu.VMEM(shape, dtype)
 
 
-def call(kernel, out_shape, *args, scratch=(), limit=8):
+def call(kernel, out_shape, *args, aliases=None, limit=8):
     args = [pltpu.with_memory_space_constraint(arg, pltpu.VMEM) for arg in args]
     space = pl.BlockSpec(memory_space=pltpu.VMEM)
     return pl.pallas_call(
@@ -264,7 +292,7 @@
         out_shape=out_shape,
         in_specs=[space] * len(args),
         out_specs=jax.tree.map(lambda _: space, out_shape),
-        scratch_shapes=scratch,
+        input_output_aliases=aliases or {},
         compiler_params=pltpu.CompilerParams(vmem_limit_bytes=limit * 1024 * 1024),
     )(*args)
 
@@ -287,11 +315,17 @@
 
     vec = vmem((8, size))
     mat = vmem((size, size), BF16)
+    filled = call(
+        early_kernel,
+        (mat, mat, mat, mat, vmem((size, cols + LANES))),
+        *[pieces[number] for number in EARLY],
+    )
     d_high, d_low, c_high, c_low, source, diag, wanted = call(
-        functools.partial(first_kernel, size=size, cols=cols),
+        late_kernel,
         (mat, mat, mat, mat, vec, vec, vmem((8, LANES))),
-        *pieces,
-        scratch=[pltpu.VMEM((size, cols + LANES), F32)],
+        *[pieces[number] for number in LATE],
+        *filled,
+        aliases={len(LATE) + number: number for number in range(4)},
     )
     mats = (d_high, d_low, c_high, c_low)
 
@@ -303,6 +337,7 @@
             vec, *mats, source, diag, *lefts[-1:],
         )
         lefts.append(hop(carried, k, k + 1))
+    turned = call(functools.partial(transpose_kernel, last), (mat, mat), c_high, c_low)
     right_hand, panel = call(
         functools.partial(turn_kernel, last),
         (vec, vec), d_high, d_low, source, diag, *lefts,
@@ -313,12 +348,12 @@
         if k > 0:
             panel = call(
                 functools.partial(backward_kernel, k),
-                vec, *mats, right_hand, diag, aheads[-1],
+                vec, d_high, d_low, *turned, right_hand, diag, aheads[-1],
             )
     send = call(
         functools.partial(last_kernel, last),
         vmem((size // rows, 8, LANES)),
-        *mats, right_hand, diag, wanted, *aheads,
+        d_high, d_low, *turned, right_hand, diag, wanted, *aheads,
     )
     got = lax.all_to_all(send, "panel", 0, 0, tiled=True).reshape(cols, LANES)
     panels, picked = call(

time: 91 us -> 88.2 us (0.969)
  waiting for transfers between devices: 25.7 us -> 18.9 us
  starting transfers between devices: 37.3 us -> 40.6 us
    ppermute x9, waiting for transfers between devices: 10.5 us -> 6.02 us  [from_partner(): return lax.ppermute(block, 'panel', pairs)]
    ppermute x8, starting transfers between devices: 16 us -> 19.6 us  [gathered(): return pieces + [lax.ppermute(piece, 'panel', SIBLINGS) for piece in pieces]]
    ppermute x6, waiting for transfers between devices: 13.7 us -> 12.5 us  [hop(): return lax.ppermute(block, 'depth', route)]
    ppermute x8, waiting for transfers between devices: 1.53 us -> 0.4 us  [gathered(): return pieces + [lax.ppermute(piece, 'panel', SIBLINGS) for piece in pieces]]
    ppermute x6, starting transfers between devices: 8.4 us -> 7.29 us  [hop(): return lax.ppermute(block, 'depth', route)]
    pallas_call x11 -> x13, Pallas kernels: 8.14 us -> 8.79 us  [call(): pl.pallas_call(kernel, out_shape=out_shape, in_specs=[space] * len(args),...]
  transfers between devices with their start and end apart: 23 -> 23, of which waited for: 12 -> 10; matrix products, arithmetic and copies ran while one was open for 0% -> 0% of each run, Pallas kernels for 0% -> 3%
where the time goes in v1:
time: 88.2 us; the launch traced here: 88.1 us
  starting transfers between devices  40.6 us (46%)
  waiting for transfers between devices  18.9 us (21%)
  blocking collectives  18.1 us (21%)
  Pallas kernels  9.78 us (11%)
    ppermute x8, starting transfers between devices, gathered(): return pieces + [lax.ppermute(piece, 'panel', SIBLINGS) for piece in pieces]  19.6 us
    all_to_all x1, blocking collectives, per_device(): got = lax.all_to_all(send, 'panel', 0, 0, tiled=True).reshape(cols, LANES)  18.1 us
    ppermute x9, starting transfers between devices, from_partner(): return lax.ppermute(block, 'panel', pairs)  13.7 us
    ppermute x6, waiting for transfers between devices, hop(): return lax.ppermute(block, 'depth', route)  12.5 us
    pallas_call x13, Pallas kernels, call(): pl.pallas_call(kernel, out_shape=out_shape, in_specs=[space] * len(args),...  8.79 us
    ppermute x6, starting transfers between devices, hop(): return lax.ppermute(block, 'depth', route)  7.29 us
    ppermute x9, waiting for transfers between devices, from_partner(): return lax.ppermute(block, 'panel', pairs)  6.02 us
  transfers between devices with their start and end apart: 23, of which 10 were waited for; matrix products, arithmetic and copies ran while one was open for 0% of the time, Pallas kernels for 3%

profile of v1, /device:TPU:1, one launch (start us, length us, event | category | flops | bytes accessed | tf_op | source)
XLA Modules:
  0.0 88.1 jit_solution(9375656778550726447)
XLA Ops:
  1.6 2.2 %collective-permute-start = (f32[32,2048]{1,0:T(8,128)S(1)}, f32[32,2048]{1,0:T(8,128)S(1)}, u32[]{:S(2)}, u32[]{:S(2)}) collective-permute-start(f32[32,2048]{1,0:T(8,128)S(1)} %shard_map.59.first), channel_id=1, source_target_pairs={{0,2},{1,9},{2,0},{3,11},{4,6},{5,13},{6,4},{7,15},{8,10},{9,1},{1... | collective-permute-start | bytes 786440 | tf_op jit(solution)/shard_map/ppermute | solution.py:26
  3.8 2.6 %collective-permute-start.4 = (f32[32,2048]{1,0:T(8,128)S(1)}, f32[32,2048]{1,0:T(8,128)S(1)}, u32[]{:S(2)}, u32[]{:S(2)}) collective-permute-start(f32[32,2048]{1,0:T(8,128)S(1)} %shard_map.59.first), channel_id=1, source_target_pairs={{0,4},{1,17},{2,6},{3,19},{4,0},{5,21},{6,2},{7,23},{8,12},{9,25},... | collective-permute-start | bytes 786440 | tf_op jit(solution)/shard_map/ppermute | solution.py:26
  7.9 1.7 %collective-permute-start.13 = (f32[64,2048]{1,0:T(8,128)S(1)}, f32[64,2048]{1,0:T(8,128)S(1)}, u32[]{:S(2)}, u32[]{:S(2)}) collective-permute-start(f32[64,2048]{1,0:T(8,128)S(1)} %shard_map.60.refs_0_), channel_id=1, source_target_pairs={{0,1},{1,0},{2,3},{3,2},{4,5},{5,4},{6,7},{7,6},{8,9},{9,8},{10,11... | collective-permute-start | bytes 1572872 | tf_op jit(solution)/shard_map/ppermute | solution.py:59
  9.6 1.7 %collective-permute-start.12 = (f32[64,2048]{1,0:T(8,128)S(1)}, f32[64,2048]{1,0:T(8,128)S(1)}, u32[]{:S(2)}, u32[]{:S(2)}) collective-permute-start(f32[64,2048]{1,0:T(8,128)S(1)} %shard_map.60.refs_0_), channel_id=1, source_target_pairs={{0,8},{1,3},{2,10},{3,1},{4,12},{5,7},{6,14},{7,5},{8,0},{9,11},{1... | collective-permute-start | bytes 1572872 | tf_op jit(solution)/shard_map/ppermute | solution.py:26
  11.3 2.2 %collective-permute-start.1 = (f32[64,2048]{1,0:T(8,128)S(1)}, f32[64,2048]{1,0:T(8,128)S(1)}, u32[]{:S(2)}, u32[]{:S(2)}) collective-permute-start(f32[64,2048]{1,0:T(8,128)S(1)} %shard_map.60.refs_0_), channel_id=1, source_target_pairs={{0,24},{1,7},{2,26},{3,5},{4,28},{5,3},{6,30},{7,1},{8,16},{9,15},... | collective-permute-start | bytes 1572872 | tf_op jit(solution)/shard_map/ppermute | solution.py:26
  13.6 2.6 %collective-permute-done.3.first = f32[32,2048]{1,0:T(8,128)S(1)} collective-permute-done((f32[32,2048]{1,0:T(8,128)S(1)}, f32[32,2048]{1,0:T(8,128)S(1)}, u32[]{:S(2)}, u32[]{:S(2)}) %collective-permute-start.3) | collective-permute-done | bytes 262176 | tf_op jit(solution)/shard_map/ppermute | solution.py:26
  16.3 1.7 %collective-permute-start.5 = (f32[64,2048]{1,0:T(8,128)S(1)}, f32[64,2048]{1,0:T(8,128)S(1)}, u32[]{:S(2)}, u32[]{:S(2)}) collective-permute-start(f32[64,2048]{1,0:T(8,128)S(1)} %shard_map.61.refs_1_), channel_id=1, source_target_pairs={{0,8},{1,3},{2,10},{3,1},{4,12},{5,7},{6,14},{7,5},{8,0},{9,11},{1... | collective-permute-start | bytes 1572872 | tf_op jit(solution)/shard_map/ppermute | solution.py:26
  18.0 5.1 %collective-permute-start.14 = (f32[64,2048]{1,0:T(8,128)S(1)}, f32[64,2048]{1,0:T(8,128)S(1)}, u32[]{:S(2)}, u32[]{:S(2)}) collective-permute-start(f32[64,2048]{1,0:T(8,128)S(1)} %shard_map.61.refs_1_), channel_id=1, source_target_pairs={{0,1},{1,0},{2,3},{3,2},{4,5},{5,4},{6,7},{7,6},{8,9},{9,8},{10,11... | collective-permute-start | bytes 1572872 | tf_op jit(solution)/shard_map/ppermute | solution.py:59
  23.1 2.2 %collective-permute-start.15 = (f32[64,2048]{1,0:T(8,128)S(1)}, f32[64,2048]{1,0:T(8,128)S(1)}, u32[]{:S(2)}, u32[]{:S(2)}) collective-permute-start(f32[64,2048]{1,0:T(8,128)S(1)} %collective-permute-done.12.refs_2_), channel_id=1, source_target_pairs={{0,1},{1,0},{2,3},{3,2},{4,5},{5,4},{6,7},{7,6},{8,9},{9,8},{10,11... | collective-permute-start | bytes 1572872 | tf_op jit(solution)/shard_map/ppermute | solution.py:59
  25.3 3.1 %collective-permute-start.6 = (f32[64,2048]{1,0:T(8,128)S(1)}, f32[64,2048]{1,0:T(8,128)S(1)}, u32[]{:S(2)}, u32[]{:S(2)}) collective-permute-start(f32[64,2048]{1,0:T(8,128)S(1)} %collective-permute-done.5.refs_4_), channel_id=1, source_target_pairs={{0,24},{1,7},{2,26},{3,5},{4,28},{5,3},{6,30},{7,1},{8,16},{9,15},... | collective-permute-start | bytes 1572872 | tf_op jit(solution)/shard_map/ppermute | solution.py:26
  28.4 5.3 %collective-permute-start.16 = (f32[64,2048]{1,0:T(8,128)S(1)}, f32[64,2048]{1,0:T(8,128)S(1)}, u32[]{:S(2)}, u32[]{:S(2)}) collective-permute-start(f32[64,2048]{1,0:T(8,128)S(1)} %collective-permute-done.1.refs_3_), channel_id=1, source_target_pairs={{0,1},{1,0},{2,3},{3,2},{4,5},{5,4},{6,7},{7,6},{8,9},{9,8},{10,11... | collective-permute-start | bytes 1572872 | tf_op jit(solution)/shard_map/ppermute | solution.py:59
  34.2 2.1 %collective-permute-start.10 = (f32[64,2048]{1,0:T(8,128)S(1)}, f32[64,2048]{1,0:T(8,128)S(1)}, u32[]{:S(2)}, u32[]{:S(2)}) collective-permute-start(f32[64,2048]{1,0:T(8,128)S(1)} %collective-permute-done.2.refs_0_), channel_id=1, source_target_pairs={{0,1},{1,0},{2,3},{3,2},{4,5},{5,4},{6,7},{7,6},{8,9},{9,8},{10,11... | collective-permute-start | bytes 1572872 | tf_op jit(solution)/shard_map/ppermute | solution.py:59
  36.3 1.9 %collective-permute-done.6.refs_1_ = f32[64,2048]{1,0:T(8,128)S(1)} collective-permute-done((f32[64,2048]{1,0:T(8,128)S(1)}, f32[64,2048]{1,0:T(8,128)S(1)}, u32[]{:S(2)}, u32[]{:S(2)}) %collective-permute-start.6) | collective-permute-done | bytes 524320 | tf_op jit(solution)/shard_map/ppermute | solution.py:26
  38.2 2.8 %collective-permute-start.11 = (f32[64,2048]{1,0:T(8,128)S(1)}, f32[64,2048]{1,0:T(8,128)S(1)}, u32[]{:S(2)}, u32[]{:S(2)}) collective-permute-start(f32[64,2048]{1,0:T(8,128)S(1)} %collective-permute-done.6.refs_1_), channel_id=1, source_target_pairs={{0,1},{1,0},{2,3},{3,2},{4,5},{5,4},{6,7},{7,6},{8,9},{9,8},{10,11... | collective-permute-start | bytes 1572872 | tf_op jit(solution)/shard_map/ppermute | solution.py:59
  42.6 1.8 %shard_map.63 = (bf16[1024,1024]{1,0:T(8,128)(2,1)S(1)}, bf16[1024,1024]{1,0:T(8,128)(2,1)S(1)}, bf16[1024,1024]{1,0:T(8,128)(2,1)S(1)}, bf16[1024,1024]{1,0:T(8...) custom-call(f32[64,2048]{1,0:T(8,128)S(1)} %collective-permute-done., ...), custom_call_target="tpu_custom_call", output_to_operand_aliasing={{0}: (6, {}), {1}: (7, {}), {2}: (8, {}), {3}: (9, {})} | custom-call | tf_op jit(solution)/shard_map/pallas_call | solution.py:290
  44.4 1.8 %shard_map.65 = f32[8,1024]{1,0:T(8,128)S(1)} custom-call(bf16[1024,1024]{1,0:T(8,128)(2,1)S(1)} %get-tuple-element.25.d_high, bf16[1024,1024]{1,0:T(8,128)(2,1)S(1)} %get-tuple-element.26.d_low, bf16[1024,1024]{1,0:T(8,128)(2,1)S(1)} %get-tuple-element.27.high.c_high, bf16[1024,1024]{1,0:T(8,128)(2,1)S(1)} %get-tuple-element.28.low.c_low, ...), custom_call_target="tpu_custom_call" | custom-call | tf_op jit(solution)/shard_map/pallas_call | solution.py:290
  46.2 2.8 %collective-permute-done.17.refs_0_ = f32[8,1024]{1,0:T(8,128)S(1)} collective-permute-done((f32[8,1024]{1,0:T(8,128)S(1)}, f32[8,1024]{1,0:T(8,128)S(1)}, u32[]{:S(2)}, u32[]{:S(2)}) %collective-permute-start.17) | collective-permute-done | bytes 32800 | tf_op jit(solution)/shard_map/ppermute | solution.py:204
  49.8 3.2 %collective-permute-done.18.refs_0_.refs_1_ = f32[8,1024]{1,0:T(8,128)S(1)} collective-permute-done((f32[8,1024]{1,0:T(8,128)S(1)}, f32[8,1024]{1,0:T(8,128)S(1)}, u32[]{:S(2)}, u32[]{:S(2)}) %collective-permute-start.18) | collective-permute-done | bytes 32800 | tf_op jit(solution)/shard_map/ppermute | solution.py:204
  53.5 2.2 %collective-permute-done.19.refs_2_ = f32[8,1024]{1,0:T(8,128)S(1)} collective-permute-done((f32[8,1024]{1,0:T(8,128)S(1)}, f32[8,1024]{1,0:T(8,128)S(1)}, u32[]{:S(2)}, u32[]{:S(2)}) %collective-permute-start.19) | collective-permute-done | bytes 32800 | tf_op jit(solution)/shard_map/ppermute | solution.py:204
  59.0 2.3 %collective-permute-start.21 = (f32[8,1024]{1,0:T(8,128)S(1)}, f32[8,1024]{1,0:T(8,128)S(1)}, u32[]{:S(2)}, u32[]{:S(2)}) collective-permute-start(f32[8,1024]{1,0:T(8,128)S(1)} %shard_map.69), channel_id=1, source_target_pairs={{64,32},{32,64},{0,96},{96,0},{65,33},{33,65},{1,97},{97,1},{66,34... | collective-permute-start | bytes 98312 | tf_op jit(solution)/shard_map/ppermute | solution.py:204
  61.2 1.7 %collective-permute-done.21.ahead.refs_1_ = f32[8,1024]{1,0:T(8,128)S(1)} collective-permute-done((f32[8,1024]{1,0:T(8,128)S(1)}, f32[8,1024]{1,0:T(8,128)S(1)}, u32[]{:S(2)}, u32[]{:S(2)}) %collective-permute-start.21) | collective-permute-done | bytes 32800 | tf_op jit(solution)/shard_map/ppermute | solution.py:204
  62.9 3.0 %collective-permute-start.22 = (f32[8,1024]{1,0:T(8,128)S(1)}, f32[8,1024]{1,0:T(8,128)S(1)}, u32[]{:S(2)}, u32[]{:S(2)}) collective-permute-start(f32[8,1024]{1,0:T(8,128)S(1)} %shard_map.70), channel_id=1, source_target_pairs={{32,0},{0,32},{64,96},{96,64},{33,1},{1,33},{65,97},{97,65},{34,2}... | collective-permute-start | bytes 98312 | tf_op jit(solution)/shard_map/ppermute | solution.py:204
  67.2 2.1 %shard_map.71 = f32[32,8,128]{2,1,0:T(8,128)S(1)} custom-call(bf16[1024,1024]{1,0:T(8,128)(2,1)S(1)} %get-tuple-element.25.d_high, bf16[1024,1024]{1,0:T(8,128)(2,1)S(1)} %get-tuple-element.26.d_low, bf16[1024,1024]{1,0:T(8,128)(2,1)S(1)} %get-tuple-element.29.c_high, bf16[1024,1024]{1,0:T(8,128)(2,1)S(1)} %get-tuple-element.30.c_low, ...), custom_call_target="tpu_custom_call" | custom-call | tf_op jit(solution)/shard_map/pallas_call | solution.py:290
  69.3 18.1 %all_to_all.5 = f32[32,8,128]{2,1,0:T(8,128)S(1)} all-to-all(f32[32,8,128]{2,1,0:T(8,128)S(1)} %shard_map.71), channel_id=1, replica_groups=mesh['depth'=4,'panel'=32] {'panel'}, dimensions={0} | all-to-all | bytes 262144 | tf_op jit(solution)/shard_map/all_to_all | solution.py:358
  (37 shorter events, 11.1 us)
Async XLA Ops:
  1.6 6.3 %collective-permute-start = (f32[32,2048]{1,0:T(8,128)S(1)}, f32[32,2048]{1,0:T(8,128)S(1)}, u32[]{:S(2)}, u32[]{:S(2)}) collective-permute-start(f32[32,2048]{1,0:T(8,128)S(1)} %shard_map.59.first), channel_id=1, source_target_pairs={{0,2},{1,9},{2,0},{3,11},{4,6},{5,13},{6,4},{7,15},{8,10},{9,1},{1... | collective-permute-start | bytes 786440 | tf_op jit(solution)/shard_map/ppermute | solution.py:26
  3.8 9.8 %collective-permute-start.4 = (f32[32,2048]{1,0:T(8,128)S(1)}, f32[32,2048]{1,0:T(8,128)S(1)}, u32[]{:S(2)}, u32[]{:S(2)}) collective-permute-start(f32[32,2048]{1,0:T(8,128)S(1)} %shard_map.59.first), channel_id=1, source_target_pairs={{0,4},{1,17},{2,6},{3,19},{4,0},{5,21},{6,2},{7,23},{8,12},{9,25},... | collective-permute-start | bytes 786440 | tf_op jit(solution)/shard_map/ppermute | solution.py:26
  6.4 9.8 %collective-permute-start.3 = (f32[32,2048]{1,0:T(8,128)S(1)}, f32[32,2048]{1,0:T(8,128)S(1)}, u32[]{:S(2)}, u32[]{:S(2)}) collective-permute-start(f32[32,2048]{1,0:T(8,128)S(1)} %shard_map.59.first), channel_id=1, source_target_pairs={{0,6},{1,25},{2,4},{3,27},{4,2},{5,29},{6,0},{7,31},{8,14},{9,17},... | collective-permute-start | bytes 786440 | tf_op jit(solution)/shard_map/ppermute | solution.py:26
  7.9 15.2 %collective-permute-start.13 = (f32[64,2048]{1,0:T(8,128)S(1)}, f32[64,2048]{1,0:T(8,128)S(1)}, u32[]{:S(2)}, u32[]{:S(2)}) collective-permute-start(f32[64,2048]{1,0:T(8,128)S(1)} %shard_map.60.refs_0_), channel_id=1, source_target_pairs={{0,1},{1,0},{2,3},{3,2},{4,5},{5,4},{6,7},{7,6},{8,9},{9,8},{10,11... | collective-permute-start | bytes 1572872 | tf_op jit(solution)/shard_map/ppermute | solution.py:59
  9.6 13.5 %collective-permute-start.12 = (f32[64,2048]{1,0:T(8,128)S(1)}, f32[64,2048]{1,0:T(8,128)S(1)}, u32[]{:S(2)}, u32[]{:S(2)}) collective-permute-start(f32[64,2048]{1,0:T(8,128)S(1)} %shard_map.60.refs_0_), channel_id=1, source_target_pairs={{0,8},{1,3},{2,10},{3,1},{4,12},{5,7},{6,14},{7,5},{8,0},{9,11},{1... | collective-permute-start | bytes 1572872 | tf_op jit(solution)/shard_map/ppermute | solution.py:26
  11.3 13.9 %collective-permute-start.1 = (f32[64,2048]{1,0:T(8,128)S(1)}, f32[64,2048]{1,0:T(8,128)S(1)}, u32[]{:S(2)}, u32[]{:S(2)}) collective-permute-start(f32[64,2048]{1,0:T(8,128)S(1)} %shard_map.60.refs_0_), channel_id=1, source_target_pairs={{0,24},{1,7},{2,26},{3,5},{4,28},{5,3},{6,30},{7,1},{8,16},{9,15},... | collective-permute-start | bytes 1572872 | tf_op jit(solution)/shard_map/ppermute | solution.py:26
  16.3 9.0 %collective-permute-start.5 = (f32[64,2048]{1,0:T(8,128)S(1)}, f32[64,2048]{1,0:T(8,128)S(1)}, u32[]{:S(2)}, u32[]{:S(2)}) collective-permute-start(f32[64,2048]{1,0:T(8,128)S(1)} %shard_map.61.refs_1_), channel_id=1, source_target_pairs={{0,8},{1,3},{2,10},{3,1},{4,12},{5,7},{6,14},{7,5},{8,0},{9,11},{1... | collective-permute-start | bytes 1572872 | tf_op jit(solution)/shard_map/ppermute | solution.py:26
  18.0 10.4 %collective-permute-start.14 = (f32[64,2048]{1,0:T(8,128)S(1)}, f32[64,2048]{1,0:T(8,128)S(1)}, u32[]{:S(2)}, u32[]{:S(2)}) collective-permute-start(f32[64,2048]{1,0:T(8,128)S(1)} %shard_map.61.refs_1_), channel_id=1, source_target_pairs={{0,1},{1,0},{2,3},{3,2},{4,5},{5,4},{6,7},{7,6},{8,9},{9,8},{10,11... | collective-permute-start | bytes 1572872 | tf_op jit(solution)/shard_map/ppermute | solution.py:59
  23.1 10.6 %collective-permute-start.8 = (f32[64,2048]{1,0:T(8,128)S(1)}, f32[64,2048]{1,0:T(8,128)S(1)}, u32[]{:S(2)}, u32[]{:S(2)}) collective-permute-start(f32[64,2048]{1,0:T(8,128)S(1)} %shard_map.61.refs_1_), channel_id=1, source_target_pairs={{0,24},{1,7},{2,26},{3,5},{4,28},{5,3},{6,30},{7,1},{8,16},{9,15},... | collective-permute-start | bytes 1572872 | tf_op jit(solution)/shard_map/ppermute | solution.py:26
  23.1 10.7 %collective-permute-start.15 = (f32[64,2048]{1,0:T(8,128)S(1)}, f32[64,2048]{1,0:T(8,128)S(1)}, u32[]{:S(2)}, u32[]{:S(2)}) collective-permute-start(f32[64,2048]{1,0:T(8,128)S(1)} %collective-permute-done.12.refs_2_), channel_id=1, source_target_pairs={{0,1},{1,0},{2,3},{3,2},{4,5},{5,4},{6,7},{7,6},{8,9},{9,8},{10,11... | collective-permute-start | bytes 1572872 | tf_op jit(solution)/shard_map/ppermute | solution.py:59
  25.3 8.9 %collective-permute-start.2 = (f32[64,2048]{1,0:T(8,128)S(1)}, f32[64,2048]{1,0:T(8,128)S(1)}, u32[]{:S(2)}, u32[]{:S(2)}) collective-permute-start(f32[64,2048]{1,0:T(8,128)S(1)} %collective-permute-done.1.refs_3_), channel_id=1, source_target_pairs={{0,8},{1,3},{2,10},{3,1},{4,12},{5,7},{6,14},{7,5},{8,0},{9,11},{1... | collective-permute-start | bytes 1572872 | tf_op jit(solution)/shard_map/ppermute | solution.py:26
  25.3 13.0 %collective-permute-start.6 = (f32[64,2048]{1,0:T(8,128)S(1)}, f32[64,2048]{1,0:T(8,128)S(1)}, u32[]{:S(2)}, u32[]{:S(2)}) collective-permute-start(f32[64,2048]{1,0:T(8,128)S(1)} %collective-permute-done.5.refs_4_), channel_id=1, source_target_pairs={{0,24},{1,7},{2,26},{3,5},{4,28},{5,3},{6,30},{7,1},{8,16},{9,15},... | collective-permute-start | bytes 1572872 | tf_op jit(solution)/shard_map/ppermute | solution.py:26
  28.4 12.6 %collective-permute-start.16 = (f32[64,2048]{1,0:T(8,128)S(1)}, f32[64,2048]{1,0:T(8,128)S(1)}, u32[]{:S(2)}, u32[]{:S(2)}) collective-permute-start(f32[64,2048]{1,0:T(8,128)S(1)} %collective-permute-done.1.refs_3_), channel_id=1, source_target_pairs={{0,1},{1,0},{2,3},{3,2},{4,5},{5,4},{6,7},{7,6},{8,9},{9,8},{10,11... | collective-permute-start | bytes 1572872 | tf_op jit(solution)/shard_map/ppermute | solution.py:59
  33.7 8.5 %collective-permute-start.7 = (f32[64,2048]{1,0:T(8,128)S(1)}, f32[64,2048]{1,0:T(8,128)S(1)}, u32[]{:S(2)}, u32[]{:S(2)}) collective-permute-start(f32[64,2048]{1,0:T(8,128)S(1)} %collective-permute-done.5.refs_4_), channel_id=1, source_target_pairs={{0,1},{1,0},{2,3},{3,2},{4,5},{5,4},{6,7},{7,6},{8,9},{9,8},{10,11... | collective-permute-start | bytes 1572872 | tf_op jit(solution)/shard_map/ppermute | solution.py:59
  33.8 8.4 %collective-permute-start.9 = (f32[64,2048]{1,0:T(8,128)S(1)}, f32[64,2048]{1,0:T(8,128)S(1)}, u32[]{:S(2)}, u32[]{:S(2)}) collective-permute-start(f32[64,2048]{1,0:T(8,128)S(1)} %collective-permute-done.8.refs_5_), channel_id=1, source_target_pairs={{0,1},{1,0},{2,3},{3,2},{4,5},{5,4},{6,7},{7,6},{8,9},{9,8},{10,11... | collective-permute-start | bytes 1572872 | tf_op jit(solution)/shard_map/ppermute | solution.py:59
  34.2 8.0 %collective-permute-start.10 = (f32[64,2048]{1,0:T(8,128)S(1)}, f32[64,2048]{1,0:T(8,128)S(1)}, u32[]{:S(2)}, u32[]{:S(2)}) collective-permute-start(f32[64,2048]{1,0:T(8,128)S(1)} %collective-permute-done.2.refs_0_), channel_id=1, source_target_pairs={{0,1},{1,0},{2,3},{3,2},{4,5},{5,4},{6,7},{7,6},{8,9},{9,8},{10,11... | collective-permute-start | bytes 1572872 | tf_op jit(solution)/shard_map/ppermute | solution.py:59
  38.2 4.4 %collective-permute-start.11 = (f32[64,2048]{1,0:T(8,128)S(1)}, f32[64,2048]{1,0:T(8,128)S(1)}, u32[]{:S(2)}, u32[]{:S(2)}) collective-permute-start(f32[64,2048]{1,0:T(8,128)S(1)} %collective-permute-done.6.refs_1_), channel_id=1, source_target_pairs={{0,1},{1,0},{2,3},{3,2},{4,5},{5,4},{6,7},{7,6},{8,9},{9,8},{10,11... | collective-permute-start | bytes 1572872 | tf_op jit(solution)/shard_map/ppermute | solution.py:59
  46.2 2.8 %collective-permute-start.17 = (f32[8,1024]{1,0:T(8,128)S(1)}, f32[8,1024]{1,0:T(8,128)S(1)}, u32[]{:S(2)}, u32[]{:S(2)}) collective-permute-start(f32[8,1024]{1,0:T(8,128)S(1)} %shard_map.65), channel_id=1, source_target_pairs={{0,32},{32,0},{64,96},{96,64},{1,33},{33,1},{65,97},{97,65},{2,34}... | collective-permute-start | bytes 98312 | tf_op jit(solution)/shard_map/ppermute | solution.py:204
  49.0 4.0 %collective-permute-start.18 = (f32[8,1024]{1,0:T(8,128)S(1)}, f32[8,1024]{1,0:T(8,128)S(1)}, u32[]{:S(2)}, u32[]{:S(2)}) collective-permute-start(f32[8,1024]{1,0:T(8,128)S(1)} %shard_map.66), channel_id=1, source_target_pairs={{32,64},{64,32},{0,96},{96,0},{33,65},{65,33},{1,97},{97,1},{34,66... | collective-permute-start | bytes 98312 | tf_op jit(solution)/shard_map/ppermute | solution.py:204
  53.0 2.8 %collective-permute-start.19 = (f32[8,1024]{1,0:T(8,128)S(1)}, f32[8,1024]{1,0:T(8,128)S(1)}, u32[]{:S(2)}, u32[]{:S(2)}) collective-permute-start(f32[8,1024]{1,0:T(8,128)S(1)} %shard_map.67), channel_id=1, source_target_pairs={{64,96},{96,64},{0,32},{32,0},{65,97},{97,65},{1,33},{33,1},{66,98... | collective-permute-start | bytes 98312 | tf_op jit(solution)/shard_map/ppermute | solution.py:204
  55.7 3.2 %collective-permute-start.20 = (f32[8,1024]{1,0:T(8,128)S(1)}, f32[8,1024]{1,0:T(8,128)S(1)}, u32[]{:S(2)}, u32[]{:S(2)}) collective-permute-start(f32[8,1024]{1,0:T(8,128)S(1)} %get-tuple-element.35), channel_id=1, source_target_pairs={{96,64},{64,96},{0,32},{32,0},{97,65},{65,97},{1,33},{33,1},{98,66... | collective-permute-start | bytes 98312 | tf_op jit(solution)/shard_map/ppermute | solution.py:204
  59.0 4.0 %collective-permute-start.21 = (f32[8,1024]{1,0:T(8,128)S(1)}, f32[8,1024]{1,0:T(8,128)S(1)}, u32[]{:S(2)}, u32[]{:S(2)}) collective-permute-start(f32[8,1024]{1,0:T(8,128)S(1)} %shard_map.69), channel_id=1, source_target_pairs={{64,32},{32,64},{0,96},{96,0},{65,33},{33,65},{1,97},{97,1},{66,34... | collective-permute-start | bytes 98312 | tf_op jit(solution)/shard_map/ppermute | solution.py:204
  62.9 4.3 %collective-permute-start.22 = (f32[8,1024]{1,0:T(8,128)S(1)}, f32[8,1024]{1,0:T(8,128)S(1)}, u32[]{:S(2)}, u32[]{:S(2)}) collective-permute-start(f32[8,1024]{1,0:T(8,128)S(1)} %shard_map.70), channel_id=1, source_target_pairs={{32,0},{0,32},{64,96},{96,64},{33,1},{1,33},{65,97},{97,65},{34,2}... | collective-permute-start | bytes 98312 | tf_op jit(solution)/shard_map/ppermute | solution.py:204

commit v2 on v1

--- a/solution.py
+++ b/solution.py
@@ -32,17 +32,28 @@
     both[rows:] = second[...]
 
 
+def cut_kernel(part, both, one):
+    rows = one.shape[0]
+    one[...] = both[part * rows : (part + 1) * rows]
+
+
+def cut(both, part):
+    shape = (both.shape[0] // 2, both.shape[1])
+    return call(functools.partial(cut_kernel, part), vmem(shape), both)
+
+
 def joined(first, second):
     return call(join_kernel, vmem((first.shape[0] * 2, first.shape[1])), first, second)
 
 
-PIECES = (("A", None), ("B", None), ("A", 0), ("A", 1), ("B", 0), ("B", 1), ("A", 2), ("B", 2))
-
-
-def offset_of(core, piece, unit):
-    half, line = piece
-    near = AXES[core]
-    offset = ((0, near[0]) if half == "A" else (near[1], near[2]))[unit]
+PIECES = (
+    (None, (0, 1)), (None, (2, 3)), (0, (0, 1)), (1, (0, 1)), (0, (2, 3)), (1, (2, 3)),
+    (2, (0,)), (2, (1,)), (2, (2,)), (2, (3,)),
+)
+
+
+def offset_of(core, line, unit):
+    offset = (0, *AXES[core])[unit]
     return offset ^ (0 if line is None else AXES[1 - core][line])
 
 
@@ -54,8 +65,13 @@
     a1, a0 = from_partner(a, 1, 1), from_partner(a, 1, 0)
     b = joined(other, far)
     b0, b1 = from_partner(b, 1, 0), from_partner(b, 1, 1)
-    a2, b2 = from_partner(a1, 1, 0), from_partner(b0, 1, 1)
-    pieces = [a, b, a0, a1, b0, b1, a2, b2]
+    far_pieces = [
+        from_partner(cut(a1, 0), 1, 0),
+        from_partner(cut(a0, 1), 1, 1),
+        from_partner(cut(b0, 0), 1, 1),
+        from_partner(cut(b1, 1), 1, 0),
+    ]
+    pieces = [a, b, a0, a1, b0, b1, *far_pieces]
     return pieces + [lax.ppermute(piece, "panel", SIBLINGS) for piece in pieces]
 
 
@@ -139,18 +155,18 @@
         lax.fori_loop(0, unit_rows // step, body, 0)
 
     for number, held in zip(numbers, pieces):
-        sibling = number // 8
-        for unit in range(2):
-            piece = PIECES[number % 8]
+        sibling = number // len(PIECES)
+        line, units = PIECES[number % len(PIECES)]
+        for place_in, unit in enumerate(units):
             offset = jnp.where(
-                core == sibling, offset_of(0, piece, unit), offset_of(1, piece, unit)
+                core == sibling, offset_of(0, line, unit), offset_of(1, line, unit)
             )
             owner = lax.bitwise_xor(place, offset) * 2 + lax.bitwise_xor(core, sibling)
-            move(held, unit * unit_rows, owner * unit_rows)
-
-
-EARLY = (0, 1, 2, 3, 4, 5, 8, 9, 10, 11)
-LATE = tuple(number for number in range(16) if number not in EARLY)
+            move(held, place_in * unit_rows, owner * unit_rows)
+
+
+EARLY = (0, 1, 2, 3, 10, 11, 12, 13)
+LATE = tuple(number for number in range(2 * len(PIECES)) if number not in EARLY)
 
 
 def early_kernel(*refs):

time: 88.2 us -> 96.2 us (1.091)
  waiting for transfers between devices: 18.9 us -> 32.1 us
  starting transfers between devices: 40.6 us -> 34.9 us
    ppermute x9 -> x11, waiting for transfers between devices: 6.02 us -> 18.2 us  [from_partner(): return lax.ppermute(block, 'panel', pairs)]
    ppermute x8 -> x10, starting transfers between devices: 19.6 us -> 14.6 us  [gathered(): return pieces + [lax.ppermute(piece, 'panel', SIBLINGS) for piece in pieces]]
    ppermute x8 -> x10, waiting for transfers between devices: 0.4 us -> 1.48 us  [gathered(): return pieces + [lax.ppermute(piece, 'panel', SIBLINGS) for piece in pieces]]
    ppermute x9 -> x11, starting transfers between devices: 13.7 us -> 13 us  [from_partner(): return lax.ppermute(block, 'panel', pairs)]
    pallas_call x13 -> x17, Pallas kernels: 8.79 us -> 8.91 us  [call(): pl.pallas_call(kernel, out_shape=out_shape, in_specs=[space] * len(args),...]
  transfers between devices with their start and end apart: 23 -> 27, of which waited for: 10 -> 15; matrix products, arithmetic and copies ran while one was open for 0% -> 0% of each run, Pallas kernels for 3% -> 2%
where the time goes in v2:
time: 96.2 us; the launch traced here: 96.1 us
  starting transfers between devices  34.9 us (36%)
  waiting for transfers between devices  32.1 us (33%)
  blocking collectives  18.3 us (19%)
  Pallas kernels  9.89 us (10%)
    all_to_all x1, blocking collectives, per_device(): got = lax.all_to_all(send, 'panel', 0, 0, tiled=True).reshape(cols, LANES)  18.3 us
    ppermute x11, waiting for transfers between devices, from_partner(): return lax.ppermute(block, 'panel', pairs)  18.2 us
    ppermute x10, starting transfers between devices, gathered(): return pieces + [lax.ppermute(piece, 'panel', SIBLINGS) for piece in pieces]  14.6 us
    ppermute x11, starting transfers between devices, from_partner(): return lax.ppermute(block, 'panel', pairs)  13 us
    ppermute x6, waiting for transfers between devices, hop(): return lax.ppermute(block, 'depth', route)  12.4 us
    pallas_call x17, Pallas kernels, call(): pl.pallas_call(kernel, out_shape=out_shape, in_specs=[space] * len(args),...  8.91 us
    ppermute x6, starting transfers between devices, hop(): return lax.ppermute(block, 'depth', route)  7.32 us
  transfers between devices with their start and end apart: 27, of which 15 were waited for; matrix products, arithmetic and copies ran while one was open for 0% of the time, Pallas kernels for 2%

profile of v2, /device:TPU:1, one launch (start us, length us, event | category | flops | bytes accessed | tf_op | source)
XLA Modules:
  0.0 96.1 jit_solution(16954459992841842697)
XLA Ops:
  1.6 3.8 %collective-permute-start.1 = (f32[32,2048]{1,0:T(8,128)S(1)}, f32[32,2048]{1,0:T(8,128)S(1)}, u32[]{:S(2)}, u32[]{:S(2)}) collective-permute-start(f32[32,2048]{1,0:T(8,128)S(1)} %shard_map.59.first), channel_id=1, source_target_pairs={{0,4},{1,17},{2,6},{3,19},{4,0},{5,21},{6,2},{7,23},{8,12},{9,25},... | collective-permute-start | bytes 786440 | tf_op jit(solution)/shard_map/ppermute | solution.py:26
  6.2 3.3 %collective-permute-done.1.second = f32[32,2048]{1,0:T(8,128)S(1)} collective-permute-done((f32[32,2048]{1,0:T(8,128)S(1)}, f32[32,2048]{1,0:T(8,128)S(1)}, u32[]{:S(2)}, u32[]{:S(2)}) %collective-permute-start.1) | collective-permute-done | bytes 262176 | tf_op jit(solution)/shard_map/ppermute | solution.py:26
  9.5 2.8 %collective-permute-done.first = f32[32,2048]{1,0:T(8,128)S(1)} collective-permute-done((f32[32,2048]{1,0:T(8,128)S(1)}, f32[32,2048]{1,0:T(8,128)S(1)}, u32[]{:S(2)}, u32[]{:S(2)}) %collective-permute-start) | collective-permute-done | bytes 262176 | tf_op jit(solution)/shard_map/ppermute | solution.py:26
  12.3 3.9 %collective-permute-start.3 = (f32[64,2048]{1,0:T(8,128)S(1)}, f32[64,2048]{1,0:T(8,128)S(1)}, u32[]{:S(2)}, u32[]{:S(2)}) collective-permute-start(f32[64,2048]{1,0:T(8,128)S(1)} %shard_map.60.refs_1_), channel_id=1, source_target_pairs={{0,24},{1,7},{2,26},{3,5},{4,28},{5,3},{6,30},{7,1},{8,16},{9,15},... | collective-permute-start | bytes 1572872 | tf_op jit(solution)/shard_map/ppermute | solution.py:26
  16.2 1.3 %collective-permute-start.4 = (f32[32,2048]{1,0:T(8,128)S(1)}, f32[32,2048]{1,0:T(8,128)S(1)}, u32[]{:S(2)}, u32[]{:S(2)}) collective-permute-start(f32[32,2048]{1,0:T(8,128)S(1)} %shard_map.59.first), channel_id=1, source_target_pairs={{0,2},{1,9},{2,0},{3,11},{4,6},{5,13},{6,4},{7,15},{8,10},{9,1},{1... | collective-permute-start | bytes 786440 | tf_op jit(solution)/shard_map/ppermute | solution.py:26
  17.5 4.4 %collective-permute-done.4.second = f32[32,2048]{1,0:T(8,128)S(1)} collective-permute-done((f32[32,2048]{1,0:T(8,128)S(1)}, f32[32,2048]{1,0:T(8,128)S(1)}, u32[]{:S(2)}, u32[]{:S(2)}) %collective-permute-start.4) | collective-permute-done | bytes 262176 | tf_op jit(solution)/shard_map/ppermute | solution.py:26
  22.1 5.1 %collective-permute-start.18 = (f32[64,2048]{1,0:T(8,128)S(1)}, f32[64,2048]{1,0:T(8,128)S(1)}, u32[]{:S(2)}, u32[]{:S(2)}) collective-permute-start(f32[64,2048]{1,0:T(8,128)S(1)} %shard_map.60.refs_1_), channel_id=1, source_target_pairs={{0,1},{1,0},{2,3},{3,2},{4,5},{5,4},{6,7},{7,6},{8,9},{9,8},{10,11... | collective-permute-start | bytes 1572872 | tf_op jit(solution)/shard_map/ppermute | solution.py:75
  28.6 5.7 %collective-permute-done.7.both.refs_2_ = f32[64,2048]{1,0:T(8,128)S(1)} collective-permute-done((f32[64,2048]{1,0:T(8,128)S(1)}, f32[64,2048]{1,0:T(8,128)S(1)}, u32[]{:S(2)}, u32[]{:S(2)}) %collective-permute-start.7) | collective-permute-done | bytes 524320 | tf_op jit(solution)/shard_map/ppermute | solution.py:26
  34.4 2.7 %collective-permute-start.8 = (f32[32,2048]{1,0:T(8,128)S(1)}, f32[32,2048]{1,0:T(8,128)S(1)}, u32[]{:S(2)}, u32[]{:S(2)}) collective-permute-start(f32[32,2048]{1,0:T(8,128)S(1)} %shard_map.63), channel_id=1, source_target_pairs={{0,24},{1,7},{2,26},{3,5},{4,28},{5,3},{6,30},{7,1},{8,16},{9,15},... | collective-permute-start | bytes 786440 | tf_op jit(solution)/shard_map/ppermute | solution.py:26
  37.2 2.6 %collective-permute-start.19 = (f32[64,2048]{1,0:T(8,128)S(1)}, f32[64,2048]{1,0:T(8,128)S(1)}, u32[]{:S(2)}, u32[]{:S(2)}) collective-permute-start(f32[64,2048]{1,0:T(8,128)S(1)} %collective-permute-done.7.both.refs_2_), channel_id=1, source_target_pairs={{0,1},{1,0},{2,3},{3,2},{4,5},{5,4},{6,7},{7,6},{8,9},{9,8},{10,11... | collective-permute-start | bytes 1572872 | tf_op jit(solution)/shard_map/ppermute | solution.py:75
  41.0 2.8 %collective-permute-start.16 = (f32[32,2048]{1,0:T(8,128)S(1)}, f32[32,2048]{1,0:T(8,128)S(1)}, u32[]{:S(2)}, u32[]{:S(2)}) collective-permute-start(f32[32,2048]{1,0:T(8,128)S(1)} %collective-permute-done.10.refs_5_), channel_id=1, source_target_pairs={{0,1},{1,0},{2,3},{3,2},{4,5},{5,4},{6,7},{7,6},{8,9},{9,8},{10,11... | collective-permute-start | bytes 786440 | tf_op jit(solution)/shard_map/ppermute | solution.py:75
  43.9 2.8 %collective-permute-start.12 = (f32[64,2048]{1,0:T(8,128)S(1)}, f32[64,2048]{1,0:T(8,128)S(1)}, u32[]{:S(2)}, u32[]{:S(2)}) collective-permute-start(f32[64,2048]{1,0:T(8,128)S(1)} %collective-permute-done.3.both.refs_1_), channel_id=1, source_target_pairs={{0,1},{1,0},{2,3},{3,2},{4,5},{5,4},{6,7},{7,6},{8,9},{9,8},{10,11... | collective-permute-start | bytes 1572872 | tf_op jit(solution)/shard_map/ppermute | solution.py:75
  50.1 2.1 %shard_map.67 = (bf16[1024,1024]{1,0:T(8,128)(2,1)S(1)}, bf16[1024,1024]{1,0:T(8,128)(2,1)S(1)}, bf16[1024,1024]{1,0:T(8,128)(2,1)S(1)}, bf16[1024,1024]{1,0:T(8...) custom-call(f32[64,2048]{1,0:T(8,128)S(1)} %collective-permute-done., ...), custom_call_target="tpu_custom_call", output_to_operand_aliasing={{0}: (12, {}), {1}: (13, {}), {2}: (14, {}), {3}: (15, {})} | custom-call | tf_op jit(solution)/shard_map/pallas_call | solution.py:306
  52.1 1.8 %shard_map.69 = f32[8,1024]{1,0:T(8,128)S(1)} custom-call(bf16[1024,1024]{1,0:T(8,128)(2,1)S(1)} %get-tuple-element.25.d_high, bf16[1024,1024]{1,0:T(8,128)(2,1)S(1)} %get-tuple-element.26.d_low, bf16[1024,1024]{1,0:T(8,128)(2,1)S(1)} %get-tuple-element.27.high.c_high, bf16[1024,1024]{1,0:T(8,128)(2,1)S(1)} %get-tuple-element.28.low.c_low, ...), custom_call_target="tpu_custom_call" | custom-call | tf_op jit(solution)/shard_map/pallas_call | solution.py:306
  53.9 2.8 %collective-permute-done.21.refs_0_ = f32[8,1024]{1,0:T(8,128)S(1)} collective-permute-done((f32[8,1024]{1,0:T(8,128)S(1)}, f32[8,1024]{1,0:T(8,128)S(1)}, u32[]{:S(2)}, u32[]{:S(2)}) %collective-permute-start.21) | collective-permute-done | bytes 32800 | tf_op jit(solution)/shard_map/ppermute | solution.py:220
  57.5 3.2 %collective-permute-done.22.refs_0_.refs_1_ = f32[8,1024]{1,0:T(8,128)S(1)} collective-permute-done((f32[8,1024]{1,0:T(8,128)S(1)}, f32[8,1024]{1,0:T(8,128)S(1)}, u32[]{:S(2)}, u32[]{:S(2)}) %collective-permute-start.22) | collective-permute-done | bytes 32800 | tf_op jit(solution)/shard_map/ppermute | solution.py:220
  61.3 2.2 %collective-permute-done.23.refs_2_ = f32[8,1024]{1,0:T(8,128)S(1)} collective-permute-done((f32[8,1024]{1,0:T(8,128)S(1)}, f32[8,1024]{1,0:T(8,128)S(1)}, u32[]{:S(2)}, u32[]{:S(2)}) %collective-permute-start.23) | collective-permute-done | bytes 32800 | tf_op jit(solution)/shard_map/ppermute | solution.py:220
  65.4 1.3 %collective-permute-done.24.ahead.refs_0_ = f32[8,1024]{1,0:T(8,128)S(1)} collective-permute-done((f32[8,1024]{1,0:T(8,128)S(1)}, f32[8,1024]{1,0:T(8,128)S(1)}, u32[]{:S(2)}, u32[]{:S(2)}) %collective-permute-start.24) | collective-permute-done | bytes 32800 | tf_op jit(solution)/shard_map/ppermute | solution.py:220
  66.7 2.3 %collective-permute-start.25 = (f32[8,1024]{1,0:T(8,128)S(1)}, f32[8,1024]{1,0:T(8,128)S(1)}, u32[]{:S(2)}, u32[]{:S(2)}) collective-permute-start(f32[8,1024]{1,0:T(8,128)S(1)} %shard_map.73), channel_id=1, source_target_pairs={{64,32},{32,64},{0,96},{96,0},{65,33},{33,65},{1,97},{97,1},{66,34... | collective-permute-start | bytes 98312 | tf_op jit(solution)/shard_map/ppermute | solution.py:220
  69.0 1.7 %collective-permute-done.25.ahead.refs_1_ = f32[8,1024]{1,0:T(8,128)S(1)} collective-permute-done((f32[8,1024]{1,0:T(8,128)S(1)}, f32[8,1024]{1,0:T(8,128)S(1)}, u32[]{:S(2)}, u32[]{:S(2)}) %collective-permute-start.25) | collective-permute-done | bytes 32800 | tf_op jit(solution)/shard_map/ppermute | solution.py:220
  70.7 3.0 %collective-permute-start.26 = (f32[8,1024]{1,0:T(8,128)S(1)}, f32[8,1024]{1,0:T(8,128)S(1)}, u32[]{:S(2)}, u32[]{:S(2)}) collective-permute-start(f32[8,1024]{1,0:T(8,128)S(1)} %shard_map.74), channel_id=1, source_target_pairs={{32,0},{0,32},{64,96},{96,64},{33,1},{1,33},{65,97},{97,65},{34,2}... | collective-permute-start | bytes 98312 | tf_op jit(solution)/shard_map/ppermute | solution.py:220
  73.7 1.3 %collective-permute-done.26.refs_2_ = f32[8,1024]{1,0:T(8,128)S(1)} collective-permute-done((f32[8,1024]{1,0:T(8,128)S(1)}, f32[8,1024]{1,0:T(8,128)S(1)}, u32[]{:S(2)}, u32[]{:S(2)}) %collective-permute-start.26) | collective-permute-done | bytes 32800 | tf_op jit(solution)/shard_map/ppermute | solution.py:220
  75.0 2.1 %shard_map.75 = f32[32,8,128]{2,1,0:T(8,128)S(1)} custom-call(bf16[1024,1024]{1,0:T(8,128)(2,1)S(1)} %get-tuple-element.25.d_high, bf16[1024,1024]{1,0:T(8,128)(2,1)S(1)} %get-tuple-element.26.d_low, bf16[1024,1024]{1,0:T(8,128)(2,1)S(1)} %get-tuple-element.29.c_high, bf16[1024,1024]{1,0:T(8,128)(2,1)S(1)} %get-tuple-element.30.c_low, ...), custom_call_target="tpu_custom_call" | custom-call | tf_op jit(solution)/shard_map/pallas_call | solution.py:306
  77.1 18.3 %all_to_all.5 = f32[32,8,128]{2,1,0:T(8,128)S(1)} all-to-all(f32[32,8,128]{2,1,0:T(8,128)S(1)} %shard_map.75), channel_id=1, replica_groups=mesh['depth'=4,'panel'=32] {'panel'}, dimensions={0} | all-to-all | bytes 262144 | tf_op jit(solution)/shard_map/all_to_all | solution.py:374
  (49 shorter events, 12.1 us)
Async XLA Ops:
  1.6 7.9 %collective-permute-start.1 = (f32[32,2048]{1,0:T(8,128)S(1)}, f32[32,2048]{1,0:T(8,128)S(1)}, u32[]{:S(2)}, u32[]{:S(2)}) collective-permute-start(f32[32,2048]{1,0:T(8,128)S(1)} %shard_map.59.first), channel_id=1, source_target_pairs={{0,4},{1,17},{2,6},{3,19},{4,0},{5,21},{6,2},{7,23},{8,12},{9,25},... | collective-permute-start | bytes 786440 | tf_op jit(solution)/shard_map/ppermute | solution.py:26
  5.4 6.9 %collective-permute-start = (f32[32,2048]{1,0:T(8,128)S(1)}, f32[32,2048]{1,0:T(8,128)S(1)}, u32[]{:S(2)}, u32[]{:S(2)}) collective-permute-start(f32[32,2048]{1,0:T(8,128)S(1)} %shard_map.59.first), channel_id=1, source_target_pairs={{0,6},{1,25},{2,4},{3,27},{4,2},{5,29},{6,0},{7,31},{8,14},{9,17},... | collective-permute-start | bytes 786440 | tf_op jit(solution)/shard_map/ppermute | solution.py:26
  12.3 14.9 %collective-permute-start.3 = (f32[64,2048]{1,0:T(8,128)S(1)}, f32[64,2048]{1,0:T(8,128)S(1)}, u32[]{:S(2)}, u32[]{:S(2)}) collective-permute-start(f32[64,2048]{1,0:T(8,128)S(1)} %shard_map.60.refs_1_), channel_id=1, source_target_pairs={{0,24},{1,7},{2,26},{3,5},{4,28},{5,3},{6,30},{7,1},{8,16},{9,15},... | collective-permute-start | bytes 1572872 | tf_op jit(solution)/shard_map/ppermute | solution.py:26
  16.2 5.7 %collective-permute-start.4 = (f32[32,2048]{1,0:T(8,128)S(1)}, f32[32,2048]{1,0:T(8,128)S(1)}, u32[]{:S(2)}, u32[]{:S(2)}) collective-permute-start(f32[32,2048]{1,0:T(8,128)S(1)} %shard_map.59.first), channel_id=1, source_target_pairs={{0,2},{1,9},{2,0},{3,11},{4,6},{5,13},{6,4},{7,15},{8,10},{9,1},{1... | collective-permute-start | bytes 786440 | tf_op jit(solution)/shard_map/ppermute | solution.py:26
  17.5 10.8 %collective-permute-start.2 = (f32[64,2048]{1,0:T(8,128)S(1)}, f32[64,2048]{1,0:T(8,128)S(1)}, u32[]{:S(2)}, u32[]{:S(2)}) collective-permute-start(f32[64,2048]{1,0:T(8,128)S(1)} %shard_map.60.refs_1_), channel_id=1, source_target_pairs={{0,8},{1,3},{2,10},{3,1},{4,12},{5,7},{6,14},{7,5},{8,0},{9,11},{1... | collective-permute-start | bytes 1572872 | tf_op jit(solution)/shard_map/ppermute | solution.py:26
  22.0 12.3 %collective-permute-start.7 = (f32[64,2048]{1,0:T(8,128)S(1)}, f32[64,2048]{1,0:T(8,128)S(1)}, u32[]{:S(2)}, u32[]{:S(2)}) collective-permute-start(f32[64,2048]{1,0:T(8,128)S(1)} %shard_map.61.refs_0_), channel_id=1, source_target_pairs={{0,8},{1,3},{2,10},{3,1},{4,12},{5,7},{6,14},{7,5},{8,0},{9,11},{1... | collective-permute-start | bytes 1572872 | tf_op jit(solution)/shard_map/ppermute | solution.py:26
  22.1 12.3 %collective-permute-start.5 = (f32[64,2048]{1,0:T(8,128)S(1)}, f32[64,2048]{1,0:T(8,128)S(1)}, u32[]{:S(2)}, u32[]{:S(2)}) collective-permute-start(f32[64,2048]{1,0:T(8,128)S(1)} %shard_map.61.refs_0_), channel_id=1, source_target_pairs={{0,24},{1,7},{2,26},{3,5},{4,28},{5,3},{6,30},{7,1},{8,16},{9,15},... | collective-permute-start | bytes 1572872 | tf_op jit(solution)/shard_map/ppermute | solution.py:26
  22.1 14.9 %collective-permute-start.18 = (f32[64,2048]{1,0:T(8,128)S(1)}, f32[64,2048]{1,0:T(8,128)S(1)}, u32[]{:S(2)}, u32[]{:S(2)}) collective-permute-start(f32[64,2048]{1,0:T(8,128)S(1)} %shard_map.60.refs_1_), channel_id=1, source_target_pairs={{0,1},{1,0},{2,3},{3,2},{4,5},{5,4},{6,7},{7,6},{8,9},{9,8},{10,11... | collective-permute-start | bytes 1572872 | tf_op jit(solution)/shard_map/ppermute | solution.py:75
  27.3 9.9 %collective-permute-start.17 = (f32[64,2048]{1,0:T(8,128)S(1)}, f32[64,2048]{1,0:T(8,128)S(1)}, u32[]{:S(2)}, u32[]{:S(2)}) collective-permute-start(f32[64,2048]{1,0:T(8,128)S(1)} %shard_map.61.refs_0_), channel_id=1, source_target_pairs={{0,1},{1,0},{2,3},{3,2},{4,5},{5,4},{6,7},{7,6},{8,9},{9,8},{10,11... | collective-permute-start | bytes 1572872 | tf_op jit(solution)/shard_map/ppermute | solution.py:75
  28.4 11.5 %collective-permute-start.10 = (f32[32,2048]{1,0:T(8,128)S(1)}, f32[32,2048]{1,0:T(8,128)S(1)}, u32[]{:S(2)}, u32[]{:S(2)}) collective-permute-start(f32[32,2048]{1,0:T(8,128)S(1)} %shard_map.65), channel_id=1, source_target_pairs={{0,8},{1,3},{2,10},{3,1},{4,12},{5,7},{6,14},{7,5},{8,0},{9,11},{1... | collective-permute-start | bytes 786440 | tf_op jit(solution)/shard_map/ppermute | solution.py:26
  34.3 6.7 %collective-permute-start.9 = (f32[32,2048]{1,0:T(8,128)S(1)}, f32[32,2048]{1,0:T(8,128)S(1)}, u32[]{:S(2)}, u32[]{:S(2)}) collective-permute-start(f32[32,2048]{1,0:T(8,128)S(1)} %shard_map.64), channel_id=1, source_target_pairs={{0,24},{1,7},{2,26},{3,5},{4,28},{5,3},{6,30},{7,1},{8,16},{9,15},... | collective-permute-start | bytes 786440 | tf_op jit(solution)/shard_map/ppermute | solution.py:26
  34.4 9.5 %collective-permute-start.8 = (f32[32,2048]{1,0:T(8,128)S(1)}, f32[32,2048]{1,0:T(8,128)S(1)}, u32[]{:S(2)}, u32[]{:S(2)}) collective-permute-start(f32[32,2048]{1,0:T(8,128)S(1)} %shard_map.63), channel_id=1, source_target_pairs={{0,24},{1,7},{2,26},{3,5},{4,28},{5,3},{6,30},{7,1},{8,16},{9,15},... | collective-permute-start | bytes 786440 | tf_op jit(solution)/shard_map/ppermute | solution.py:26
  37.1 9.6 %collective-permute-start.6 = (f32[32,2048]{1,0:T(8,128)S(1)}, f32[32,2048]{1,0:T(8,128)S(1)}, u32[]{:S(2)}, u32[]{:S(2)}) collective-permute-start(f32[32,2048]{1,0:T(8,128)S(1)} %shard_map.62), channel_id=1, source_target_pairs={{0,8},{1,3},{2,10},{3,1},{4,12},{5,7},{6,14},{7,5},{8,0},{9,11},{1... | collective-permute-start | bytes 786440 | tf_op jit(solution)/shard_map/ppermute | solution.py:26
  37.2 10.0 %collective-permute-start.19 = (f32[64,2048]{1,0:T(8,128)S(1)}, f32[64,2048]{1,0:T(8,128)S(1)}, u32[]{:S(2)}, u32[]{:S(2)}) collective-permute-start(f32[64,2048]{1,0:T(8,128)S(1)} %collective-permute-done.7.both.refs_2_), channel_id=1, source_target_pairs={{0,1},{1,0},{2,3},{3,2},{4,5},{5,4},{6,7},{7,6},{8,9},{9,8},{10,11... | collective-permute-start | bytes 1572872 | tf_op jit(solution)/shard_map/ppermute | solution.py:75
  39.8 7.4 %collective-permute-start.20 = (f32[64,2048]{1,0:T(8,128)S(1)}, f32[64,2048]{1,0:T(8,128)S(1)}, u32[]{:S(2)}, u32[]{:S(2)}) collective-permute-start(f32[64,2048]{1,0:T(8,128)S(1)} %collective-permute-done.5.both.refs_3_), channel_id=1, source_target_pairs={{0,1},{1,0},{2,3},{3,2},{4,5},{5,4},{6,7},{7,6},{8,9},{9,8},{10,11... | collective-permute-start | bytes 1572872 | tf_op jit(solution)/shard_map/ppermute | solution.py:75
  41.0 5.7 %collective-permute-start.16 = (f32[32,2048]{1,0:T(8,128)S(1)}, f32[32,2048]{1,0:T(8,128)S(1)}, u32[]{:S(2)}, u32[]{:S(2)}) collective-permute-start(f32[32,2048]{1,0:T(8,128)S(1)} %collective-permute-done.10.refs_5_), channel_id=1, source_target_pairs={{0,1},{1,0},{2,3},{3,2},{4,5},{5,4},{6,7},{7,6},{8,9},{9,8},{10,11... | collective-permute-start | bytes 786440 | tf_op jit(solution)/shard_map/ppermute | solution.py:75
  43.9 4.7 %collective-permute-start.12 = (f32[64,2048]{1,0:T(8,128)S(1)}, f32[64,2048]{1,0:T(8,128)S(1)}, u32[]{:S(2)}, u32[]{:S(2)}) collective-permute-start(f32[64,2048]{1,0:T(8,128)S(1)} %collective-permute-done.3.both.refs_1_), channel_id=1, source_target_pairs={{0,1},{1,0},{2,3},{3,2},{4,5},{5,4},{6,7},{7,6},{8,9},{9,8},{10,11... | collective-permute-start | bytes 1572872 | tf_op jit(solution)/shard_map/ppermute | solution.py:75
  47.3 2.8 %collective-permute-start.13 = (f32[32,2048]{1,0:T(8,128)S(1)}, f32[32,2048]{1,0:T(8,128)S(1)}, u32[]{:S(2)}, u32[]{:S(2)}) collective-permute-start(f32[32,2048]{1,0:T(8,128)S(1)} %collective-permute-done.6.refs_2_), channel_id=1, source_target_pairs={{0,1},{1,0},{2,3},{3,2},{4,5},{5,4},{6,7},{7,6},{8,9},{9,8},{10,11... | collective-permute-start | bytes 786440 | tf_op jit(solution)/shard_map/ppermute | solution.py:75
  53.9 2.8 %collective-permute-start.21 = (f32[8,1024]{1,0:T(8,128)S(1)}, f32[8,1024]{1,0:T(8,128)S(1)}, u32[]{:S(2)}, u32[]{:S(2)}) collective-permute-start(f32[8,1024]{1,0:T(8,128)S(1)} %shard_map.69), channel_id=1, source_target_pairs={{0,32},{32,0},{64,96},{96,64},{1,33},{33,1},{65,97},{97,65},{2,34}... | collective-permute-start | bytes 98312 | tf_op jit(solution)/shard_map/ppermute | solution.py:220
  56.7 4.0 %collective-permute-start.22 = (f32[8,1024]{1,0:T(8,128)S(1)}, f32[8,1024]{1,0:T(8,128)S(1)}, u32[]{:S(2)}, u32[]{:S(2)}) collective-permute-start(f32[8,1024]{1,0:T(8,128)S(1)} %shard_map.70), channel_id=1, source_target_pairs={{32,64},{64,32},{0,96},{96,0},{33,65},{65,33},{1,97},{97,1},{34,66... | collective-permute-start | bytes 98312 | tf_op jit(solution)/shard_map/ppermute | solution.py:220
  60.7 2.8 %collective-permute-start.23 = (f32[8,1024]{1,0:T(8,128)S(1)}, f32[8,1024]{1,0:T(8,128)S(1)}, u32[]{:S(2)}, u32[]{:S(2)}) collective-permute-start(f32[8,1024]{1,0:T(8,128)S(1)} %shard_map.71), channel_id=1, source_target_pairs={{64,96},{96,64},{0,32},{32,0},{65,97},{97,65},{1,33},{33,1},{66,98... | collective-permute-start | bytes 98312 | tf_op jit(solution)/shard_map/ppermute | solution.py:220
  63.5 3.2 %collective-permute-start.24 = (f32[8,1024]{1,0:T(8,128)S(1)}, f32[8,1024]{1,0:T(8,128)S(1)}, u32[]{:S(2)}, u32[]{:S(2)}) collective-permute-start(f32[8,1024]{1,0:T(8,128)S(1)} %get-tuple-element.35), channel_id=1, source_target_pairs={{96,64},{64,96},{0,32},{32,0},{97,65},{65,97},{1,33},{33,1},{98,66... | collective-permute-start | bytes 98312 | tf_op jit(solution)/shard_map/ppermute | solution.py:220
  66.7 4.0 %collective-permute-start.25 = (f32[8,1024]{1,0:T(8,128)S(1)}, f32[8,1024]{1,0:T(8,128)S(1)}, u32[]{:S(2)}, u32[]{:S(2)}) collective-permute-start(f32[8,1024]{1,0:T(8,128)S(1)} %shard_map.73), channel_id=1, source_target_pairs={{64,32},{32,64},{0,96},{96,0},{65,33},{33,65},{1,97},{97,1},{66,34... | collective-permute-start | bytes 98312 | tf_op jit(solution)/shard_map/ppermute | solution.py:220
  70.7 4.3 %collective-permute-start.26 = (f32[8,1024]{1,0:T(8,128)S(1)}, f32[8,1024]{1,0:T(8,128)S(1)}, u32[]{:S(2)}, u32[]{:S(2)}) collective-permute-start(f32[8,1024]{1,0:T(8,128)S(1)} %shard_map.74), channel_id=1, source_target_pairs={{32,0},{0,32},{64,96},{96,64},{33,1},{1,33},{65,97},{97,65},{34,2}... | collective-permute-start | bytes 98312 | tf_op jit(solution)/shard_map/ppermute | solution.py:220
  (3 other events, 7.8 us)

commit v3 on v2

--- a/solution.py
+++ b/solution.py
@@ -73,6 +73,13 @@
     ]
     pieces = [a, b, a0, a1, b0, b1, *far_pieces]
     return pieces + [lax.ppermute(piece, "panel", SIBLINGS) for piece in pieces]
+
+
+COLUMNS = 16
+
+
+def sweeps():
+    return lax.rem(lax.axis_index("panel"), 2) == 1
 
 
 def split(x):
@@ -191,9 +198,11 @@
             block = d_high[rows, where].astype(F32) + d_low[rows, where].astype(F32)
             d_high[where, rows], d_low[where, rows] = split(block.T)
 
-    pick = lax.broadcasted_iota(jnp.int32, (8, cols), 1) == (
-        lax.broadcasted_iota(jnp.int32, (8, cols), 0) + lax.axis_index("panel") * 8
-    )
+    line = lax.broadcasted_iota(jnp.int32, (COLUMNS, cols), 0)
+    few = COLUMNS // 2
+    mine = line + lax.div(lax.axis_index("panel"), 2) * few
+    mine = jnp.where(line < few, mine, mine + cols // 2 - few)
+    pick = lax.broadcasted_iota(jnp.int32, (COLUMNS, cols), 1) == mine
     own = lax.dot_general(
         pick.astype(F32),
         side[:, 0:cols],
@@ -209,7 +218,7 @@
         tiles = slice(start, start + LANES)
         tile = d_high[tiles, tiles].astype(F32) + d_low[tiles, tiles].astype(F32)
         line = jnp.sum(jnp.where(eye, tile, 0.0), axis=0, keepdims=True)
-        diag[:, start : start + LANES] = jnp.broadcast_to(line, (8, LANES))
+        diag[:, start : start + LANES] = jnp.broadcast_to(line, (COLUMNS, LANES))
     line = jnp.sum(side[:, cols : cols + LANES], axis=0, keepdims=True)
     wanted[...] = jnp.broadcast_to(line, (8, LANES))
 
@@ -228,7 +237,7 @@
 
 
 def forward_kernel(stage, d_high, d_low, c_high, c_low, source, diag, *refs):
-    @pl.when(lax.axis_index("depth") == stage)
+    @pl.when(sweeps() & (lax.axis_index("depth") == stage))
     def _():
         right_hand = source[...] - refs[0][...] if stage else source[...]
         forward = jacobi(right_hand, diag[...], d_high, d_low)
@@ -236,7 +245,7 @@
 
 
 def transpose_kernel(last, high, low, high_turned, low_turned):
-    @pl.when(lax.axis_index("depth") != last)
+    @pl.when(sweeps() & (lax.axis_index("depth") != last))
     def _():
         for ref, turned in ((high, high_turned), (low, low_turned)):
             for row in range(0, ref.shape[0], LANES):
@@ -249,51 +258,58 @@
     right_hand = source[...] - taken(lax.axis_index("depth"), range(1, count + 1), refs[:count])
     refs[count][...] = right_hand
 
-    @pl.when(lax.axis_index("depth") == count)
+    @pl.when(sweeps() & (lax.axis_index("depth") == count))
     def _():
         refs[count + 1][...] = jacobi(right_hand, diag[...], d_high, d_low)
 
 
 def backward_kernel(plane, d_high, d_low, c_high, c_low, right_hand, diag, ahead, panel):
-    @pl.when(lax.axis_index("depth") == plane)
+    @pl.when(sweeps() & (lax.axis_index("depth") == plane))
     def _():
         rest = right_hand[...] - product(ahead[...], c_high, c_low)
         panel[...] = jacobi(rest, diag[...], d_high, d_low)
 
 
 def last_kernel(count, d_high, d_low, c_high, c_low, right_hand, diag, wanted, *refs):
-    ahead = taken(lax.axis_index("depth"), range(count - 1, -1, -1), refs[:count])
-    coupled = jnp.where(lax.axis_index("depth") == count, 0.0, product(ahead, c_high, c_low))
-    panel = jacobi(right_hand[...] - coupled, diag[...], d_high, d_low)
-    size = panel.shape[1]
-    high = panel.astype(BF16)
-    rest = panel - high.astype(F32)
-    middle = rest.astype(BF16)
-    low = (rest - middle.astype(F32)).astype(BF16)
-    line = wanted[0:1, :].astype(jnp.int32)
-    chosen = (lax.broadcasted_iota(jnp.int32, (size, LANES), 0) == line).astype(BF16)
-    parts = [jnp.dot(part, chosen, preferred_element_type=F32) for part in (high, middle, low)]
-    picked = parts[0] + parts[1] + parts[2]
-    send = refs[count]
-    blocks = send.shape[0]
-    own, few = size // blocks, LANES // blocks
-    filler = jnp.zeros((8, LANES - own - few), F32)
-    for block in range(blocks):
-        send[block] = jnp.concatenate(
-            [
-                panel[:, block * own : (block + 1) * own],
-                picked[:, block * few : (block + 1) * few],
-                filler,
-            ],
-            1,
-        )
+    @pl.when(sweeps())
+    def _():
+        ahead = taken(lax.axis_index("depth"), range(count - 1, -1, -1), refs[:count])
+        coupled = product(ahead, c_high, c_low)
+        coupled = jnp.where(lax.axis_index("depth") == count, 0.0, coupled)
+        panel = jacobi(right_hand[...] - coupled, diag[...], d_high, d_low)
+        size = panel.shape[1]
+        high = panel.astype(BF16)
+        rest = panel - high.astype(F32)
+        middle = rest.astype(BF16)
+        low = (rest - middle.astype(F32)).astype(BF16)
+        line = wanted[0:1, :].astype(jnp.int32)
+        chosen = (lax.broadcasted_iota(jnp.int32, (size, LANES), 0) == line).astype(BF16)
+        parts = [jnp.dot(x, chosen, preferred_element_type=F32) for x in (high, middle, low)]
+        picked = parts[0] + parts[1] + parts[2]
+        send = refs[count]
+        blocks = send.shape[0]
+        own, few = size // blocks, LANES // blocks
+        lines = COLUMNS // 2
+        filler = jnp.zeros((lines, LANES // 2 - own - few), F32)
+        for block in range(blocks):
+            tile = []
+            for half in range(2):
+                rows = slice(half * lines, (half + 1) * lines)
+                tile.append(panel[rows, block * own : (block + 1) * own])
+                tile.append(picked[rows, block * few : (block + 1) * few])
+                tile.append(filler)
+            send[block] = jnp.concatenate(tile, 1)
 
 
 def unpack_kernel(got, panels, picked):
-    turned = got[...].T
-    own = panels.shape[0]
-    panels[...] = turned[:own]
-    picked[...] = turned[own : own + picked.shape[0]]
+    turned = jnp.concatenate([got[k] for k in range(1, got.shape[0], 2)], 0).T
+    own, few = panels.shape[0], picked.shape[0]
+    width = turned.shape[1]
+    for half in range(2):
+        at = half * LANES // 2
+        cols = slice(half * width, (half + 1) * width)
+        panels[:, cols] = turned[at : at + own]
+        picked[:, cols] = turned[at + own : at + own + few]
 
 
 def vmem(shape, dtype=F32):
@@ -329,7 +345,7 @@
     )(*[pltpu.with_memory_space_constraint(x, pltpu.HBM) for x in operands])
     pieces = gathered(packed)
 
-    vec = vmem((8, size))
+    vec = vmem((COLUMNS, size))
     mat = vmem((size, size), BF16)
     filled = call(
         early_kernel,
@@ -368,10 +384,10 @@
             )
     send = call(
         functools.partial(last_kernel, last),
-        vmem((size // rows, 8, LANES)),
+        vmem((size // rows, COLUMNS // 2, LANES)),
         d_high, d_low, *turned, right_hand, diag, wanted, *aheads,
     )
-    got = lax.all_to_all(send, "panel", 0, 0, tiled=True).reshape(cols, LANES)
+    got = lax.all_to_all(send, "panel", 0, 0, tiled=True)
     panels, picked = call(
         unpack_kernel,
         (jax.ShapeDtypeStruct((rows, cols), F32), jax.ShapeDtypeStruct((few, cols), F32)),

time: 96.2 us -> 97.3 us (1.011)
  blocking collectives: 18.3 us -> 12.3 us
  starting transfers between devices: 34.9 us -> 39.1 us
  waiting for transfers between devices: 32.1 us -> 34.3 us
    all_to_all x1, blocking collectives: 18.3 us -> 12.3 us  [per_device(): got = lax.all_to_all(send, 'panel', 0, 0, tiled=True)]
    ppermute x6, starting transfers between devices: 7.32 us -> 11.4 us  [hop(): return lax.ppermute(block, 'depth', route)]
    ppermute x6, waiting for transfers between devices: 12.4 us -> 14.6 us  [hop(): return lax.ppermute(block, 'depth', route)]
where the time goes in v3:
time: 97.3 us; the launch traced here: 97.1 us
  starting transfers between devices  39.1 us (40%)
  waiting for transfers between devices  34.3 us (35%)
  blocking collectives  12.3 us (13%)
  Pallas kernels  10.7 us (11%)
    ppermute x11, waiting for transfers between devices, from_partner(): return lax.ppermute(block, 'panel', pairs)  18.2 us
    ppermute x10, starting transfers between devices, gathered(): return pieces + [lax.ppermute(piece, 'panel', SIBLINGS) for piece in pieces]  14.6 us
    ppermute x6, waiting for transfers between devices, hop(): return lax.ppermute(block, 'depth', route)  14.6 us
    ppermute x11, starting transfers between devices, from_partner(): return lax.ppermute(block, 'panel', pairs)  13 us
    all_to_all x1, blocking collectives, per_device(): got = lax.all_to_all(send, 'panel', 0, 0, tiled=True)  12.3 us
    ppermute x6, starting transfers between devices, hop(): return lax.ppermute(block, 'depth', route)  11.4 us
    pallas_call x17, Pallas kernels, call(): pl.pallas_call(kernel, out_shape=out_shape, in_specs=[space] * len(args),...  9.7 us
  transfers between devices with their start and end apart: 27, of which 15 were waited for; matrix products, arithmetic and copies ran while one was open for 0% of the time, Pallas kernels for 2%

profile of v3, /device:TPU:1, one launch (start us, length us, event | category | flops | bytes accessed | tf_op | source)
XLA Modules:
  0.0 97.1 jit_solution(17711361430788685279)
XLA Ops:
  1.6 3.8 %collective-permute-start.1 = (f32[32,2048]{1,0:T(8,128)S(1)}, f32[32,2048]{1,0:T(8,128)S(1)}, u32[]{:S(2)}, u32[]{:S(2)}) collective-permute-start(f32[32,2048]{1,0:T(8,128)S(1)} %shard_map.59.first), channel_id=1, source_target_pairs={{0,4},{1,17},{2,6},{3,19},{4,0},{5,21},{6,2},{7,23},{8,12},{9,25},... | collective-permute-start | bytes 786440 | tf_op jit(solution)/shard_map/ppermute | solution.py:26
  6.2 3.3 %collective-permute-done.1.second = f32[32,2048]{1,0:T(8,128)S(1)} collective-permute-done((f32[32,2048]{1,0:T(8,128)S(1)}, f32[32,2048]{1,0:T(8,128)S(1)}, u32[]{:S(2)}, u32[]{:S(2)}) %collective-permute-start.1) | collective-permute-done | bytes 262176 | tf_op jit(solution)/shard_map/ppermute | solution.py:26
  9.5 2.8 %collective-permute-done.first = f32[32,2048]{1,0:T(8,128)S(1)} collective-permute-done((f32[32,2048]{1,0:T(8,128)S(1)}, f32[32,2048]{1,0:T(8,128)S(1)}, u32[]{:S(2)}, u32[]{:S(2)}) %collective-permute-start) | collective-permute-done | bytes 262176 | tf_op jit(solution)/shard_map/ppermute | solution.py:26
  12.3 3.9 %collective-permute-start.3 = (f32[64,2048]{1,0:T(8,128)S(1)}, f32[64,2048]{1,0:T(8,128)S(1)}, u32[]{:S(2)}, u32[]{:S(2)}) collective-permute-start(f32[64,2048]{1,0:T(8,128)S(1)} %shard_map.60.refs_1_), channel_id=1, source_target_pairs={{0,24},{1,7},{2,26},{3,5},{4,28},{5,3},{6,30},{7,1},{8,16},{9,15},... | collective-permute-start | bytes 1572872 | tf_op jit(solution)/shard_map/ppermute | solution.py:26
  16.2 1.3 %collective-permute-start.4 = (f32[32,2048]{1,0:T(8,128)S(1)}, f32[32,2048]{1,0:T(8,128)S(1)}, u32[]{:S(2)}, u32[]{:S(2)}) collective-permute-start(f32[32,2048]{1,0:T(8,128)S(1)} %shard_map.59.first), channel_id=1, source_target_pairs={{0,2},{1,9},{2,0},{3,11},{4,6},{5,13},{6,4},{7,15},{8,10},{9,1},{1... | collective-permute-start | bytes 786440 | tf_op jit(solution)/shard_map/ppermute | solution.py:26
  17.5 4.4 %collective-permute-done.4.second = f32[32,2048]{1,0:T(8,128)S(1)} collective-permute-done((f32[32,2048]{1,0:T(8,128)S(1)}, f32[32,2048]{1,0:T(8,128)S(1)}, u32[]{:S(2)}, u32[]{:S(2)}) %collective-permute-start.4) | collective-permute-done | bytes 262176 | tf_op jit(solution)/shard_map/ppermute | solution.py:26
  22.1 5.1 %collective-permute-start.18 = (f32[64,2048]{1,0:T(8,128)S(1)}, f32[64,2048]{1,0:T(8,128)S(1)}, u32[]{:S(2)}, u32[]{:S(2)}) collective-permute-start(f32[64,2048]{1,0:T(8,128)S(1)} %shard_map.60.refs_1_), channel_id=1, source_target_pairs={{0,1},{1,0},{2,3},{3,2},{4,5},{5,4},{6,7},{7,6},{8,9},{9,8},{10,11... | collective-permute-start | bytes 1572872 | tf_op jit(solution)/shard_map/ppermute | solution.py:75
  28.6 5.7 %collective-permute-done.7.both.refs_2_ = f32[64,2048]{1,0:T(8,128)S(1)} collective-permute-done((f32[64,2048]{1,0:T(8,128)S(1)}, f32[64,2048]{1,0:T(8,128)S(1)}, u32[]{:S(2)}, u32[]{:S(2)}) %collective-permute-start.7) | collective-permute-done | bytes 524320 | tf_op jit(solution)/shard_map/ppermute | solution.py:26
  34.4 2.7 %collective-permute-start.8 = (f32[32,2048]{1,0:T(8,128)S(1)}, f32[32,2048]{1,0:T(8,128)S(1)}, u32[]{:S(2)}, u32[]{:S(2)}) collective-permute-start(f32[32,2048]{1,0:T(8,128)S(1)} %shard_map.63), channel_id=1, source_target_pairs={{0,24},{1,7},{2,26},{3,5},{4,28},{5,3},{6,30},{7,1},{8,16},{9,15},... | collective-permute-start | bytes 786440 | tf_op jit(solution)/shard_map/ppermute | solution.py:26
  37.2 2.6 %collective-permute-start.19 = (f32[64,2048]{1,0:T(8,128)S(1)}, f32[64,2048]{1,0:T(8,128)S(1)}, u32[]{:S(2)}, u32[]{:S(2)}) collective-permute-start(f32[64,2048]{1,0:T(8,128)S(1)} %collective-permute-done.7.both.refs_2_), channel_id=1, source_target_pairs={{0,1},{1,0},{2,3},{3,2},{4,5},{5,4},{6,7},{7,6},{8,9},{9,8},{10,11... | collective-permute-start | bytes 1572872 | tf_op jit(solution)/shard_map/ppermute | solution.py:75
  41.0 2.8 %collective-permute-start.16 = (f32[32,2048]{1,0:T(8,128)S(1)}, f32[32,2048]{1,0:T(8,128)S(1)}, u32[]{:S(2)}, u32[]{:S(2)}) collective-permute-start(f32[32,2048]{1,0:T(8,128)S(1)} %collective-permute-done.10.refs_5_), channel_id=1, source_target_pairs={{0,1},{1,0},{2,3},{3,2},{4,5},{5,4},{6,7},{7,6},{8,9},{9,8},{10,11... | collective-permute-start | bytes 786440 | tf_op jit(solution)/shard_map/ppermute | solution.py:75
  43.9 2.8 %collective-permute-start.12 = (f32[64,2048]{1,0:T(8,128)S(1)}, f32[64,2048]{1,0:T(8,128)S(1)}, u32[]{:S(2)}, u32[]{:S(2)}) collective-permute-start(f32[64,2048]{1,0:T(8,128)S(1)} %collective-permute-done.3.both.refs_1_), channel_id=1, source_target_pairs={{0,1},{1,0},{2,3},{3,2},{4,5},{5,4},{6,7},{7,6},{8,9},{9,8},{10,11... | collective-permute-start | bytes 1572872 | tf_op jit(solution)/shard_map/ppermute | solution.py:75
  50.1 2.0 %shard_map.67 = (bf16[1024,1024]{1,0:T(8,128)(2,1)S(1)}, bf16[1024,1024]{1,0:T(8,128)(2,1)S(1)}, bf16[1024,1024]{1,0:T(8,128)(2,1)S(1)}, bf16[1024,1024]{1,0:T(8...) custom-call(f32[64,2048]{1,0:T(8,128)S(1)} %collective-permute-done., ...), custom_call_target="tpu_custom_call", output_to_operand_aliasing={{0}: (12, {}), {1}: (13, {}), {2}: (14, {}), {3}: (15, {})} | custom-call | tf_op jit(solution)/shard_map/pallas_call | solution.py:322
  52.1 2.2 %shard_map.69 = f32[16,1024]{1,0:T(8,128)S(1)} custom-call(bf16[1024,1024]{1,0:T(8,128)(2,1)S(1)} %get-tuple-element.25.d_high, bf16[1024,1024]{1,0:T(8,128)(2,1)S(1)} %get-tuple-element.26.d_low, bf16[1024,1024]{1,0:T(8,128)(2,1)S(1)} %get-tuple-element.27.high.c_high, bf16[1024,1024]{1,0:T(8,128)(2,1)S(1)} %get-tuple-element.28.low.c_low, ...), custom_call_target="tpu_custom_call" | custom-call | tf_op jit(solution)/shard_map/pallas_call | solution.py:322
  54.3 3.1 %collective-permute-done.21.refs_0_ = f32[16,1024]{1,0:T(8,128)S(1)} collective-permute-done((f32[16,1024]{1,0:T(8,128)S(1)}, f32[16,1024]{1,0:T(8,128)S(1)}, u32[]{:S(2)}, u32[]{:S(2)}) %collective-permute-start.21) | collective-permute-done | bytes 65568 | tf_op jit(solution)/shard_map/ppermute | solution.py:229
  57.8 4.7 %collective-permute-done.22.refs_0_.refs_1_ = f32[16,1024]{1,0:T(8,128)S(1)} collective-permute-done((f32[16,1024]{1,0:T(8,128)S(1)}, f32[16,1024]{1,0:T(8,128)S(1)}, u32[]{:S(2)}, u32[]{:S(2)}) %collective-permute-start.22) | collective-permute-done | bytes 65568 | tf_op jit(solution)/shard_map/ppermute | solution.py:229
  63.6 2.0 %collective-permute-done.23.refs_2_ = f32[16,1024]{1,0:T(8,128)S(1)} collective-permute-done((f32[16,1024]{1,0:T(8,128)S(1)}, f32[16,1024]{1,0:T(8,128)S(1)}, u32[]{:S(2)}, u32[]{:S(2)}) %collective-permute-start.23) | collective-permute-done | bytes 65568 | tf_op jit(solution)/shard_map/ppermute | solution.py:229
  65.7 1.8 %collective-permute-start.24 = (f32[16,1024]{1,0:T(8,128)S(1)}, f32[16,1024]{1,0:T(8,128)S(1)}, u32[]{:S(2)}, u32[]{:S(2)}) collective-permute-start(f32[16,1024]{1,0:T(8,128)S(1)} %get-tuple-element.35), channel_id=1, source_target_pairs={{96,64},{64,96},{0,32},{32,0},{97,65},{65,97},{1,33},{33,1},{98,66... | collective-permute-start | bytes 196616 | tf_op jit(solution)/shard_map/ppermute | solution.py:229
  69.1 4.8 %collective-permute-start.25 = (f32[16,1024]{1,0:T(8,128)S(1)}, f32[16,1024]{1,0:T(8,128)S(1)}, u32[]{:S(2)}, u32[]{:S(2)}) collective-permute-start(f32[16,1024]{1,0:T(8,128)S(1)} %shard_map.73), channel_id=1, source_target_pairs={{64,32},{32,64},{0,96},{96,0},{65,33},{33,65},{1,97},{97,1},{66,34... | collective-permute-start | bytes 196616 | tf_op jit(solution)/shard_map/ppermute | solution.py:229
  73.9 1.7 %collective-permute-done.25.ahead.refs_1_ = f32[16,1024]{1,0:T(8,128)S(1)} collective-permute-done((f32[16,1024]{1,0:T(8,128)S(1)}, f32[16,1024]{1,0:T(8,128)S(1)}, u32[]{:S(2)}, u32[]{:S(2)}) %collective-permute-start.25) | collective-permute-done | bytes 65568 | tf_op jit(solution)/shard_map/ppermute | solution.py:229
  75.6 3.4 %collective-permute-start.26 = (f32[16,1024]{1,0:T(8,128)S(1)}, f32[16,1024]{1,0:T(8,128)S(1)}, u32[]{:S(2)}, u32[]{:S(2)}) collective-permute-start(f32[16,1024]{1,0:T(8,128)S(1)} %shard_map.74), channel_id=1, source_target_pairs={{32,0},{0,32},{64,96},{96,64},{33,1},{1,33},{65,97},{97,65},{34,2}... | collective-permute-start | bytes 196616 | tf_op jit(solution)/shard_map/ppermute | solution.py:229
  78.9 2.6 %collective-permute-done.26.refs_2_ = f32[16,1024]{1,0:T(8,128)S(1)} collective-permute-done((f32[16,1024]{1,0:T(8,128)S(1)}, f32[16,1024]{1,0:T(8,128)S(1)}, u32[]{:S(2)}, u32[]{:S(2)}) %collective-permute-start.26) | collective-permute-done | bytes 65568 | tf_op jit(solution)/shard_map/ppermute | solution.py:229
  81.6 2.5 %shard_map.75 = f32[32,8,128]{2,1,0:T(8,128)S(1)} custom-call(bf16[1024,1024]{1,0:T(8,128)(2,1)S(1)} %get-tuple-element.25.d_high, bf16[1024,1024]{1,0:T(8,128)(2,1)S(1)} %get-tuple-element.26.d_low, bf16[1024,1024]{1,0:T(8,128)(2,1)S(1)} %get-tuple-element.29.c_high, bf16[1024,1024]{1,0:T(8,128)(2,1)S(1)} %get-tuple-element.30.c_low, ...), custom_call_target="tpu_custom_call" | custom-call | tf_op jit(solution)/shard_map/pallas_call | solution.py:322
  84.1 12.3 %all_to_all.5.got = f32[32,8,128]{2,1,0:T(8,128)S(1)} all-to-all(f32[32,8,128]{2,1,0:T(8,128)S(1)} %shard_map.75), channel_id=1, replica_groups=mesh['depth'=4,'panel'=32] {'panel'}, dimensions={0} | all-to-all | bytes 262144 | tf_op jit(solution)/shard_map/all_to_all | solution.py:390
  (49 shorter events, 12.0 us)
Async XLA Ops:
  1.6 7.9 %collective-permute-start.1 = (f32[32,2048]{1,0:T(8,128)S(1)}, f32[32,2048]{1,0:T(8,128)S(1)}, u32[]{:S(2)}, u32[]{:S(2)}) collective-permute-start(f32[32,2048]{1,0:T(8,128)S(1)} %shard_map.59.first), channel_id=1, source_target_pairs={{0,4},{1,17},{2,6},{3,19},{4,0},{5,21},{6,2},{7,23},{8,12},{9,25},... | collective-permute-start | bytes 786440 | tf_op jit(solution)/shard_map/ppermute | solution.py:26
  5.4 6.9 %collective-permute-start = (f32[32,2048]{1,0:T(8,128)S(1)}, f32[32,2048]{1,0:T(8,128)S(1)}, u32[]{:S(2)}, u32[]{:S(2)}) collective-permute-start(f32[32,2048]{1,0:T(8,128)S(1)} %shard_map.59.first), channel_id=1, source_target_pairs={{0,6},{1,25},{2,4},{3,27},{4,2},{5,29},{6,0},{7,31},{8,14},{9,17},... | collective-permute-start | bytes 786440 | tf_op jit(solution)/shard_map/ppermute | solution.py:26
  12.3 14.9 %collective-permute-start.3 = (f32[64,2048]{1,0:T(8,128)S(1)}, f32[64,2048]{1,0:T(8,128)S(1)}, u32[]{:S(2)}, u32[]{:S(2)}) collective-permute-start(f32[64,2048]{1,0:T(8,128)S(1)} %shard_map.60.refs_1_), channel_id=1, source_target_pairs={{0,24},{1,7},{2,26},{3,5},{4,28},{5,3},{6,30},{7,1},{8,16},{9,15},... | collective-permute-start | bytes 1572872 | tf_op jit(solution)/shard_map/ppermute | solution.py:26
  16.2 5.7 %collective-permute-start.4 = (f32[32,2048]{1,0:T(8,128)S(1)}, f32[32,2048]{1,0:T(8,128)S(1)}, u32[]{:S(2)}, u32[]{:S(2)}) collective-permute-start(f32[32,2048]{1,0:T(8,128)S(1)} %shard_map.59.first), channel_id=1, source_target_pairs={{0,2},{1,9},{2,0},{3,11},{4,6},{5,13},{6,4},{7,15},{8,10},{9,1},{1... | collective-permute-start | bytes 786440 | tf_op jit(solution)/shard_map/ppermute | solution.py:26
  17.5 10.8 %collective-permute-start.2 = (f32[64,2048]{1,0:T(8,128)S(1)}, f32[64,2048]{1,0:T(8,128)S(1)}, u32[]{:S(2)}, u32[]{:S(2)}) collective-permute-start(f32[64,2048]{1,0:T(8,128)S(1)} %shard_map.60.refs_1_), channel_id=1, source_target_pairs={{0,8},{1,3},{2,10},{3,1},{4,12},{5,7},{6,14},{7,5},{8,0},{9,11},{1... | collective-permute-start | bytes 1572872 | tf_op jit(solution)/shard_map/ppermute | solution.py:26
  22.0 12.3 %collective-permute-start.7 = (f32[64,2048]{1,0:T(8,128)S(1)}, f32[64,2048]{1,0:T(8,128)S(1)}, u32[]{:S(2)}, u32[]{:S(2)}) collective-permute-start(f32[64,2048]{1,0:T(8,128)S(1)} %shard_map.61.refs_0_), channel_id=1, source_target_pairs={{0,8},{1,3},{2,10},{3,1},{4,12},{5,7},{6,14},{7,5},{8,0},{9,11},{1... | collective-permute-start | bytes 1572872 | tf_op jit(solution)/shard_map/ppermute | solution.py:26
  22.1 12.3 %collective-permute-start.5 = (f32[64,2048]{1,0:T(8,128)S(1)}, f32[64,2048]{1,0:T(8,128)S(1)}, u32[]{:S(2)}, u32[]{:S(2)}) collective-permute-start(f32[64,2048]{1,0:T(8,128)S(1)} %shard_map.61.refs_0_), channel_id=1, source_target_pairs={{0,24},{1,7},{2,26},{3,5},{4,28},{5,3},{6,30},{7,1},{8,16},{9,15},... | collective-permute-start | bytes 1572872 | tf_op jit(solution)/shard_map/ppermute | solution.py:26
  22.1 14.9 %collective-permute-start.18 = (f32[64,2048]{1,0:T(8,128)S(1)}, f32[64,2048]{1,0:T(8,128)S(1)}, u32[]{:S(2)}, u32[]{:S(2)}) collective-permute-start(f32[64,2048]{1,0:T(8,128)S(1)} %shard_map.60.refs_1_), channel_id=1, source_target_pairs={{0,1},{1,0},{2,3},{3,2},{4,5},{5,4},{6,7},{7,6},{8,9},{9,8},{10,11... | collective-permute-start | bytes 1572872 | tf_op jit(solution)/shard_map/ppermute | solution.py:75
  27.3 9.9 %collective-permute-start.17 = (f32[64,2048]{1,0:T(8,128)S(1)}, f32[64,2048]{1,0:T(8,128)S(1)}, u32[]{:S(2)}, u32[]{:S(2)}) collective-permute-start(f32[64,2048]{1,0:T(8,128)S(1)} %shard_map.61.refs_0_), channel_id=1, source_target_pairs={{0,1},{1,0},{2,3},{3,2},{4,5},{5,4},{6,7},{7,6},{8,9},{9,8},{10,11... | collective-permute-start | bytes 1572872 | tf_op jit(solution)/shard_map/ppermute | solution.py:75
  28.4 11.5 %collective-permute-start.10 = (f32[32,2048]{1,0:T(8,128)S(1)}, f32[32,2048]{1,0:T(8,128)S(1)}, u32[]{:S(2)}, u32[]{:S(2)}) collective-permute-start(f32[32,2048]{1,0:T(8,128)S(1)} %shard_map.65), channel_id=1, source_target_pairs={{0,8},{1,3},{2,10},{3,1},{4,12},{5,7},{6,14},{7,5},{8,0},{9,11},{1... | collective-permute-start | bytes 786440 | tf_op jit(solution)/shard_map/ppermute | solution.py:26
  34.3 6.7 %collective-permute-start.9 = (f32[32,2048]{1,0:T(8,128)S(1)}, f32[32,2048]{1,0:T(8,128)S(1)}, u32[]{:S(2)}, u32[]{:S(2)}) collective-permute-start(f32[32,2048]{1,0:T(8,128)S(1)} %shard_map.64), channel_id=1, source_target_pairs={{0,24},{1,7},{2,26},{3,5},{4,28},{5,3},{6,30},{7,1},{8,16},{9,15},... | collective-permute-start | bytes 786440 | tf_op jit(solution)/shard_map/ppermute | solution.py:26
  34.4 9.5 %collective-permute-start.8 = (f32[32,2048]{1,0:T(8,128)S(1)}, f32[32,2048]{1,0:T(8,128)S(1)}, u32[]{:S(2)}, u32[]{:S(2)}) collective-permute-start(f32[32,2048]{1,0:T(8,128)S(1)} %shard_map.63), channel_id=1, source_target_pairs={{0,24},{1,7},{2,26},{3,5},{4,28},{5,3},{6,30},{7,1},{8,16},{9,15},... | collective-permute-start | bytes 786440 | tf_op jit(solution)/shard_map/ppermute | solution.py:26
  37.1 9.6 %collective-permute-start.6 = (f32[32,2048]{1,0:T(8,128)S(1)}, f32[32,2048]{1,0:T(8,128)S(1)}, u32[]{:S(2)}, u32[]{:S(2)}) collective-permute-start(f32[32,2048]{1,0:T(8,128)S(1)} %shard_map.62), channel_id=1, source_target_pairs={{0,8},{1,3},{2,10},{3,1},{4,12},{5,7},{6,14},{7,5},{8,0},{9,11},{1... | collective-permute-start | bytes 786440 | tf_op jit(solution)/shard_map/ppermute | solution.py:26
  37.2 10.0 %collective-permute-start.19 = (f32[64,2048]{1,0:T(8,128)S(1)}, f32[64,2048]{1,0:T(8,128)S(1)}, u32[]{:S(2)}, u32[]{:S(2)}) collective-permute-start(f32[64,2048]{1,0:T(8,128)S(1)} %collective-permute-done.7.both.refs_2_), channel_id=1, source_target_pairs={{0,1},{1,0},{2,3},{3,2},{4,5},{5,4},{6,7},{7,6},{8,9},{9,8},{10,11... | collective-permute-start | bytes 1572872 | tf_op jit(solution)/shard_map/ppermute | solution.py:75
  39.8 7.4 %collective-permute-start.20 = (f32[64,2048]{1,0:T(8,128)S(1)}, f32[64,2048]{1,0:T(8,128)S(1)}, u32[]{:S(2)}, u32[]{:S(2)}) collective-permute-start(f32[64,2048]{1,0:T(8,128)S(1)} %collective-permute-done.5.both.refs_3_), channel_id=1, source_target_pairs={{0,1},{1,0},{2,3},{3,2},{4,5},{5,4},{6,7},{7,6},{8,9},{9,8},{10,11... | collective-permute-start | bytes 1572872 | tf_op jit(solution)/shard_map/ppermute | solution.py:75
  41.0 5.7 %collective-permute-start.16 = (f32[32,2048]{1,0:T(8,128)S(1)}, f32[32,2048]{1,0:T(8,128)S(1)}, u32[]{:S(2)}, u32[]{:S(2)}) collective-permute-start(f32[32,2048]{1,0:T(8,128)S(1)} %collective-permute-done.10.refs_5_), channel_id=1, source_target_pairs={{0,1},{1,0},{2,3},{3,2},{4,5},{5,4},{6,7},{7,6},{8,9},{9,8},{10,11... | collective-permute-start | bytes 786440 | tf_op jit(solution)/shard_map/ppermute | solution.py:75
  43.9 4.7 %collective-permute-start.12 = (f32[64,2048]{1,0:T(8,128)S(1)}, f32[64,2048]{1,0:T(8,128)S(1)}, u32[]{:S(2)}, u32[]{:S(2)}) collective-permute-start(f32[64,2048]{1,0:T(8,128)S(1)} %collective-permute-done.3.both.refs_1_), channel_id=1, source_target_pairs={{0,1},{1,0},{2,3},{3,2},{4,5},{5,4},{6,7},{7,6},{8,9},{9,8},{10,11... | collective-permute-start | bytes 1572872 | tf_op jit(solution)/shard_map/ppermute | solution.py:75
  47.3 2.8 %collective-permute-start.13 = (f32[32,2048]{1,0:T(8,128)S(1)}, f32[32,2048]{1,0:T(8,128)S(1)}, u32[]{:S(2)}, u32[]{:S(2)}) collective-permute-start(f32[32,2048]{1,0:T(8,128)S(1)} %collective-permute-done.6.refs_2_), channel_id=1, source_target_pairs={{0,1},{1,0},{2,3},{3,2},{4,5},{5,4},{6,7},{7,6},{8,9},{9,8},{10,11... | collective-permute-start | bytes 786440 | tf_op jit(solution)/shard_map/ppermute | solution.py:75
  54.3 3.1 %collective-permute-start.21 = (f32[16,1024]{1,0:T(8,128)S(1)}, f32[16,1024]{1,0:T(8,128)S(1)}, u32[]{:S(2)}, u32[]{:S(2)}) collective-permute-start(f32[16,1024]{1,0:T(8,128)S(1)} %shard_map.69), channel_id=1, source_target_pairs={{0,32},{32,0},{64,96},{96,64},{1,33},{33,1},{65,97},{97,65},{2,34}... | collective-permute-start | bytes 196616 | tf_op jit(solution)/shard_map/ppermute | solution.py:229
  57.4 5.1 %collective-permute-start.22 = (f32[16,1024]{1,0:T(8,128)S(1)}, f32[16,1024]{1,0:T(8,128)S(1)}, u32[]{:S(2)}, u32[]{:S(2)}) collective-permute-start(f32[16,1024]{1,0:T(8,128)S(1)} %shard_map.70), channel_id=1, source_target_pairs={{32,64},{64,32},{0,96},{96,0},{33,65},{65,33},{1,97},{97,1},{34,66... | collective-permute-start | bytes 196616 | tf_op jit(solution)/shard_map/ppermute | solution.py:229
  62.5 3.1 %collective-permute-start.23 = (f32[16,1024]{1,0:T(8,128)S(1)}, f32[16,1024]{1,0:T(8,128)S(1)}, u32[]{:S(2)}, u32[]{:S(2)}) collective-permute-start(f32[16,1024]{1,0:T(8,128)S(1)} %shard_map.71), channel_id=1, source_target_pairs={{64,96},{96,64},{0,32},{32,0},{65,97},{97,65},{1,33},{33,1},{66,98... | collective-permute-start | bytes 196616 | tf_op jit(solution)/shard_map/ppermute | solution.py:229
  65.7 3.5 %collective-permute-start.24 = (f32[16,1024]{1,0:T(8,128)S(1)}, f32[16,1024]{1,0:T(8,128)S(1)}, u32[]{:S(2)}, u32[]{:S(2)}) collective-permute-start(f32[16,1024]{1,0:T(8,128)S(1)} %get-tuple-element.35), channel_id=1, source_target_pairs={{96,64},{64,96},{0,32},{32,0},{97,65},{65,97},{1,33},{33,1},{98,66... | collective-permute-start | bytes 196616 | tf_op jit(solution)/shard_map/ppermute | solution.py:229
  69.1 6.4 %collective-permute-start.25 = (f32[16,1024]{1,0:T(8,128)S(1)}, f32[16,1024]{1,0:T(8,128)S(1)}, u32[]{:S(2)}, u32[]{:S(2)}) collective-permute-start(f32[16,1024]{1,0:T(8,128)S(1)} %shard_map.73), channel_id=1, source_target_pairs={{64,32},{32,64},{0,96},{96,0},{65,33},{33,65},{1,97},{97,1},{66,34... | collective-permute-start | bytes 196616 | tf_op jit(solution)/shard_map/ppermute | solution.py:229
  75.6 6.0 %collective-permute-start.26 = (f32[16,1024]{1,0:T(8,128)S(1)}, f32[16,1024]{1,0:T(8,128)S(1)}, u32[]{:S(2)}, u32[]{:S(2)}) collective-permute-start(f32[16,1024]{1,0:T(8,128)S(1)} %shard_map.74), channel_id=1, source_target_pairs={{32,0},{0,32},{64,96},{96,64},{33,1},{1,33},{65,97},{97,65},{34,2}... | collective-permute-start | bytes 196616 | tf_op jit(solution)/shard_map/ppermute | solution.py:229
  (3 other events, 7.8 us)

commit v4 on v2

--- a/solution.py
+++ b/solution.py
@@ -72,7 +72,10 @@
         from_partner(cut(b1, 1), 1, 0),
     ]
     pieces = [a, b, a0, a1, b0, b1, *far_pieces]
-    return pieces + [lax.ppermute(piece, "panel", SIBLINGS) for piece in pieces]
+    sibling = []
+    for piece in pieces:
+        sibling.append(lax.ppermute(piece, "panel", SIBLINGS))
+    return pieces + sibling
 
 
 def split(x):
@@ -165,7 +168,7 @@
             move(held, place_in * unit_rows, owner * unit_rows)
 
 
-EARLY = (0, 1, 2, 3, 10, 11, 12, 13)
+EARLY = (0, 1, 2, 3, 4, 5, 10, 11, 12, 13, 14, 15)
 LATE = tuple(number for number in range(2 * len(PIECES)) if number not in EARLY)
 
 

time: 96.2 us -> 99.7 us (1.036)
  starting transfers between devices: 34.9 us -> 44.8 us
  waiting for transfers between devices: 32.1 us -> 25.2 us
    ppermute x11, waiting for transfers between devices: 18.2 us -> 12.4 us  [from_partner(): return lax.ppermute(block, 'panel', pairs)]
    ppermute x10, starting transfers between devices: 14.6 us -> 20.4 us  [gathered(): sibling.append(lax.ppermute(piece, 'panel', SIBLINGS))]
    ppermute x11, starting transfers between devices: 13 us -> 17.1 us  [from_partner(): return lax.ppermute(block, 'panel', pairs)]
    ppermute x10, waiting for transfers between devices: 1.48 us -> 0.33 us  [gathered(): sibling.append(lax.ppermute(piece, 'panel', SIBLINGS))]
  transfers between devices with their start and end apart: 27 -> 27, of which waited for: 15 -> 13; matrix products, arithmetic and copies ran while one was open for 0% -> 0% of each run, Pallas kernels for 2% -> 3%
where the time goes in v4:
time: 99.7 us; the launch traced here: 99.5 us
  starting transfers between devices  44.8 us (45%)
  waiting for transfers between devices  25.2 us (25%)
  blocking collectives  18.9 us (19%)
  Pallas kernels  9.85 us (10%)
    ppermute x10, starting transfers between devices, gathered(): sibling.append(lax.ppermute(piece, 'panel', SIBLINGS))  20.4 us
    all_to_all x1, blocking collectives, per_device(): got = lax.all_to_all(send, 'panel', 0, 0, tiled=True).reshape(cols, LANES)  18.9 us
    ppermute x11, starting transfers between devices, from_partner(): return lax.ppermute(block, 'panel', pairs)  17.1 us
    ppermute x6, waiting for transfers between devices, hop(): return lax.ppermute(block, 'depth', route)  12.5 us
    ppermute x11, waiting for transfers between devices, from_partner(): return lax.ppermute(block, 'panel', pairs)  12.4 us
    pallas_call x17, Pallas kernels, call(): pl.pallas_call(kernel, out_shape=out_shape, in_specs=[space] * len(args),...  8.87 us
    ppermute x6, starting transfers between devices, hop(): return lax.ppermute(block, 'depth', route)  7.28 us
  transfers between devices with their start and end apart: 27, of which 13 were waited for; matrix products, arithmetic and copies ran while one was open for 0% of the time, Pallas kernels for 3%

profile of v4, /device:TPU:1, one launch (start us, length us, event | category | flops | bytes accessed | tf_op | source)
XLA Modules:
  0.0 99.5 jit_solution(1793051290337929761)
XLA Ops:
  1.6 2.2 %collective-permute-start = (f32[32,2048]{1,0:T(8,128)S(1)}, f32[32,2048]{1,0:T(8,128)S(1)}, u32[]{:S(2)}, u32[]{:S(2)}) collective-permute-start(f32[32,2048]{1,0:T(8,128)S(1)} %shard_map.59.first), channel_id=1, source_target_pairs={{0,2},{1,9},{2,0},{3,11},{4,6},{5,13},{6,4},{7,15},{8,10},{9,1},{1... | collective-permute-start | bytes 786440 | tf_op jit(solution)/shard_map/ppermute | solution.py:26
  3.8 4.1 %collective-permute-done.second = f32[32,2048]{1,0:T(8,128)S(1)} collective-permute-done((f32[32,2048]{1,0:T(8,128)S(1)}, f32[32,2048]{1,0:T(8,128)S(1)}, u32[]{:S(2)}, u32[]{:S(2)}) %collective-permute-start) | collective-permute-done | bytes 262176 | tf_op jit(solution)/shard_map/ppermute | solution.py:26
  7.9 1.9 %collective-permute-start.3 = (f32[64,2048]{1,0:T(8,128)S(1)}, f32[64,2048]{1,0:T(8,128)S(1)}, u32[]{:S(2)}, u32[]{:S(2)}) collective-permute-start(f32[64,2048]{1,0:T(8,128)S(1)} %shard_map.60.refs_0_), channel_id=1, source_target_pairs={{0,8},{1,3},{2,10},{3,1},{4,12},{5,7},{6,14},{7,5},{8,0},{9,11},{1... | collective-permute-start | bytes 1572872 | tf_op jit(solution)/shard_map/ppermute | solution.py:26
  9.8 2.9 %collective-permute-start.6 = (f32[32,2048]{1,0:T(8,128)S(1)}, f32[32,2048]{1,0:T(8,128)S(1)}, u32[]{:S(2)}, u32[]{:S(2)}) collective-permute-start(f32[32,2048]{1,0:T(8,128)S(1)} %shard_map.59.first), channel_id=1, source_target_pairs={{0,4},{1,17},{2,6},{3,19},{4,0},{5,21},{6,2},{7,23},{8,12},{9,25},... | collective-permute-start | bytes 786440 | tf_op jit(solution)/shard_map/ppermute | solution.py:26
  13.5 2.2 %collective-permute-start.1 = (f32[64,2048]{1,0:T(8,128)S(1)}, f32[64,2048]{1,0:T(8,128)S(1)}, u32[]{:S(2)}, u32[]{:S(2)}) collective-permute-start(f32[64,2048]{1,0:T(8,128)S(1)} %shard_map.60.refs_0_), channel_id=1, source_target_pairs={{0,24},{1,7},{2,26},{3,5},{4,28},{5,3},{6,30},{7,1},{8,16},{9,15},... | collective-permute-start | bytes 1572872 | tf_op jit(solution)/shard_map/ppermute | solution.py:26
  15.7 3.1 %collective-permute-done.6.second = f32[32,2048]{1,0:T(8,128)S(1)} collective-permute-done((f32[32,2048]{1,0:T(8,128)S(1)}, f32[32,2048]{1,0:T(8,128)S(1)}, u32[]{:S(2)}, u32[]{:S(2)}) %collective-permute-start.6) | collective-permute-done | bytes 262176 | tf_op jit(solution)/shard_map/ppermute | solution.py:26
  20.4 1.6 %collective-permute-start.9 = (f32[64,2048]{1,0:T(8,128)S(1)}, f32[64,2048]{1,0:T(8,128)S(1)}, u32[]{:S(2)}, u32[]{:S(2)}) collective-permute-start(f32[64,2048]{1,0:T(8,128)S(1)} %shard_map.63.refs_1_), channel_id=1, source_target_pairs={{0,24},{1,7},{2,26},{3,5},{4,28},{5,3},{6,30},{7,1},{8,16},{9,15},... | collective-permute-start | bytes 1572872 | tf_op jit(solution)/shard_map/ppermute | solution.py:26
  22.0 7.0 %collective-permute-start.15 = (f32[64,2048]{1,0:T(8,128)S(1)}, f32[64,2048]{1,0:T(8,128)S(1)}, u32[]{:S(2)}, u32[]{:S(2)}) collective-permute-start(f32[64,2048]{1,0:T(8,128)S(1)} %shard_map.60.refs_0_), channel_id=1, source_target_pairs={{0,1},{1,0},{2,3},{3,2},{4,5},{5,4},{6,7},{7,6},{8,9},{9,8},{10,11... | collective-permute-start | bytes 1572872 | tf_op jit(solution)/shard_map/ppermute | solution.py:77
  29.5 1.6 %collective-permute-start.4 = (f32[32,2048]{1,0:T(8,128)S(1)}, f32[32,2048]{1,0:T(8,128)S(1)}, u32[]{:S(2)}, u32[]{:S(2)}) collective-permute-start(f32[32,2048]{1,0:T(8,128)S(1)} %shard_map.62), channel_id=1, source_target_pairs={{0,24},{1,7},{2,26},{3,5},{4,28},{5,3},{6,30},{7,1},{8,16},{9,15},... | collective-permute-start | bytes 786440 | tf_op jit(solution)/shard_map/ppermute | solution.py:26
  31.1 2.6 %collective-permute-done.9.both.refs_5_ = f32[64,2048]{1,0:T(8,128)S(1)} collective-permute-done((f32[64,2048]{1,0:T(8,128)S(1)}, f32[64,2048]{1,0:T(8,128)S(1)}, u32[]{:S(2)}, u32[]{:S(2)}) %collective-permute-start.9) | collective-permute-done | bytes 524320 | tf_op jit(solution)/shard_map/ppermute | solution.py:26
  35.3 4.1 %collective-permute-start.17 = (f32[64,2048]{1,0:T(8,128)S(1)}, f32[64,2048]{1,0:T(8,128)S(1)}, u32[]{:S(2)}, u32[]{:S(2)}) collective-permute-start(f32[64,2048]{1,0:T(8,128)S(1)} %collective-permute-done.3.both.refs_2_), channel_id=1, source_target_pairs={{0,1},{1,0},{2,3},{3,2},{4,5},{5,4},{6,7},{7,6},{8,9},{9,8},{10,11... | collective-permute-start | bytes 1572872 | tf_op jit(solution)/shard_map/ppermute | solution.py:77
  40.1 2.0 %collective-permute-start.8 = (f32[32,2048]{1,0:T(8,128)S(1)}, f32[32,2048]{1,0:T(8,128)S(1)}, u32[]{:S(2)}, u32[]{:S(2)}) collective-permute-start(f32[32,2048]{1,0:T(8,128)S(1)} %shard_map.64), channel_id=1, source_target_pairs={{0,24},{1,7},{2,26},{3,5},{4,28},{5,3},{6,30},{7,1},{8,16},{9,15},... | collective-permute-start | bytes 786440 | tf_op jit(solution)/shard_map/ppermute | solution.py:26
  43.0 3.4 %collective-permute-start.19 = (f32[64,2048]{1,0:T(8,128)S(1)}, f32[64,2048]{1,0:T(8,128)S(1)}, u32[]{:S(2)}, u32[]{:S(2)}) collective-permute-start(f32[64,2048]{1,0:T(8,128)S(1)} %collective-permute-done.7.both.refs_4_), channel_id=1, source_target_pairs={{0,1},{1,0},{2,3},{3,2},{4,5},{5,4},{6,7},{7,6},{8,9},{9,8},{10,11... | collective-permute-start | bytes 1572872 | tf_op jit(solution)/shard_map/ppermute | solution.py:77
  46.6 4.6 %collective-permute-start.12 = (f32[32,2048]{1,0:T(8,128)S(1)}, f32[32,2048]{1,0:T(8,128)S(1)}, u32[]{:S(2)}, u32[]{:S(2)}) collective-permute-start(f32[32,2048]{1,0:T(8,128)S(1)} %collective-permute-done.4.refs_1_), channel_id=1, source_target_pairs={{0,1},{1,0},{2,3},{3,2},{4,5},{5,4},{6,7},{7,6},{8,9},{9,8},{10,11... | collective-permute-start | bytes 786440 | tf_op jit(solution)/shard_map/ppermute | solution.py:77
  53.5 1.6 %shard_map.67 = (bf16[1024,1024]{1,0:T(8,128)(2,1)S(1)}, bf16[1024,1024]{1,0:T(8,128)(2,1)S(1)}, bf16[1024,1024]{1,0:T(8,128)(2,1)S(1)}, bf16[1024,1024]{1,0:T(8...) custom-call(f32[32,2048]{1,0:T(8,128)S(1)} %collective-permute-done., ...), custom_call_target="tpu_custom_call", output_to_operand_aliasing={{0}: (8, {}), {1}: (9, {}), {2}: (10, {}), {3}: (11, {})} | custom-call | tf_op jit(solution)/shard_map/pallas_call | solution.py:309
  55.1 1.8 %shard_map.69 = f32[8,1024]{1,0:T(8,128)S(1)} custom-call(bf16[1024,1024]{1,0:T(8,128)(2,1)S(1)} %get-tuple-element.25.d_high, bf16[1024,1024]{1,0:T(8,128)(2,1)S(1)} %get-tuple-element.26.d_low, bf16[1024,1024]{1,0:T(8,128)(2,1)S(1)} %get-tuple-element.27.high.c_high, bf16[1024,1024]{1,0:T(8,128)(2,1)S(1)} %get-tuple-element.28.low.c_low, ...), custom_call_target="tpu_custom_call" | custom-call | tf_op jit(solution)/shard_map/pallas_call | solution.py:309
  56.9 2.8 %collective-permute-done.21.refs_0_ = f32[8,1024]{1,0:T(8,128)S(1)} collective-permute-done((f32[8,1024]{1,0:T(8,128)S(1)}, f32[8,1024]{1,0:T(8,128)S(1)}, u32[]{:S(2)}, u32[]{:S(2)}) %collective-permute-start.21) | collective-permute-done | bytes 32800 | tf_op jit(solution)/shard_map/ppermute | solution.py:223
  60.4 3.2 %collective-permute-done.22.refs_0_.refs_1_ = f32[8,1024]{1,0:T(8,128)S(1)} collective-permute-done((f32[8,1024]{1,0:T(8,128)S(1)}, f32[8,1024]{1,0:T(8,128)S(1)}, u32[]{:S(2)}, u32[]{:S(2)}) %collective-permute-start.22) | collective-permute-done | bytes 32800 | tf_op jit(solution)/shard_map/ppermute | solution.py:223
  64.2 2.2 %collective-permute-done.23.refs_2_ = f32[8,1024]{1,0:T(8,128)S(1)} collective-permute-done((f32[8,1024]{1,0:T(8,128)S(1)}, f32[8,1024]{1,0:T(8,128)S(1)}, u32[]{:S(2)}, u32[]{:S(2)}) %collective-permute-start.23) | collective-permute-done | bytes 32800 | tf_op jit(solution)/shard_map/ppermute | solution.py:223
  69.6 2.3 %collective-permute-start.25 = (f32[8,1024]{1,0:T(8,128)S(1)}, f32[8,1024]{1,0:T(8,128)S(1)}, u32[]{:S(2)}, u32[]{:S(2)}) collective-permute-start(f32[8,1024]{1,0:T(8,128)S(1)} %shard_map.73), channel_id=1, source_target_pairs={{64,32},{32,64},{0,96},{96,0},{65,33},{33,65},{1,97},{97,1},{66,34... | collective-permute-start | bytes 98312 | tf_op jit(solution)/shard_map/ppermute | solution.py:223
  71.9 1.7 %collective-permute-done.25.ahead.refs_1_ = f32[8,1024]{1,0:T(8,128)S(1)} collective-permute-done((f32[8,1024]{1,0:T(8,128)S(1)}, f32[8,1024]{1,0:T(8,128)S(1)}, u32[]{:S(2)}, u32[]{:S(2)}) %collective-permute-start.25) | collective-permute-done | bytes 32800 | tf_op jit(solution)/shard_map/ppermute | solution.py:223
  73.6 3.0 %collective-permute-start.26 = (f32[8,1024]{1,0:T(8,128)S(1)}, f32[8,1024]{1,0:T(8,128)S(1)}, u32[]{:S(2)}, u32[]{:S(2)}) collective-permute-start(f32[8,1024]{1,0:T(8,128)S(1)} %shard_map.74), channel_id=1, source_target_pairs={{32,0},{0,32},{64,96},{96,64},{33,1},{1,33},{65,97},{97,65},{34,2}... | collective-permute-start | bytes 98312 | tf_op jit(solution)/shard_map/ppermute | solution.py:223
  77.9 2.1 %shard_map.75 = f32[32,8,128]{2,1,0:T(8,128)S(1)} custom-call(bf16[1024,1024]{1,0:T(8,128)(2,1)S(1)} %get-tuple-element.25.d_high, bf16[1024,1024]{1,0:T(8,128)(2,1)S(1)} %get-tuple-element.26.d_low, bf16[1024,1024]{1,0:T(8,128)(2,1)S(1)} %get-tuple-element.29.c_high, bf16[1024,1024]{1,0:T(8,128)(2,1)S(1)} %get-tuple-element.30.c_low, ...), custom_call_target="tpu_custom_call" | custom-call | tf_op jit(solution)/shard_map/pallas_call | solution.py:309
  80.0 18.9 %all_to_all.5 = f32[32,8,128]{2,1,0:T(8,128)S(1)} all-to-all(f32[32,8,128]{2,1,0:T(8,128)S(1)} %shard_map.75), channel_id=1, replica_groups=mesh['depth'=4,'panel'=32] {'panel'}, dimensions={0} | all-to-all | bytes 262144 | tf_op jit(solution)/shard_map/all_to_all | solution.py:377
  (49 shorter events, 16.0 us)
Async XLA Ops:
  1.6 6.3 %collective-permute-start = (f32[32,2048]{1,0:T(8,128)S(1)}, f32[32,2048]{1,0:T(8,128)S(1)}, u32[]{:S(2)}, u32[]{:S(2)}) collective-permute-start(f32[32,2048]{1,0:T(8,128)S(1)} %shard_map.59.first), channel_id=1, source_target_pairs={{0,2},{1,9},{2,0},{3,11},{4,6},{5,13},{6,4},{7,15},{8,10},{9,1},{1... | collective-permute-start | bytes 786440 | tf_op jit(solution)/shard_map/ppermute | solution.py:26
  7.9 21.1 %collective-permute-start.3 = (f32[64,2048]{1,0:T(8,128)S(1)}, f32[64,2048]{1,0:T(8,128)S(1)}, u32[]{:S(2)}, u32[]{:S(2)}) collective-permute-start(f32[64,2048]{1,0:T(8,128)S(1)} %shard_map.60.refs_0_), channel_id=1, source_target_pairs={{0,8},{1,3},{2,10},{3,1},{4,12},{5,7},{6,14},{7,5},{8,0},{9,11},{1... | collective-permute-start | bytes 1572872 | tf_op jit(solution)/shard_map/ppermute | solution.py:26
  9.8 9.0 %collective-permute-start.6 = (f32[32,2048]{1,0:T(8,128)S(1)}, f32[32,2048]{1,0:T(8,128)S(1)}, u32[]{:S(2)}, u32[]{:S(2)}) collective-permute-start(f32[32,2048]{1,0:T(8,128)S(1)} %shard_map.59.first), channel_id=1, source_target_pairs={{0,4},{1,17},{2,6},{3,19},{4,0},{5,21},{6,2},{7,23},{8,12},{9,25},... | collective-permute-start | bytes 786440 | tf_op jit(solution)/shard_map/ppermute | solution.py:26
  12.7 7.6 %collective-permute-start.5 = (f32[32,2048]{1,0:T(8,128)S(1)}, f32[32,2048]{1,0:T(8,128)S(1)}, u32[]{:S(2)}, u32[]{:S(2)}) collective-permute-start(f32[32,2048]{1,0:T(8,128)S(1)} %shard_map.59.first), channel_id=1, source_target_pairs={{0,6},{1,25},{2,4},{3,27},{4,2},{5,29},{6,0},{7,31},{8,14},{9,17},... | collective-permute-start | bytes 786440 | tf_op jit(solution)/shard_map/ppermute | solution.py:26
  13.5 16.0 %collective-permute-start.1 = (f32[64,2048]{1,0:T(8,128)S(1)}, f32[64,2048]{1,0:T(8,128)S(1)}, u32[]{:S(2)}, u32[]{:S(2)}) collective-permute-start(f32[64,2048]{1,0:T(8,128)S(1)} %shard_map.60.refs_0_), channel_id=1, source_target_pairs={{0,24},{1,7},{2,26},{3,5},{4,28},{5,3},{6,30},{7,1},{8,16},{9,15},... | collective-permute-start | bytes 1572872 | tf_op jit(solution)/shard_map/ppermute | solution.py:26
  20.4 13.3 %collective-permute-start.9 = (f32[64,2048]{1,0:T(8,128)S(1)}, f32[64,2048]{1,0:T(8,128)S(1)}, u32[]{:S(2)}, u32[]{:S(2)}) collective-permute-start(f32[64,2048]{1,0:T(8,128)S(1)} %shard_map.63.refs_1_), channel_id=1, source_target_pairs={{0,24},{1,7},{2,26},{3,5},{4,28},{5,3},{6,30},{7,1},{8,16},{9,15},... | collective-permute-start | bytes 1572872 | tf_op jit(solution)/shard_map/ppermute | solution.py:26
  22.0 12.5 %collective-permute-start.15 = (f32[64,2048]{1,0:T(8,128)S(1)}, f32[64,2048]{1,0:T(8,128)S(1)}, u32[]{:S(2)}, u32[]{:S(2)}) collective-permute-start(f32[64,2048]{1,0:T(8,128)S(1)} %shard_map.60.refs_0_), channel_id=1, source_target_pairs={{0,1},{1,0},{2,3},{3,2},{4,5},{5,4},{6,7},{7,6},{8,9},{9,8},{10,11... | collective-permute-start | bytes 1572872 | tf_op jit(solution)/shard_map/ppermute | solution.py:77
  29.0 6.3 %collective-permute-start.16 = (f32[64,2048]{1,0:T(8,128)S(1)}, f32[64,2048]{1,0:T(8,128)S(1)}, u32[]{:S(2)}, u32[]{:S(2)}) collective-permute-start(f32[64,2048]{1,0:T(8,128)S(1)} %shard_map.63.refs_1_), channel_id=1, source_target_pairs={{0,1},{1,0},{2,3},{3,2},{4,5},{5,4},{6,7},{7,6},{8,9},{9,8},{10,11... | collective-permute-start | bytes 1572872 | tf_op jit(solution)/shard_map/ppermute | solution.py:77
  29.0 10.3 %collective-permute-start.7 = (f32[64,2048]{1,0:T(8,128)S(1)}, f32[64,2048]{1,0:T(8,128)S(1)}, u32[]{:S(2)}, u32[]{:S(2)}) collective-permute-start(f32[64,2048]{1,0:T(8,128)S(1)} %shard_map.63.refs_1_), channel_id=1, source_target_pairs={{0,8},{1,3},{2,10},{3,1},{4,12},{5,7},{6,14},{7,5},{8,0},{9,11},{1... | collective-permute-start | bytes 1572872 | tf_op jit(solution)/shard_map/ppermute | solution.py:26
  29.5 10.0 %collective-permute-start.4 = (f32[32,2048]{1,0:T(8,128)S(1)}, f32[32,2048]{1,0:T(8,128)S(1)}, u32[]{:S(2)}, u32[]{:S(2)}) collective-permute-start(f32[32,2048]{1,0:T(8,128)S(1)} %shard_map.62), channel_id=1, source_target_pairs={{0,24},{1,7},{2,26},{3,5},{4,28},{5,3},{6,30},{7,1},{8,16},{9,15},... | collective-permute-start | bytes 786440 | tf_op jit(solution)/shard_map/ppermute | solution.py:26
  33.7 6.4 %collective-permute-start.2 = (f32[32,2048]{1,0:T(8,128)S(1)}, f32[32,2048]{1,0:T(8,128)S(1)}, u32[]{:S(2)}, u32[]{:S(2)}) collective-permute-start(f32[32,2048]{1,0:T(8,128)S(1)} %shard_map.61), channel_id=1, source_target_pairs={{0,8},{1,3},{2,10},{3,1},{4,12},{5,7},{6,14},{7,5},{8,0},{9,11},{1... | collective-permute-start | bytes 786440 | tf_op jit(solution)/shard_map/ppermute | solution.py:26
  34.5 8.4 %collective-permute-start.10 = (f32[32,2048]{1,0:T(8,128)S(1)}, f32[32,2048]{1,0:T(8,128)S(1)}, u32[]{:S(2)}, u32[]{:S(2)}) collective-permute-start(f32[32,2048]{1,0:T(8,128)S(1)} %shard_map.65), channel_id=1, source_target_pairs={{0,8},{1,3},{2,10},{3,1},{4,12},{5,7},{6,14},{7,5},{8,0},{9,11},{1... | collective-permute-start | bytes 786440 | tf_op jit(solution)/shard_map/ppermute | solution.py:26
  35.3 15.9 %collective-permute-start.17 = (f32[64,2048]{1,0:T(8,128)S(1)}, f32[64,2048]{1,0:T(8,128)S(1)}, u32[]{:S(2)}, u32[]{:S(2)}) collective-permute-start(f32[64,2048]{1,0:T(8,128)S(1)} %collective-permute-done.3.both.refs_2_), channel_id=1, source_target_pairs={{0,1},{1,0},{2,3},{3,2},{4,5},{5,4},{6,7},{7,6},{8,9},{9,8},{10,11... | collective-permute-start | bytes 1572872 | tf_op jit(solution)/shard_map/ppermute | solution.py:77
  39.4 11.8 %collective-permute-start.18 = (f32[64,2048]{1,0:T(8,128)S(1)}, f32[64,2048]{1,0:T(8,128)S(1)}, u32[]{:S(2)}, u32[]{:S(2)}) collective-permute-start(f32[64,2048]{1,0:T(8,128)S(1)} %collective-permute-done.1.both.refs_3_), channel_id=1, source_target_pairs={{0,1},{1,0},{2,3},{3,2},{4,5},{5,4},{6,7},{7,6},{8,9},{9,8},{10,11... | collective-permute-start | bytes 1572872 | tf_op jit(solution)/shard_map/ppermute | solution.py:77
  39.5 12.2 %collective-permute-start.20 = (f32[64,2048]{1,0:T(8,128)S(1)}, f32[64,2048]{1,0:T(8,128)S(1)}, u32[]{:S(2)}, u32[]{:S(2)}) collective-permute-start(f32[64,2048]{1,0:T(8,128)S(1)} %collective-permute-done.9.both.refs_5_), channel_id=1, source_target_pairs={{0,1},{1,0},{2,3},{3,2},{4,5},{5,4},{6,7},{7,6},{8,9},{9,8},{10,11... | collective-permute-start | bytes 1572872 | tf_op jit(solution)/shard_map/ppermute | solution.py:77
  40.1 6.5 %collective-permute-start.8 = (f32[32,2048]{1,0:T(8,128)S(1)}, f32[32,2048]{1,0:T(8,128)S(1)}, u32[]{:S(2)}, u32[]{:S(2)}) collective-permute-start(f32[32,2048]{1,0:T(8,128)S(1)} %shard_map.64), channel_id=1, source_target_pairs={{0,24},{1,7},{2,26},{3,5},{4,28},{5,3},{6,30},{7,1},{8,16},{9,15},... | collective-permute-start | bytes 786440 | tf_op jit(solution)/shard_map/ppermute | solution.py:26
  43.0 8.8 %collective-permute-start.19 = (f32[64,2048]{1,0:T(8,128)S(1)}, f32[64,2048]{1,0:T(8,128)S(1)}, u32[]{:S(2)}, u32[]{:S(2)}) collective-permute-start(f32[64,2048]{1,0:T(8,128)S(1)} %collective-permute-done.7.both.refs_4_), channel_id=1, source_target_pairs={{0,1},{1,0},{2,3},{3,2},{4,5},{5,4},{6,7},{7,6},{8,9},{9,8},{10,11... | collective-permute-start | bytes 1572872 | tf_op jit(solution)/shard_map/ppermute | solution.py:77
  46.6 6.6 %collective-permute-start.12 = (f32[32,2048]{1,0:T(8,128)S(1)}, f32[32,2048]{1,0:T(8,128)S(1)}, u32[]{:S(2)}, u32[]{:S(2)}) collective-permute-start(f32[32,2048]{1,0:T(8,128)S(1)} %collective-permute-done.4.refs_1_), channel_id=1, source_target_pairs={{0,1},{1,0},{2,3},{3,2},{4,5},{5,4},{6,7},{7,6},{8,9},{9,8},{10,11... | collective-permute-start | bytes 786440 | tf_op jit(solution)/shard_map/ppermute | solution.py:77
  56.9 2.8 %collective-permute-start.21 = (f32[8,1024]{1,0:T(8,128)S(1)}, f32[8,1024]{1,0:T(8,128)S(1)}, u32[]{:S(2)}, u32[]{:S(2)}) collective-permute-start(f32[8,1024]{1,0:T(8,128)S(1)} %shard_map.69), channel_id=1, source_target_pairs={{0,32},{32,0},{64,96},{96,64},{1,33},{33,1},{65,97},{97,65},{2,34}... | collective-permute-start | bytes 98312 | tf_op jit(solution)/shard_map/ppermute | solution.py:223
  59.6 4.0 %collective-permute-start.22 = (f32[8,1024]{1,0:T(8,128)S(1)}, f32[8,1024]{1,0:T(8,128)S(1)}, u32[]{:S(2)}, u32[]{:S(2)}) collective-permute-start(f32[8,1024]{1,0:T(8,128)S(1)} %shard_map.70), channel_id=1, source_target_pairs={{32,64},{64,32},{0,96},{96,0},{33,65},{65,33},{1,97},{97,1},{34,66... | collective-permute-start | bytes 98312 | tf_op jit(solution)/shard_map/ppermute | solution.py:223
  63.6 2.8 %collective-permute-start.23 = (f32[8,1024]{1,0:T(8,128)S(1)}, f32[8,1024]{1,0:T(8,128)S(1)}, u32[]{:S(2)}, u32[]{:S(2)}) collective-permute-start(f32[8,1024]{1,0:T(8,128)S(1)} %shard_map.71), channel_id=1, source_target_pairs={{64,96},{96,64},{0,32},{32,0},{65,97},{97,65},{1,33},{33,1},{66,98... | collective-permute-start | bytes 98312 | tf_op jit(solution)/shard_map/ppermute | solution.py:223
  66.4 3.2 %collective-permute-start.24 = (f32[8,1024]{1,0:T(8,128)S(1)}, f32[8,1024]{1,0:T(8,128)S(1)}, u32[]{:S(2)}, u32[]{:S(2)}) collective-permute-start(f32[8,1024]{1,0:T(8,128)S(1)} %get-tuple-element.35), channel_id=1, source_target_pairs={{96,64},{64,96},{0,32},{32,0},{97,65},{65,97},{1,33},{33,1},{98,66... | collective-permute-start | bytes 98312 | tf_op jit(solution)/shard_map/ppermute | solution.py:223
  69.6 4.0 %collective-permute-start.25 = (f32[8,1024]{1,0:T(8,128)S(1)}, f32[8,1024]{1,0:T(8,128)S(1)}, u32[]{:S(2)}, u32[]{:S(2)}) collective-permute-start(f32[8,1024]{1,0:T(8,128)S(1)} %shard_map.73), channel_id=1, source_target_pairs={{64,32},{32,64},{0,96},{96,0},{65,33},{33,65},{1,97},{97,1},{66,34... | collective-permute-start | bytes 98312 | tf_op jit(solution)/shard_map/ppermute | solution.py:223
  73.6 4.3 %collective-permute-start.26 = (f32[8,1024]{1,0:T(8,128)S(1)}, f32[8,1024]{1,0:T(8,128)S(1)}, u32[]{:S(2)}, u32[]{:S(2)}) collective-permute-start(f32[8,1024]{1,0:T(8,128)S(1)} %shard_map.74), channel_id=1, source_target_pairs={{32,0},{0,32},{64,96},{96,64},{33,1},{1,33},{65,97},{97,65},{34,2}... | collective-permute-start | bytes 98312 | tf_op jit(solution)/shard_map/ppermute | solution.py:223
  (3 other events, 5.7 us)

commit v5 on v4

--- a/solution.py
+++ b/solution.py
@@ -180,7 +180,7 @@
 def late_kernel(*refs):
     count = len(LATE)
     side = refs[count + 4]
-    d_high, d_low, c_high, c_low, source, diag, wanted = refs[count + 5 :]
+    d_high, d_low, c_high, c_low, source, diag, wanted, flipped = refs[count + 5 :]
     size = d_high.shape[0]
     groups = size // LANES
     cols = side.shape[1] - LANES
@@ -194,17 +194,11 @@
             block = d_high[rows, where].astype(F32) + d_low[rows, where].astype(F32)
             d_high[where, rows], d_low[where, rows] = split(block.T)
 
-    pick = lax.broadcasted_iota(jnp.int32, (8, cols), 1) == (
-        lax.broadcasted_iota(jnp.int32, (8, cols), 0) + lax.axis_index("panel") * 8
-    )
-    own = lax.dot_general(
-        pick.astype(F32),
-        side[:, 0:cols],
-        (((1,), (1,)), ((), ())),
-        precision=lax.Precision.HIGHEST,
-        preferred_element_type=F32,
-    )
-    source[...] = own
+    first = lax.axis_index("panel") * 8
+    group = pl.ds(pl.multiple_of(lax.div(first, LANES) * LANES, LANES), LANES)
+    for start in range(0, size, LANES):
+        flipped[:, start : start + LANES] = side[start : start + LANES, group].T
+    source[...] = flipped[pl.ds(pl.multiple_of(lax.rem(first, LANES), 8), 8), :]
     eye = lax.broadcasted_iota(jnp.int32, (LANES, LANES), 0) == lax.broadcasted_iota(
         jnp.int32, (LANES, LANES), 1
     )
@@ -303,7 +297,7 @@
     return pltpu.VMEM(shape, dtype)
 
 
-def call(kernel, out_shape, *args, aliases=None, limit=8):
+def call(kernel, out_shape, *args, aliases=None, scratch=(), limit=8):
     args = [pltpu.with_memory_space_constraint(arg, pltpu.VMEM) for arg in args]
     space = pl.BlockSpec(memory_space=pltpu.VMEM)
     return pl.pallas_call(
@@ -312,6 +306,7 @@
         in_specs=[space] * len(args),
         out_specs=jax.tree.map(lambda _: space, out_shape),
         input_output_aliases=aliases or {},
+        scratch_shapes=scratch,
         compiler_params=pltpu.CompilerParams(vmem_limit_bytes=limit * 1024 * 1024),
     )(*args)
 
@@ -345,6 +340,7 @@
         *[pieces[number] for number in LATE],
         *filled,
         aliases={len(LATE) + number: number for number in range(4)},
+        scratch=[pltpu.VMEM((LANES, size), F32)],
     )
     mats = (d_high, d_low, c_high, c_low)
 

time: 99.7 us -> 99.2 us (level)
  no operation moved by 1% of the time
where the time goes in v5:
time: 99.2 us; the launch traced here: 99.1 us
  starting transfers between devices  44.8 us (45%)
  waiting for transfers between devices  25.2 us (25%)
  blocking collectives  18.9 us (19%)
  Pallas kernels  9.42 us (9%)
    ppermute x10, starting transfers between devices, gathered(): sibling.append(lax.ppermute(piece, 'panel', SIBLINGS))  20.4 us
    all_to_all x1, blocking collectives, per_device(): got = lax.all_to_all(send, 'panel', 0, 0, tiled=True).reshape(cols, LANES)  18.9 us
    ppermute x11, starting transfers between devices, from_partner(): return lax.ppermute(block, 'panel', pairs)  17.1 us
    ppermute x6, waiting for transfers between devices, hop(): return lax.ppermute(block, 'depth', route)  12.5 us
    ppermute x11, waiting for transfers between devices, from_partner(): return lax.ppermute(block, 'panel', pairs)  12.4 us
    pallas_call x17, Pallas kernels, call(): pl.pallas_call(kernel, out_shape=out_shape, in_specs=[space] * len(args),...  8.43 us
    ppermute x6, starting transfers between devices, hop(): return lax.ppermute(block, 'depth', route)  7.28 us
  transfers between devices with their start and end apart: 27, of which 13 were waited for; matrix products, arithmetic and copies ran while one was open for 0% of the time, Pallas kernels for 3%

profile of v5, /device:TPU:1, one launch (start us, length us, event | category | flops | bytes accessed | tf_op | source)
XLA Modules:
  0.0 99.1 jit_solution(5466010517346349313)
XLA Ops:
  1.6 2.2 %collective-permute-start = (f32[32,2048]{1,0:T(8,128)S(1)}, f32[32,2048]{1,0:T(8,128)S(1)}, u32[]{:S(2)}, u32[]{:S(2)}) collective-permute-start(f32[32,2048]{1,0:T(8,128)S(1)} %shard_map.59.first), channel_id=1, source_target_pairs={{0,2},{1,9},{2,0},{3,11},{4,6},{5,13},{6,4},{7,15},{8,10},{9,1},{1... | collective-permute-start | bytes 786440 | tf_op jit(solution)/shard_map/ppermute | solution.py:26
  3.8 4.1 %collective-permute-done.second = f32[32,2048]{1,0:T(8,128)S(1)} collective-permute-done((f32[32,2048]{1,0:T(8,128)S(1)}, f32[32,2048]{1,0:T(8,128)S(1)}, u32[]{:S(2)}, u32[]{:S(2)}) %collective-permute-start) | collective-permute-done | bytes 262176 | tf_op jit(solution)/shard_map/ppermute | solution.py:26
  7.9 1.9 %collective-permute-start.3 = (f32[64,2048]{1,0:T(8,128)S(1)}, f32[64,2048]{1,0:T(8,128)S(1)}, u32[]{:S(2)}, u32[]{:S(2)}) collective-permute-start(f32[64,2048]{1,0:T(8,128)S(1)} %shard_map.60.refs_0_), channel_id=1, source_target_pairs={{0,8},{1,3},{2,10},{3,1},{4,12},{5,7},{6,14},{7,5},{8,0},{9,11},{1... | collective-permute-start | bytes 1572872 | tf_op jit(solution)/shard_map/ppermute | solution.py:26
  9.8 2.9 %collective-permute-start.6 = (f32[32,2048]{1,0:T(8,128)S(1)}, f32[32,2048]{1,0:T(8,128)S(1)}, u32[]{:S(2)}, u32[]{:S(2)}) collective-permute-start(f32[32,2048]{1,0:T(8,128)S(1)} %shard_map.59.first), channel_id=1, source_target_pairs={{0,4},{1,17},{2,6},{3,19},{4,0},{5,21},{6,2},{7,23},{8,12},{9,25},... | collective-permute-start | bytes 786440 | tf_op jit(solution)/shard_map/ppermute | solution.py:26
  13.5 2.2 %collective-permute-start.1 = (f32[64,2048]{1,0:T(8,128)S(1)}, f32[64,2048]{1,0:T(8,128)S(1)}, u32[]{:S(2)}, u32[]{:S(2)}) collective-permute-start(f32[64,2048]{1,0:T(8,128)S(1)} %shard_map.60.refs_0_), channel_id=1, source_target_pairs={{0,24},{1,7},{2,26},{3,5},{4,28},{5,3},{6,30},{7,1},{8,16},{9,15},... | collective-permute-start | bytes 1572872 | tf_op jit(solution)/shard_map/ppermute | solution.py:26
  15.7 3.1 %collective-permute-done.6.second = f32[32,2048]{1,0:T(8,128)S(1)} collective-permute-done((f32[32,2048]{1,0:T(8,128)S(1)}, f32[32,2048]{1,0:T(8,128)S(1)}, u32[]{:S(2)}, u32[]{:S(2)}) %collective-permute-start.6) | collective-permute-done | bytes 262176 | tf_op jit(solution)/shard_map/ppermute | solution.py:26
  18.8 1.5 %collective-permute-done.5.first = f32[32,2048]{1,0:T(8,128)S(1)} collective-permute-done((f32[32,2048]{1,0:T(8,128)S(1)}, f32[32,2048]{1,0:T(8,128)S(1)}, u32[]{:S(2)}, u32[]{:S(2)}) %collective-permute-start.5) | collective-permute-done | bytes 262176 | tf_op jit(solution)/shard_map/ppermute | solution.py:26
  20.4 1.6 %collective-permute-start.9 = (f32[64,2048]{1,0:T(8,128)S(1)}, f32[64,2048]{1,0:T(8,128)S(1)}, u32[]{:S(2)}, u32[]{:S(2)}) collective-permute-start(f32[64,2048]{1,0:T(8,128)S(1)} %shard_map.63.refs_1_), channel_id=1, source_target_pairs={{0,24},{1,7},{2,26},{3,5},{4,28},{5,3},{6,30},{7,1},{8,16},{9,15},... | collective-permute-start | bytes 1572872 | tf_op jit(solution)/shard_map/ppermute | solution.py:26
  22.0 7.0 %collective-permute-start.15 = (f32[64,2048]{1,0:T(8,128)S(1)}, f32[64,2048]{1,0:T(8,128)S(1)}, u32[]{:S(2)}, u32[]{:S(2)}) collective-permute-start(f32[64,2048]{1,0:T(8,128)S(1)} %shard_map.60.refs_0_), channel_id=1, source_target_pairs={{0,1},{1,0},{2,3},{3,2},{4,5},{5,4},{6,7},{7,6},{8,9},{9,8},{10,11... | collective-permute-start | bytes 1572872 | tf_op jit(solution)/shard_map/ppermute | solution.py:77
  29.5 1.6 %collective-permute-start.4 = (f32[32,2048]{1,0:T(8,128)S(1)}, f32[32,2048]{1,0:T(8,128)S(1)}, u32[]{:S(2)}, u32[]{:S(2)}) collective-permute-start(f32[32,2048]{1,0:T(8,128)S(1)} %shard_map.62), channel_id=1, source_target_pairs={{0,24},{1,7},{2,26},{3,5},{4,28},{5,3},{6,30},{7,1},{8,16},{9,15},... | collective-permute-start | bytes 786440 | tf_op jit(solution)/shard_map/ppermute | solution.py:26
  31.1 2.6 %collective-permute-done.9.both.refs_5_ = f32[64,2048]{1,0:T(8,128)S(1)} collective-permute-done((f32[64,2048]{1,0:T(8,128)S(1)}, f32[64,2048]{1,0:T(8,128)S(1)}, u32[]{:S(2)}, u32[]{:S(2)}) %collective-permute-start.9) | collective-permute-done | bytes 524320 | tf_op jit(solution)/shard_map/ppermute | solution.py:26
  35.3 4.1 %collective-permute-start.17 = (f32[64,2048]{1,0:T(8,128)S(1)}, f32[64,2048]{1,0:T(8,128)S(1)}, u32[]{:S(2)}, u32[]{:S(2)}) collective-permute-start(f32[64,2048]{1,0:T(8,128)S(1)} %collective-permute-done.3.both.refs_2_), channel_id=1, source_target_pairs={{0,1},{1,0},{2,3},{3,2},{4,5},{5,4},{6,7},{7,6},{8,9},{9,8},{10,11... | collective-permute-start | bytes 1572872 | tf_op jit(solution)/shard_map/ppermute | solution.py:77
  40.1 2.0 %collective-permute-start.8 = (f32[32,2048]{1,0:T(8,128)S(1)}, f32[32,2048]{1,0:T(8,128)S(1)}, u32[]{:S(2)}, u32[]{:S(2)}) collective-permute-start(f32[32,2048]{1,0:T(8,128)S(1)} %shard_map.64), channel_id=1, source_target_pairs={{0,24},{1,7},{2,26},{3,5},{4,28},{5,3},{6,30},{7,1},{8,16},{9,15},... | collective-permute-start | bytes 786440 | tf_op jit(solution)/shard_map/ppermute | solution.py:26
  43.0 3.4 %collective-permute-start.19 = (f32[64,2048]{1,0:T(8,128)S(1)}, f32[64,2048]{1,0:T(8,128)S(1)}, u32[]{:S(2)}, u32[]{:S(2)}) collective-permute-start(f32[64,2048]{1,0:T(8,128)S(1)} %collective-permute-done.7.both.refs_4_), channel_id=1, source_target_pairs={{0,1},{1,0},{2,3},{3,2},{4,5},{5,4},{6,7},{7,6},{8,9},{9,8},{10,11... | collective-permute-start | bytes 1572872 | tf_op jit(solution)/shard_map/ppermute | solution.py:77
  46.6 4.6 %collective-permute-start.12 = (f32[32,2048]{1,0:T(8,128)S(1)}, f32[32,2048]{1,0:T(8,128)S(1)}, u32[]{:S(2)}, u32[]{:S(2)}) collective-permute-start(f32[32,2048]{1,0:T(8,128)S(1)} %collective-permute-done.4.refs_1_), channel_id=1, source_target_pairs={{0,1},{1,0},{2,3},{3,2},{4,5},{5,4},{6,7},{7,6},{8,9},{9,8},{10,11... | collective-permute-start | bytes 786440 | tf_op jit(solution)/shard_map/ppermute | solution.py:77
  54.6 1.8 %shard_map.69 = f32[8,1024]{1,0:T(8,128)S(1)} custom-call(bf16[1024,1024]{1,0:T(8,128)(2,1)S(1)} %get-tuple-element.25.d_high, bf16[1024,1024]{1,0:T(8,128)(2,1)S(1)} %get-tuple-element.26.d_low, bf16[1024,1024]{1,0:T(8,128)(2,1)S(1)} %get-tuple-element.27.high.c_high, bf16[1024,1024]{1,0:T(8,128)(2,1)S(1)} %get-tuple-element.28.low.c_low, ...), custom_call_target="tpu_custom_call" | custom-call | tf_op jit(solution)/shard_map/pallas_call | solution.py:303
  56.4 2.8 %collective-permute-done.21.refs_0_ = f32[8,1024]{1,0:T(8,128)S(1)} collective-permute-done((f32[8,1024]{1,0:T(8,128)S(1)}, f32[8,1024]{1,0:T(8,128)S(1)}, u32[]{:S(2)}, u32[]{:S(2)}) %collective-permute-start.21) | collective-permute-done | bytes 32800 | tf_op jit(solution)/shard_map/ppermute | solution.py:217
  60.0 3.2 %collective-permute-done.22.refs_0_.refs_1_ = f32[8,1024]{1,0:T(8,128)S(1)} collective-permute-done((f32[8,1024]{1,0:T(8,128)S(1)}, f32[8,1024]{1,0:T(8,128)S(1)}, u32[]{:S(2)}, u32[]{:S(2)}) %collective-permute-start.22) | collective-permute-done | bytes 32800 | tf_op jit(solution)/shard_map/ppermute | solution.py:217
  63.8 2.2 %collective-permute-done.23.refs_2_ = f32[8,1024]{1,0:T(8,128)S(1)} collective-permute-done((f32[8,1024]{1,0:T(8,128)S(1)}, f32[8,1024]{1,0:T(8,128)S(1)}, u32[]{:S(2)}, u32[]{:S(2)}) %collective-permute-start.23) | collective-permute-done | bytes 32800 | tf_op jit(solution)/shard_map/ppermute | solution.py:217
  69.2 2.3 %collective-permute-start.25 = (f32[8,1024]{1,0:T(8,128)S(1)}, f32[8,1024]{1,0:T(8,128)S(1)}, u32[]{:S(2)}, u32[]{:S(2)}) collective-permute-start(f32[8,1024]{1,0:T(8,128)S(1)} %shard_map.73), channel_id=1, source_target_pairs={{64,32},{32,64},{0,96},{96,0},{65,33},{33,65},{1,97},{97,1},{66,34... | collective-permute-start | bytes 98312 | tf_op jit(solution)/shard_map/ppermute | solution.py:217
  71.5 1.7 %collective-permute-done.25.ahead.refs_1_ = f32[8,1024]{1,0:T(8,128)S(1)} collective-permute-done((f32[8,1024]{1,0:T(8,128)S(1)}, f32[8,1024]{1,0:T(8,128)S(1)}, u32[]{:S(2)}, u32[]{:S(2)}) %collective-permute-start.25) | collective-permute-done | bytes 32800 | tf_op jit(solution)/shard_map/ppermute | solution.py:217
  73.2 3.0 %collective-permute-start.26 = (f32[8,1024]{1,0:T(8,128)S(1)}, f32[8,1024]{1,0:T(8,128)S(1)}, u32[]{:S(2)}, u32[]{:S(2)}) collective-permute-start(f32[8,1024]{1,0:T(8,128)S(1)} %shard_map.74), channel_id=1, source_target_pairs={{32,0},{0,32},{64,96},{96,64},{33,1},{1,33},{65,97},{97,65},{34,2}... | collective-permute-start | bytes 98312 | tf_op jit(solution)/shard_map/ppermute | solution.py:217
  77.4 2.1 %shard_map.75 = f32[32,8,128]{2,1,0:T(8,128)S(1)} custom-call(bf16[1024,1024]{1,0:T(8,128)(2,1)S(1)} %get-tuple-element.25.d_high, bf16[1024,1024]{1,0:T(8,128)(2,1)S(1)} %get-tuple-element.26.d_low, bf16[1024,1024]{1,0:T(8,128)(2,1)S(1)} %get-tuple-element.29.c_high, bf16[1024,1024]{1,0:T(8,128)(2,1)S(1)} %get-tuple-element.30.c_low, ...), custom_call_target="tpu_custom_call" | custom-call | tf_op jit(solution)/shard_map/pallas_call | solution.py:303
  79.5 18.9 %all_to_all.5 = f32[32,8,128]{2,1,0:T(8,128)S(1)} all-to-all(f32[32,8,128]{2,1,0:T(8,128)S(1)} %shard_map.75), channel_id=1, replica_groups=mesh['depth'=4,'panel'=32] {'panel'}, dimensions={0} | all-to-all | bytes 262144 | tf_op jit(solution)/shard_map/all_to_all | solution.py:373
  (49 shorter events, 15.6 us)
Async XLA Ops:
  1.6 6.3 %collective-permute-start = (f32[32,2048]{1,0:T(8,128)S(1)}, f32[32,2048]{1,0:T(8,128)S(1)}, u32[]{:S(2)}, u32[]{:S(2)}) collective-permute-start(f32[32,2048]{1,0:T(8,128)S(1)} %shard_map.59.first), channel_id=1, source_target_pairs={{0,2},{1,9},{2,0},{3,11},{4,6},{5,13},{6,4},{7,15},{8,10},{9,1},{1... | collective-permute-start | bytes 786440 | tf_op jit(solution)/shard_map/ppermute | solution.py:26
  7.9 21.1 %collective-permute-start.3 = (f32[64,2048]{1,0:T(8,128)S(1)}, f32[64,2048]{1,0:T(8,128)S(1)}, u32[]{:S(2)}, u32[]{:S(2)}) collective-permute-start(f32[64,2048]{1,0:T(8,128)S(1)} %shard_map.60.refs_0_), channel_id=1, source_target_pairs={{0,8},{1,3},{2,10},{3,1},{4,12},{5,7},{6,14},{7,5},{8,0},{9,11},{1... | collective-permute-start | bytes 1572872 | tf_op jit(solution)/shard_map/ppermute | solution.py:26
  9.8 9.0 %collective-permute-start.6 = (f32[32,2048]{1,0:T(8,128)S(1)}, f32[32,2048]{1,0:T(8,128)S(1)}, u32[]{:S(2)}, u32[]{:S(2)}) collective-permute-start(f32[32,2048]{1,0:T(8,128)S(1)} %shard_map.59.first), channel_id=1, source_target_pairs={{0,4},{1,17},{2,6},{3,19},{4,0},{5,21},{6,2},{7,23},{8,12},{9,25},... | collective-permute-start | bytes 786440 | tf_op jit(solution)/shard_map/ppermute | solution.py:26
  12.7 7.6 %collective-permute-start.5 = (f32[32,2048]{1,0:T(8,128)S(1)}, f32[32,2048]{1,0:T(8,128)S(1)}, u32[]{:S(2)}, u32[]{:S(2)}) collective-permute-start(f32[32,2048]{1,0:T(8,128)S(1)} %shard_map.59.first), channel_id=1, source_target_pairs={{0,6},{1,25},{2,4},{3,27},{4,2},{5,29},{6,0},{7,31},{8,14},{9,17},... | collective-permute-start | bytes 786440 | tf_op jit(solution)/shard_map/ppermute | solution.py:26
  13.5 16.0 %collective-permute-start.1 = (f32[64,2048]{1,0:T(8,128)S(1)}, f32[64,2048]{1,0:T(8,128)S(1)}, u32[]{:S(2)}, u32[]{:S(2)}) collective-permute-start(f32[64,2048]{1,0:T(8,128)S(1)} %shard_map.60.refs_0_), channel_id=1, source_target_pairs={{0,24},{1,7},{2,26},{3,5},{4,28},{5,3},{6,30},{7,1},{8,16},{9,15},... | collective-permute-start | bytes 1572872 | tf_op jit(solution)/shard_map/ppermute | solution.py:26
  20.4 13.3 %collective-permute-start.9 = (f32[64,2048]{1,0:T(8,128)S(1)}, f32[64,2048]{1,0:T(8,128)S(1)}, u32[]{:S(2)}, u32[]{:S(2)}) collective-permute-start(f32[64,2048]{1,0:T(8,128)S(1)} %shard_map.63.refs_1_), channel_id=1, source_target_pairs={{0,24},{1,7},{2,26},{3,5},{4,28},{5,3},{6,30},{7,1},{8,16},{9,15},... | collective-permute-start | bytes 1572872 | tf_op jit(solution)/shard_map/ppermute | solution.py:26
  22.0 12.5 %collective-permute-start.15 = (f32[64,2048]{1,0:T(8,128)S(1)}, f32[64,2048]{1,0:T(8,128)S(1)}, u32[]{:S(2)}, u32[]{:S(2)}) collective-permute-start(f32[64,2048]{1,0:T(8,128)S(1)} %shard_map.60.refs_0_), channel_id=1, source_target_pairs={{0,1},{1,0},{2,3},{3,2},{4,5},{5,4},{6,7},{7,6},{8,9},{9,8},{10,11... | collective-permute-start | bytes 1572872 | tf_op jit(solution)/shard_map/ppermute | solution.py:77
  29.0 6.3 %collective-permute-start.16 = (f32[64,2048]{1,0:T(8,128)S(1)}, f32[64,2048]{1,0:T(8,128)S(1)}, u32[]{:S(2)}, u32[]{:S(2)}) collective-permute-start(f32[64,2048]{1,0:T(8,128)S(1)} %shard_map.63.refs_1_), channel_id=1, source_target_pairs={{0,1},{1,0},{2,3},{3,2},{4,5},{5,4},{6,7},{7,6},{8,9},{9,8},{10,11... | collective-permute-start | bytes 1572872 | tf_op jit(solution)/shard_map/ppermute | solution.py:77
  29.0 10.3 %collective-permute-start.7 = (f32[64,2048]{1,0:T(8,128)S(1)}, f32[64,2048]{1,0:T(8,128)S(1)}, u32[]{:S(2)}, u32[]{:S(2)}) collective-permute-start(f32[64,2048]{1,0:T(8,128)S(1)} %shard_map.63.refs_1_), channel_id=1, source_target_pairs={{0,8},{1,3},{2,10},{3,1},{4,12},{5,7},{6,14},{7,5},{8,0},{9,11},{1... | collective-permute-start | bytes 1572872 | tf_op jit(solution)/shard_map/ppermute | solution.py:26
  29.5 10.0 %collective-permute-start.4 = (f32[32,2048]{1,0:T(8,128)S(1)}, f32[32,2048]{1,0:T(8,128)S(1)}, u32[]{:S(2)}, u32[]{:S(2)}) collective-permute-start(f32[32,2048]{1,0:T(8,128)S(1)} %shard_map.62), channel_id=1, source_target_pairs={{0,24},{1,7},{2,26},{3,5},{4,28},{5,3},{6,30},{7,1},{8,16},{9,15},... | collective-permute-start | bytes 786440 | tf_op jit(solution)/shard_map/ppermute | solution.py:26
  33.7 6.4 %collective-permute-start.2 = (f32[32,2048]{1,0:T(8,128)S(1)}, f32[32,2048]{1,0:T(8,128)S(1)}, u32[]{:S(2)}, u32[]{:S(2)}) collective-permute-start(f32[32,2048]{1,0:T(8,128)S(1)} %shard_map.61), channel_id=1, source_target_pairs={{0,8},{1,3},{2,10},{3,1},{4,12},{5,7},{6,14},{7,5},{8,0},{9,11},{1... | collective-permute-start | bytes 786440 | tf_op jit(solution)/shard_map/ppermute | solution.py:26
  34.5 8.4 %collective-permute-start.10 = (f32[32,2048]{1,0:T(8,128)S(1)}, f32[32,2048]{1,0:T(8,128)S(1)}, u32[]{:S(2)}, u32[]{:S(2)}) collective-permute-start(f32[32,2048]{1,0:T(8,128)S(1)} %shard_map.65), channel_id=1, source_target_pairs={{0,8},{1,3},{2,10},{3,1},{4,12},{5,7},{6,14},{7,5},{8,0},{9,11},{1... | collective-permute-start | bytes 786440 | tf_op jit(solution)/shard_map/ppermute | solution.py:26
  35.3 15.9 %collective-permute-start.17 = (f32[64,2048]{1,0:T(8,128)S(1)}, f32[64,2048]{1,0:T(8,128)S(1)}, u32[]{:S(2)}, u32[]{:S(2)}) collective-permute-start(f32[64,2048]{1,0:T(8,128)S(1)} %collective-permute-done.3.both.refs_2_), channel_id=1, source_target_pairs={{0,1},{1,0},{2,3},{3,2},{4,5},{5,4},{6,7},{7,6},{8,9},{9,8},{10,11... | collective-permute-start | bytes 1572872 | tf_op jit(solution)/shard_map/ppermute | solution.py:77
  39.4 11.8 %collective-permute-start.18 = (f32[64,2048]{1,0:T(8,128)S(1)}, f32[64,2048]{1,0:T(8,128)S(1)}, u32[]{:S(2)}, u32[]{:S(2)}) collective-permute-start(f32[64,2048]{1,0:T(8,128)S(1)} %collective-permute-done.1.both.refs_3_), channel_id=1, source_target_pairs={{0,1},{1,0},{2,3},{3,2},{4,5},{5,4},{6,7},{7,6},{8,9},{9,8},{10,11... | collective-permute-start | bytes 1572872 | tf_op jit(solution)/shard_map/ppermute | solution.py:77
  39.5 12.2 %collective-permute-start.20 = (f32[64,2048]{1,0:T(8,128)S(1)}, f32[64,2048]{1,0:T(8,128)S(1)}, u32[]{:S(2)}, u32[]{:S(2)}) collective-permute-start(f32[64,2048]{1,0:T(8,128)S(1)} %collective-permute-done.9.both.refs_5_), channel_id=1, source_target_pairs={{0,1},{1,0},{2,3},{3,2},{4,5},{5,4},{6,7},{7,6},{8,9},{9,8},{10,11... | collective-permute-start | bytes 1572872 | tf_op jit(solution)/shard_map/ppermute | solution.py:77
  40.1 6.5 %collective-permute-start.8 = (f32[32,2048]{1,0:T(8,128)S(1)}, f32[32,2048]{1,0:T(8,128)S(1)}, u32[]{:S(2)}, u32[]{:S(2)}) collective-permute-start(f32[32,2048]{1,0:T(8,128)S(1)} %shard_map.64), channel_id=1, source_target_pairs={{0,24},{1,7},{2,26},{3,5},{4,28},{5,3},{6,30},{7,1},{8,16},{9,15},... | collective-permute-start | bytes 786440 | tf_op jit(solution)/shard_map/ppermute | solution.py:26
  43.0 8.8 %collective-permute-start.19 = (f32[64,2048]{1,0:T(8,128)S(1)}, f32[64,2048]{1,0:T(8,128)S(1)}, u32[]{:S(2)}, u32[]{:S(2)}) collective-permute-start(f32[64,2048]{1,0:T(8,128)S(1)} %collective-permute-done.7.both.refs_4_), channel_id=1, source_target_pairs={{0,1},{1,0},{2,3},{3,2},{4,5},{5,4},{6,7},{7,6},{8,9},{9,8},{10,11... | collective-permute-start | bytes 1572872 | tf_op jit(solution)/shard_map/ppermute | solution.py:77
  46.6 6.6 %collective-permute-start.12 = (f32[32,2048]{1,0:T(8,128)S(1)}, f32[32,2048]{1,0:T(8,128)S(1)}, u32[]{:S(2)}, u32[]{:S(2)}) collective-permute-start(f32[32,2048]{1,0:T(8,128)S(1)} %collective-permute-done.4.refs_1_), channel_id=1, source_target_pairs={{0,1},{1,0},{2,3},{3,2},{4,5},{5,4},{6,7},{7,6},{8,9},{9,8},{10,11... | collective-permute-start | bytes 786440 | tf_op jit(solution)/shard_map/ppermute | solution.py:77
  56.4 2.8 %collective-permute-start.21 = (f32[8,1024]{1,0:T(8,128)S(1)}, f32[8,1024]{1,0:T(8,128)S(1)}, u32[]{:S(2)}, u32[]{:S(2)}) collective-permute-start(f32[8,1024]{1,0:T(8,128)S(1)} %shard_map.69), channel_id=1, source_target_pairs={{0,32},{32,0},{64,96},{96,64},{1,33},{33,1},{65,97},{97,65},{2,34}... | collective-permute-start | bytes 98312 | tf_op jit(solution)/shard_map/ppermute | solution.py:217
  59.2 4.0 %collective-permute-start.22 = (f32[8,1024]{1,0:T(8,128)S(1)}, f32[8,1024]{1,0:T(8,128)S(1)}, u32[]{:S(2)}, u32[]{:S(2)}) collective-permute-start(f32[8,1024]{1,0:T(8,128)S(1)} %shard_map.70), channel_id=1, source_target_pairs={{32,64},{64,32},{0,96},{96,0},{33,65},{65,33},{1,97},{97,1},{34,66... | collective-permute-start | bytes 98312 | tf_op jit(solution)/shard_map/ppermute | solution.py:217
  63.2 2.8 %collective-permute-start.23 = (f32[8,1024]{1,0:T(8,128)S(1)}, f32[8,1024]{1,0:T(8,128)S(1)}, u32[]{:S(2)}, u32[]{:S(2)}) collective-permute-start(f32[8,1024]{1,0:T(8,128)S(1)} %shard_map.71), channel_id=1, source_target_pairs={{64,96},{96,64},{0,32},{32,0},{65,97},{97,65},{1,33},{33,1},{66,98... | collective-permute-start | bytes 98312 | tf_op jit(solution)/shard_map/ppermute | solution.py:217
  66.0 3.2 %collective-permute-start.24 = (f32[8,1024]{1,0:T(8,128)S(1)}, f32[8,1024]{1,0:T(8,128)S(1)}, u32[]{:S(2)}, u32[]{:S(2)}) collective-permute-start(f32[8,1024]{1,0:T(8,128)S(1)} %get-tuple-element.35), channel_id=1, source_target_pairs={{96,64},{64,96},{0,32},{32,0},{97,65},{65,97},{1,33},{33,1},{98,66... | collective-permute-start | bytes 98312 | tf_op jit(solution)/shard_map/ppermute | solution.py:217
  69.2 4.0 %collective-permute-start.25 = (f32[8,1024]{1,0:T(8,128)S(1)}, f32[8,1024]{1,0:T(8,128)S(1)}, u32[]{:S(2)}, u32[]{:S(2)}) collective-permute-start(f32[8,1024]{1,0:T(8,128)S(1)} %shard_map.73), channel_id=1, source_target_pairs={{64,32},{32,64},{0,96},{96,0},{65,33},{33,65},{1,97},{97,1},{66,34... | collective-permute-start | bytes 98312 | tf_op jit(solution)/shard_map/ppermute | solution.py:217
  73.2 4.3 %collective-permute-start.26 = (f32[8,1024]{1,0:T(8,128)S(1)}, f32[8,1024]{1,0:T(8,128)S(1)}, u32[]{:S(2)}, u32[]{:S(2)}) collective-permute-start(f32[8,1024]{1,0:T(8,128)S(1)} %shard_map.74), channel_id=1, source_target_pairs={{32,0},{0,32},{64,96},{96,64},{33,1},{1,33},{65,97},{97,65},{34,2}... | collective-permute-start | bytes 98312 | tf_op jit(solution)/shard_map/ppermute | solution.py:217
  (3 other events, 5.7 us)

commit v6 on v5

--- a/solution.py
+++ b/solution.py
@@ -179,11 +179,9 @@
 
 def late_kernel(*refs):
     count = len(LATE)
-    side = refs[count + 4]
-    d_high, d_low, c_high, c_low, source, diag, wanted, flipped = refs[count + 5 :]
+    d_high, d_low, c_high, c_low, side, source, diag, flipped = refs[count + 5 :]
     size = d_high.shape[0]
     groups = size // LANES
-    cols = side.shape[1] - LANES
     move_pieces(LATE, refs[:count], d_high, d_low, c_high, c_low, side)
 
     for group in range(groups):
@@ -207,8 +205,6 @@
         tile = d_high[tiles, tiles].astype(F32) + d_low[tiles, tiles].astype(F32)
         line = jnp.sum(jnp.where(eye, tile, 0.0), axis=0, keepdims=True)
         diag[:, start : start + LANES] = jnp.broadcast_to(line, (8, LANES))
-    line = jnp.sum(side[:, cols : cols + LANES], axis=0, keepdims=True)
-    wanted[...] = jnp.broadcast_to(line, (8, LANES))
 
 
 def hop(block, here, there):
@@ -232,7 +228,11 @@
         refs[-1][...] = product(forward, c_high, c_low)
 
 
-def transpose_kernel(last, high, low, high_turned, low_turned):
+def transpose_kernel(last, high, low, side, high_turned, low_turned, chosen):
+    line = jnp.sum(side[:, side.shape[1] - LANES :], axis=0, keepdims=True).astype(jnp.int32)
+    row = lax.broadcasted_iota(jnp.int32, chosen.shape, 0)
+    chosen[...] = (row == line).astype(BF16)
+
     @pl.when(lax.axis_index("depth") != last)
     def _():
         for ref, turned in ((high, high_turned), (low, low_turned)):
@@ -258,7 +258,7 @@
         panel[...] = jacobi(rest, diag[...], d_high, d_low)
 
 
-def last_kernel(count, d_high, d_low, c_high, c_low, right_hand, diag, wanted, *refs):
+def last_kernel(count, d_high, d_low, c_high, c_low, right_hand, diag, chosen, *refs):
     ahead = taken(lax.axis_index("depth"), range(count - 1, -1, -1), refs[:count])
     coupled = jnp.where(lax.axis_index("depth") == count, 0.0, product(ahead, c_high, c_low))
     panel = jacobi(right_hand[...] - coupled, diag[...], d_high, d_low)
@@ -267,9 +267,7 @@
     rest = panel - high.astype(F32)
     middle = rest.astype(BF16)
     low = (rest - middle.astype(F32)).astype(BF16)
-    line = wanted[0:1, :].astype(jnp.int32)
-    chosen = (lax.broadcasted_iota(jnp.int32, (size, LANES), 0) == line).astype(BF16)
-    parts = [jnp.dot(part, chosen, preferred_element_type=F32) for part in (high, middle, low)]
+    parts = [jnp.dot(part, chosen[...], preferred_element_type=F32) for part in (high, middle, low)]
     picked = parts[0] + parts[1] + parts[2]
     send = refs[count]
     blocks = send.shape[0]
@@ -334,12 +332,12 @@
         (mat, mat, mat, mat, vmem((size, cols + LANES))),
         *[pieces[number] for number in EARLY],
     )
-    d_high, d_low, c_high, c_low, source, diag, wanted = call(
+    d_high, d_low, c_high, c_low, side, source, diag = call(
         late_kernel,
-        (mat, mat, mat, mat, vec, vec, vmem((8, LANES))),
+        (mat, mat, mat, mat, vmem((size, cols + LANES)), vec, vec),
         *[pieces[number] for number in LATE],
         *filled,
-        aliases={len(LATE) + number: number for number in range(4)},
+        aliases={len(LATE) + number: number for number in range(5)},
         scratch=[pltpu.VMEM((LANES, size), F32)],
     )
     mats = (d_high, d_low, c_high, c_low)
@@ -352,7 +350,11 @@
             vec, *mats, source, diag, *lefts[-1:],
         )
         lefts.append(hop(carried, k, k + 1))
-    turned = call(functools.partial(transpose_kernel, last), (mat, mat), c_high, c_low)
+    *turned, chosen = call(
+        functools.partial(transpose_kernel, last),
+        (mat, mat, vmem((size, LANES), BF16)),
+        c_high, c_low, side,
+    )
     right_hand, panel = call(
         functools.partial(turn_kernel, last),
         (vec, vec), d_high, d_low, source, diag, *lefts,
@@ -368,7 +370,7 @@
     send = call(
         functools.partial(last_kernel, last),
         vmem((size // rows, 8, LANES)),
-        d_high, d_low, *turned, right_hand, diag, wanted, *aheads,
+        d_high, d_low, *turned, right_hand, diag, chosen, *aheads,
     )
     got = lax.all_to_all(send, "panel", 0, 0, tiled=True).reshape(cols, LANES)
     panels, picked = call(

time: 99.2 us -> 99.2 us (level)
  no operation moved by 1% of the time
where the time goes in v6:
time: 99.2 us; the launch traced here: 99 us
  starting transfers between devices  44.8 us (45%)
  waiting for transfers between devices  25 us (25%)
  blocking collectives  18.9 us (19%)
  Pallas kernels  9.59 us (10%)
    ppermute x10, starting transfers between devices, gathered(): sibling.append(lax.ppermute(piece, 'panel', SIBLINGS))  20.4 us
    all_to_all x1, blocking collectives, per_device(): got = lax.all_to_all(send, 'panel', 0, 0, tiled=True).reshape(cols, LANES)  18.9 us
    ppermute x11, starting transfers between devices, from_partner(): return lax.ppermute(block, 'panel', pairs)  17.1 us
    ppermute x11, waiting for transfers between devices, from_partner(): return lax.ppermute(block, 'panel', pairs)  12.4 us
    ppermute x6, waiting for transfers between devices, hop(): return lax.ppermute(block, 'depth', route)  12.3 us
    pallas_call x17, Pallas kernels, call(): pl.pallas_call(kernel, out_shape=out_shape, in_specs=[space] * len(args),...  8.6 us
    ppermute x6, starting transfers between devices, hop(): return lax.ppermute(block, 'depth', route)  7.27 us
  transfers between devices with their start and end apart: 27, of which 13 were waited for; matrix products, arithmetic and copies ran while one was open for 0% of the time, Pallas kernels for 3%

profile of v6, /device:TPU:1, one launch (start us, length us, event | category | flops | bytes accessed | tf_op | source)
XLA Modules:
  0.0 99.0 jit_solution(11343521106987346442)
XLA Ops:
  1.6 2.2 %collective-permute-start = (f32[32,2048]{1,0:T(8,128)S(1)}, f32[32,2048]{1,0:T(8,128)S(1)}, u32[]{:S(2)}, u32[]{:S(2)}) collective-permute-start(f32[32,2048]{1,0:T(8,128)S(1)} %shard_map.59.first), channel_id=1, source_target_pairs={{0,2},{1,9},{2,0},{3,11},{4,6},{5,13},{6,4},{7,15},{8,10},{9,1},{1... | collective-permute-start | bytes 786440 | tf_op jit(solution)/shard_map/ppermute | solution.py:26
  3.8 4.1 %collective-permute-done.second = f32[32,2048]{1,0:T(8,128)S(1)} collective-permute-done((f32[32,2048]{1,0:T(8,128)S(1)}, f32[32,2048]{1,0:T(8,128)S(1)}, u32[]{:S(2)}, u32[]{:S(2)}) %collective-permute-start) | collective-permute-done | bytes 262176 | tf_op jit(solution)/shard_map/ppermute | solution.py:26
  7.9 1.9 %collective-permute-start.3 = (f32[64,2048]{1,0:T(8,128)S(1)}, f32[64,2048]{1,0:T(8,128)S(1)}, u32[]{:S(2)}, u32[]{:S(2)}) collective-permute-start(f32[64,2048]{1,0:T(8,128)S(1)} %shard_map.60.refs_0_), channel_id=1, source_target_pairs={{0,8},{1,3},{2,10},{3,1},{4,12},{5,7},{6,14},{7,5},{8,0},{9,11},{1... | collective-permute-start | bytes 1572872 | tf_op jit(solution)/shard_map/ppermute | solution.py:26
  9.8 2.9 %collective-permute-start.6 = (f32[32,2048]{1,0:T(8,128)S(1)}, f32[32,2048]{1,0:T(8,128)S(1)}, u32[]{:S(2)}, u32[]{:S(2)}) collective-permute-start(f32[32,2048]{1,0:T(8,128)S(1)} %shard_map.59.first), channel_id=1, source_target_pairs={{0,4},{1,17},{2,6},{3,19},{4,0},{5,21},{6,2},{7,23},{8,12},{9,25},... | collective-permute-start | bytes 786440 | tf_op jit(solution)/shard_map/ppermute | solution.py:26
  13.5 2.2 %collective-permute-start.1 = (f32[64,2048]{1,0:T(8,128)S(1)}, f32[64,2048]{1,0:T(8,128)S(1)}, u32[]{:S(2)}, u32[]{:S(2)}) collective-permute-start(f32[64,2048]{1,0:T(8,128)S(1)} %shard_map.60.refs_0_), channel_id=1, source_target_pairs={{0,24},{1,7},{2,26},{3,5},{4,28},{5,3},{6,30},{7,1},{8,16},{9,15},... | collective-permute-start | bytes 1572872 | tf_op jit(solution)/shard_map/ppermute | solution.py:26
  15.7 3.1 %collective-permute-done.6.second = f32[32,2048]{1,0:T(8,128)S(1)} collective-permute-done((f32[32,2048]{1,0:T(8,128)S(1)}, f32[32,2048]{1,0:T(8,128)S(1)}, u32[]{:S(2)}, u32[]{:S(2)}) %collective-permute-start.6) | collective-permute-done | bytes 262176 | tf_op jit(solution)/shard_map/ppermute | solution.py:26
  18.8 1.5 %collective-permute-done.5.first = f32[32,2048]{1,0:T(8,128)S(1)} collective-permute-done((f32[32,2048]{1,0:T(8,128)S(1)}, f32[32,2048]{1,0:T(8,128)S(1)}, u32[]{:S(2)}, u32[]{:S(2)}) %collective-permute-start.5) | collective-permute-done | bytes 262176 | tf_op jit(solution)/shard_map/ppermute | solution.py:26
  20.4 1.6 %collective-permute-start.9 = (f32[64,2048]{1,0:T(8,128)S(1)}, f32[64,2048]{1,0:T(8,128)S(1)}, u32[]{:S(2)}, u32[]{:S(2)}) collective-permute-start(f32[64,2048]{1,0:T(8,128)S(1)} %shard_map.63.refs_1_), channel_id=1, source_target_pairs={{0,24},{1,7},{2,26},{3,5},{4,28},{5,3},{6,30},{7,1},{8,16},{9,15},... | collective-permute-start | bytes 1572872 | tf_op jit(solution)/shard_map/ppermute | solution.py:26
  22.0 7.0 %collective-permute-start.15 = (f32[64,2048]{1,0:T(8,128)S(1)}, f32[64,2048]{1,0:T(8,128)S(1)}, u32[]{:S(2)}, u32[]{:S(2)}) collective-permute-start(f32[64,2048]{1,0:T(8,128)S(1)} %shard_map.60.refs_0_), channel_id=1, source_target_pairs={{0,1},{1,0},{2,3},{3,2},{4,5},{5,4},{6,7},{7,6},{8,9},{9,8},{10,11... | collective-permute-start | bytes 1572872 | tf_op jit(solution)/shard_map/ppermute | solution.py:77
  29.5 1.6 %collective-permute-start.4 = (f32[32,2048]{1,0:T(8,128)S(1)}, f32[32,2048]{1,0:T(8,128)S(1)}, u32[]{:S(2)}, u32[]{:S(2)}) collective-permute-start(f32[32,2048]{1,0:T(8,128)S(1)} %shard_map.62), channel_id=1, source_target_pairs={{0,24},{1,7},{2,26},{3,5},{4,28},{5,3},{6,30},{7,1},{8,16},{9,15},... | collective-permute-start | bytes 786440 | tf_op jit(solution)/shard_map/ppermute | solution.py:26
  31.1 2.6 %collective-permute-done.9.both.refs_5_ = f32[64,2048]{1,0:T(8,128)S(1)} collective-permute-done((f32[64,2048]{1,0:T(8,128)S(1)}, f32[64,2048]{1,0:T(8,128)S(1)}, u32[]{:S(2)}, u32[]{:S(2)}) %collective-permute-start.9) | collective-permute-done | bytes 524320 | tf_op jit(solution)/shard_map/ppermute | solution.py:26
  35.3 4.1 %collective-permute-start.17 = (f32[64,2048]{1,0:T(8,128)S(1)}, f32[64,2048]{1,0:T(8,128)S(1)}, u32[]{:S(2)}, u32[]{:S(2)}) collective-permute-start(f32[64,2048]{1,0:T(8,128)S(1)} %collective-permute-done.3.both.refs_2_), channel_id=1, source_target_pairs={{0,1},{1,0},{2,3},{3,2},{4,5},{5,4},{6,7},{7,6},{8,9},{9,8},{10,11... | collective-permute-start | bytes 1572872 | tf_op jit(solution)/shard_map/ppermute | solution.py:77
  40.1 2.0 %collective-permute-start.8 = (f32[32,2048]{1,0:T(8,128)S(1)}, f32[32,2048]{1,0:T(8,128)S(1)}, u32[]{:S(2)}, u32[]{:S(2)}) collective-permute-start(f32[32,2048]{1,0:T(8,128)S(1)} %shard_map.64), channel_id=1, source_target_pairs={{0,24},{1,7},{2,26},{3,5},{4,28},{5,3},{6,30},{7,1},{8,16},{9,15},... | collective-permute-start | bytes 786440 | tf_op jit(solution)/shard_map/ppermute | solution.py:26
  43.0 3.4 %collective-permute-start.19 = (f32[64,2048]{1,0:T(8,128)S(1)}, f32[64,2048]{1,0:T(8,128)S(1)}, u32[]{:S(2)}, u32[]{:S(2)}) collective-permute-start(f32[64,2048]{1,0:T(8,128)S(1)} %collective-permute-done.7.both.refs_4_), channel_id=1, source_target_pairs={{0,1},{1,0},{2,3},{3,2},{4,5},{5,4},{6,7},{7,6},{8,9},{9,8},{10,11... | collective-permute-start | bytes 1572872 | tf_op jit(solution)/shard_map/ppermute | solution.py:77
  46.6 4.6 %collective-permute-start.12 = (f32[32,2048]{1,0:T(8,128)S(1)}, f32[32,2048]{1,0:T(8,128)S(1)}, u32[]{:S(2)}, u32[]{:S(2)}) collective-permute-start(f32[32,2048]{1,0:T(8,128)S(1)} %collective-permute-done.4.refs_1_), channel_id=1, source_target_pairs={{0,1},{1,0},{2,3},{3,2},{4,5},{5,4},{6,7},{7,6},{8,9},{9,8},{10,11... | collective-permute-start | bytes 786440 | tf_op jit(solution)/shard_map/ppermute | solution.py:77
  54.6 1.8 %shard_map.69 = f32[8,1024]{1,0:T(8,128)S(1)} custom-call(bf16[1024,1024]{1,0:T(8,128)(2,1)S(1)} %get-tuple-element.26.d_high, bf16[1024,1024]{1,0:T(8,128)(2,1)S(1)} %get-tuple-element.27.d_low, bf16[1024,1024]{1,0:T(8,128)(2,1)S(1)} %get-tuple-element.28.high.c_high, bf16[1024,1024]{1,0:T(8,128)(2,1)S(1)} %get-tuple-element.29.low.c_low, ...), custom_call_target="tpu_custom_call" | custom-call | tf_op jit(solution)/shard_map/pallas_call | solution.py:301
  56.4 2.8 %collective-permute-done.21.refs_0_ = f32[8,1024]{1,0:T(8,128)S(1)} collective-permute-done((f32[8,1024]{1,0:T(8,128)S(1)}, f32[8,1024]{1,0:T(8,128)S(1)}, u32[]{:S(2)}, u32[]{:S(2)}) %collective-permute-start.21) | collective-permute-done | bytes 32800 | tf_op jit(solution)/shard_map/ppermute | solution.py:213
  59.9 3.2 %collective-permute-done.22.refs_0_.refs_1_ = f32[8,1024]{1,0:T(8,128)S(1)} collective-permute-done((f32[8,1024]{1,0:T(8,128)S(1)}, f32[8,1024]{1,0:T(8,128)S(1)}, u32[]{:S(2)}, u32[]{:S(2)}) %collective-permute-start.22) | collective-permute-done | bytes 32800 | tf_op jit(solution)/shard_map/ppermute | solution.py:213
  63.7 2.2 %collective-permute-done.23.refs_2_ = f32[8,1024]{1,0:T(8,128)S(1)} collective-permute-done((f32[8,1024]{1,0:T(8,128)S(1)}, f32[8,1024]{1,0:T(8,128)S(1)}, u32[]{:S(2)}, u32[]{:S(2)}) %collective-permute-start.23) | collective-permute-done | bytes 32800 | tf_op jit(solution)/shard_map/ppermute | solution.py:213
  69.2 2.3 %collective-permute-start.25 = (f32[8,1024]{1,0:T(8,128)S(1)}, f32[8,1024]{1,0:T(8,128)S(1)}, u32[]{:S(2)}, u32[]{:S(2)}) collective-permute-start(f32[8,1024]{1,0:T(8,128)S(1)} %shard_map.73), channel_id=1, source_target_pairs={{64,32},{32,64},{0,96},{96,0},{65,33},{33,65},{1,97},{97,1},{66,34... | collective-permute-start | bytes 98312 | tf_op jit(solution)/shard_map/ppermute | solution.py:213
  71.4 1.7 %collective-permute-done.25.ahead.refs_1_ = f32[8,1024]{1,0:T(8,128)S(1)} collective-permute-done((f32[8,1024]{1,0:T(8,128)S(1)}, f32[8,1024]{1,0:T(8,128)S(1)}, u32[]{:S(2)}, u32[]{:S(2)}) %collective-permute-start.25) | collective-permute-done | bytes 32800 | tf_op jit(solution)/shard_map/ppermute | solution.py:213
  73.1 3.0 %collective-permute-start.26 = (f32[8,1024]{1,0:T(8,128)S(1)}, f32[8,1024]{1,0:T(8,128)S(1)}, u32[]{:S(2)}, u32[]{:S(2)}) collective-permute-start(f32[8,1024]{1,0:T(8,128)S(1)} %shard_map.74), channel_id=1, source_target_pairs={{32,0},{0,32},{64,96},{96,64},{33,1},{1,33},{65,97},{97,65},{34,2}... | collective-permute-start | bytes 98312 | tf_op jit(solution)/shard_map/ppermute | solution.py:213
  77.4 2.1 %shard_map.75 = f32[32,8,128]{2,1,0:T(8,128)S(1)} custom-call(bf16[1024,1024]{1,0:T(8,128)(2,1)S(1)} %get-tuple-element.26.d_high, bf16[1024,1024]{1,0:T(8,128)(2,1)S(1)} %get-tuple-element.27.d_low, bf16[1024,1024]{1,0:T(8,128)(2,1)S(1)} %get-tuple-element.31.c_high, bf16[1024,1024]{1,0:T(8,128)(2,1)S(1)} %get-tuple-element.32.c_low, ...), custom_call_target="tpu_custom_call" | custom-call | tf_op jit(solution)/shard_map/pallas_call | solution.py:301
  79.5 18.9 %all_to_all.5 = f32[32,8,128]{2,1,0:T(8,128)S(1)} all-to-all(f32[32,8,128]{2,1,0:T(8,128)S(1)} %shard_map.75), channel_id=1, replica_groups=mesh['depth'=4,'panel'=32] {'panel'}, dimensions={0} | all-to-all | bytes 262144 | tf_op jit(solution)/shard_map/all_to_all | solution.py:375
  (49 shorter events, 15.6 us)
Async XLA Ops:
  1.6 6.3 %collective-permute-start = (f32[32,2048]{1,0:T(8,128)S(1)}, f32[32,2048]{1,0:T(8,128)S(1)}, u32[]{:S(2)}, u32[]{:S(2)}) collective-permute-start(f32[32,2048]{1,0:T(8,128)S(1)} %shard_map.59.first), channel_id=1, source_target_pairs={{0,2},{1,9},{2,0},{3,11},{4,6},{5,13},{6,4},{7,15},{8,10},{9,1},{1... | collective-permute-start | bytes 786440 | tf_op jit(solution)/shard_map/ppermute | solution.py:26
  7.9 21.1 %collective-permute-start.3 = (f32[64,2048]{1,0:T(8,128)S(1)}, f32[64,2048]{1,0:T(8,128)S(1)}, u32[]{:S(2)}, u32[]{:S(2)}) collective-permute-start(f32[64,2048]{1,0:T(8,128)S(1)} %shard_map.60.refs_0_), channel_id=1, source_target_pairs={{0,8},{1,3},{2,10},{3,1},{4,12},{5,7},{6,14},{7,5},{8,0},{9,11},{1... | collective-permute-start | bytes 1572872 | tf_op jit(solution)/shard_map/ppermute | solution.py:26
  9.8 9.0 %collective-permute-start.6 = (f32[32,2048]{1,0:T(8,128)S(1)}, f32[32,2048]{1,0:T(8,128)S(1)}, u32[]{:S(2)}, u32[]{:S(2)}) collective-permute-start(f32[32,2048]{1,0:T(8,128)S(1)} %shard_map.59.first), channel_id=1, source_target_pairs={{0,4},{1,17},{2,6},{3,19},{4,0},{5,21},{6,2},{7,23},{8,12},{9,25},... | collective-permute-start | bytes 786440 | tf_op jit(solution)/shard_map/ppermute | solution.py:26
  12.7 7.6 %collective-permute-start.5 = (f32[32,2048]{1,0:T(8,128)S(1)}, f32[32,2048]{1,0:T(8,128)S(1)}, u32[]{:S(2)}, u32[]{:S(2)}) collective-permute-start(f32[32,2048]{1,0:T(8,128)S(1)} %shard_map.59.first), channel_id=1, source_target_pairs={{0,6},{1,25},{2,4},{3,27},{4,2},{5,29},{6,0},{7,31},{8,14},{9,17},... | collective-permute-start | bytes 786440 | tf_op jit(solution)/shard_map/ppermute | solution.py:26
  13.5 16.0 %collective-permute-start.1 = (f32[64,2048]{1,0:T(8,128)S(1)}, f32[64,2048]{1,0:T(8,128)S(1)}, u32[]{:S(2)}, u32[]{:S(2)}) collective-permute-start(f32[64,2048]{1,0:T(8,128)S(1)} %shard_map.60.refs_0_), channel_id=1, source_target_pairs={{0,24},{1,7},{2,26},{3,5},{4,28},{5,3},{6,30},{7,1},{8,16},{9,15},... | collective-permute-start | bytes 1572872 | tf_op jit(solution)/shard_map/ppermute | solution.py:26
  20.4 13.3 %collective-permute-start.9 = (f32[64,2048]{1,0:T(8,128)S(1)}, f32[64,2048]{1,0:T(8,128)S(1)}, u32[]{:S(2)}, u32[]{:S(2)}) collective-permute-start(f32[64,2048]{1,0:T(8,128)S(1)} %shard_map.63.refs_1_), channel_id=1, source_target_pairs={{0,24},{1,7},{2,26},{3,5},{4,28},{5,3},{6,30},{7,1},{8,16},{9,15},... | collective-permute-start | bytes 1572872 | tf_op jit(solution)/shard_map/ppermute | solution.py:26
  22.0 12.5 %collective-permute-start.15 = (f32[64,2048]{1,0:T(8,128)S(1)}, f32[64,2048]{1,0:T(8,128)S(1)}, u32[]{:S(2)}, u32[]{:S(2)}) collective-permute-start(f32[64,2048]{1,0:T(8,128)S(1)} %shard_map.60.refs_0_), channel_id=1, source_target_pairs={{0,1},{1,0},{2,3},{3,2},{4,5},{5,4},{6,7},{7,6},{8,9},{9,8},{10,11... | collective-permute-start | bytes 1572872 | tf_op jit(solution)/shard_map/ppermute | solution.py:77
  29.0 6.3 %collective-permute-start.16 = (f32[64,2048]{1,0:T(8,128)S(1)}, f32[64,2048]{1,0:T(8,128)S(1)}, u32[]{:S(2)}, u32[]{:S(2)}) collective-permute-start(f32[64,2048]{1,0:T(8,128)S(1)} %shard_map.63.refs_1_), channel_id=1, source_target_pairs={{0,1},{1,0},{2,3},{3,2},{4,5},{5,4},{6,7},{7,6},{8,9},{9,8},{10,11... | collective-permute-start | bytes 1572872 | tf_op jit(solution)/shard_map/ppermute | solution.py:77
  29.0 10.3 %collective-permute-start.7 = (f32[64,2048]{1,0:T(8,128)S(1)}, f32[64,2048]{1,0:T(8,128)S(1)}, u32[]{:S(2)}, u32[]{:S(2)}) collective-permute-start(f32[64,2048]{1,0:T(8,128)S(1)} %shard_map.63.refs_1_), channel_id=1, source_target_pairs={{0,8},{1,3},{2,10},{3,1},{4,12},{5,7},{6,14},{7,5},{8,0},{9,11},{1... | collective-permute-start | bytes 1572872 | tf_op jit(solution)/shard_map/ppermute | solution.py:26
  29.5 10.0 %collective-permute-start.4 = (f32[32,2048]{1,0:T(8,128)S(1)}, f32[32,2048]{1,0:T(8,128)S(1)}, u32[]{:S(2)}, u32[]{:S(2)}) collective-permute-start(f32[32,2048]{1,0:T(8,128)S(1)} %shard_map.62), channel_id=1, source_target_pairs={{0,24},{1,7},{2,26},{3,5},{4,28},{5,3},{6,30},{7,1},{8,16},{9,15},... | collective-permute-start | bytes 786440 | tf_op jit(solution)/shard_map/ppermute | solution.py:26
  33.7 6.4 %collective-permute-start.2 = (f32[32,2048]{1,0:T(8,128)S(1)}, f32[32,2048]{1,0:T(8,128)S(1)}, u32[]{:S(2)}, u32[]{:S(2)}) collective-permute-start(f32[32,2048]{1,0:T(8,128)S(1)} %shard_map.61), channel_id=1, source_target_pairs={{0,8},{1,3},{2,10},{3,1},{4,12},{5,7},{6,14},{7,5},{8,0},{9,11},{1... | collective-permute-start | bytes 786440 | tf_op jit(solution)/shard_map/ppermute | solution.py:26
  34.5 8.4 %collective-permute-start.10 = (f32[32,2048]{1,0:T(8,128)S(1)}, f32[32,2048]{1,0:T(8,128)S(1)}, u32[]{:S(2)}, u32[]{:S(2)}) collective-permute-start(f32[32,2048]{1,0:T(8,128)S(1)} %shard_map.65), channel_id=1, source_target_pairs={{0,8},{1,3},{2,10},{3,1},{4,12},{5,7},{6,14},{7,5},{8,0},{9,11},{1... | collective-permute-start | bytes 786440 | tf_op jit(solution)/shard_map/ppermute | solution.py:26
  35.3 15.9 %collective-permute-start.17 = (f32[64,2048]{1,0:T(8,128)S(1)}, f32[64,2048]{1,0:T(8,128)S(1)}, u32[]{:S(2)}, u32[]{:S(2)}) collective-permute-start(f32[64,2048]{1,0:T(8,128)S(1)} %collective-permute-done.3.both.refs_2_), channel_id=1, source_target_pairs={{0,1},{1,0},{2,3},{3,2},{4,5},{5,4},{6,7},{7,6},{8,9},{9,8},{10,11... | collective-permute-start | bytes 1572872 | tf_op jit(solution)/shard_map/ppermute | solution.py:77
  39.4 11.8 %collective-permute-start.18 = (f32[64,2048]{1,0:T(8,128)S(1)}, f32[64,2048]{1,0:T(8,128)S(1)}, u32[]{:S(2)}, u32[]{:S(2)}) collective-permute-start(f32[64,2048]{1,0:T(8,128)S(1)} %collective-permute-done.1.both.refs_3_), channel_id=1, source_target_pairs={{0,1},{1,0},{2,3},{3,2},{4,5},{5,4},{6,7},{7,6},{8,9},{9,8},{10,11... | collective-permute-start | bytes 1572872 | tf_op jit(solution)/shard_map/ppermute | solution.py:77
  39.5 12.2 %collective-permute-start.20 = (f32[64,2048]{1,0:T(8,128)S(1)}, f32[64,2048]{1,0:T(8,128)S(1)}, u32[]{:S(2)}, u32[]{:S(2)}) collective-permute-start(f32[64,2048]{1,0:T(8,128)S(1)} %collective-permute-done.9.both.refs_5_), channel_id=1, source_target_pairs={{0,1},{1,0},{2,3},{3,2},{4,5},{5,4},{6,7},{7,6},{8,9},{9,8},{10,11... | collective-permute-start | bytes 1572872 | tf_op jit(solution)/shard_map/ppermute | solution.py:77
  40.1 6.5 %collective-permute-start.8 = (f32[32,2048]{1,0:T(8,128)S(1)}, f32[32,2048]{1,0:T(8,128)S(1)}, u32[]{:S(2)}, u32[]{:S(2)}) collective-permute-start(f32[32,2048]{1,0:T(8,128)S(1)} %shard_map.64), channel_id=1, source_target_pairs={{0,24},{1,7},{2,26},{3,5},{4,28},{5,3},{6,30},{7,1},{8,16},{9,15},... | collective-permute-start | bytes 786440 | tf_op jit(solution)/shard_map/ppermute | solution.py:26
  43.0 8.8 %collective-permute-start.19 = (f32[64,2048]{1,0:T(8,128)S(1)}, f32[64,2048]{1,0:T(8,128)S(1)}, u32[]{:S(2)}, u32[]{:S(2)}) collective-permute-start(f32[64,2048]{1,0:T(8,128)S(1)} %collective-permute-done.7.both.refs_4_), channel_id=1, source_target_pairs={{0,1},{1,0},{2,3},{3,2},{4,5},{5,4},{6,7},{7,6},{8,9},{9,8},{10,11... | collective-permute-start | bytes 1572872 | tf_op jit(solution)/shard_map/ppermute | solution.py:77
  46.6 6.6 %collective-permute-start.12 = (f32[32,2048]{1,0:T(8,128)S(1)}, f32[32,2048]{1,0:T(8,128)S(1)}, u32[]{:S(2)}, u32[]{:S(2)}) collective-permute-start(f32[32,2048]{1,0:T(8,128)S(1)} %collective-permute-done.4.refs_1_), channel_id=1, source_target_pairs={{0,1},{1,0},{2,3},{3,2},{4,5},{5,4},{6,7},{7,6},{8,9},{9,8},{10,11... | collective-permute-start | bytes 786440 | tf_op jit(solution)/shard_map/ppermute | solution.py:77
  56.4 2.8 %collective-permute-start.21 = (f32[8,1024]{1,0:T(8,128)S(1)}, f32[8,1024]{1,0:T(8,128)S(1)}, u32[]{:S(2)}, u32[]{:S(2)}) collective-permute-start(f32[8,1024]{1,0:T(8,128)S(1)} %shard_map.69), channel_id=1, source_target_pairs={{0,32},{32,0},{64,96},{96,64},{1,33},{33,1},{65,97},{97,65},{2,34}... | collective-permute-start | bytes 98312 | tf_op jit(solution)/shard_map/ppermute | solution.py:213
  59.2 4.0 %collective-permute-start.22 = (f32[8,1024]{1,0:T(8,128)S(1)}, f32[8,1024]{1,0:T(8,128)S(1)}, u32[]{:S(2)}, u32[]{:S(2)}) collective-permute-start(f32[8,1024]{1,0:T(8,128)S(1)} %shard_map.70), channel_id=1, source_target_pairs={{32,64},{64,32},{0,96},{96,0},{33,65},{65,33},{1,97},{97,1},{34,66... | collective-permute-start | bytes 98312 | tf_op jit(solution)/shard_map/ppermute | solution.py:213
  63.1 2.8 %collective-permute-start.23 = (f32[8,1024]{1,0:T(8,128)S(1)}, f32[8,1024]{1,0:T(8,128)S(1)}, u32[]{:S(2)}, u32[]{:S(2)}) collective-permute-start(f32[8,1024]{1,0:T(8,128)S(1)} %shard_map.71), channel_id=1, source_target_pairs={{64,96},{96,64},{0,32},{32,0},{65,97},{97,65},{1,33},{33,1},{66,98... | collective-permute-start | bytes 98312 | tf_op jit(solution)/shard_map/ppermute | solution.py:213
  65.9 3.2 %collective-permute-start.24 = (f32[8,1024]{1,0:T(8,128)S(1)}, f32[8,1024]{1,0:T(8,128)S(1)}, u32[]{:S(2)}, u32[]{:S(2)}) collective-permute-start(f32[8,1024]{1,0:T(8,128)S(1)} %get-tuple-element.37), channel_id=1, source_target_pairs={{96,64},{64,96},{0,32},{32,0},{97,65},{65,97},{1,33},{33,1},{98,66... | collective-permute-start | bytes 98312 | tf_op jit(solution)/shard_map/ppermute | solution.py:213
  69.2 4.0 %collective-permute-start.25 = (f32[8,1024]{1,0:T(8,128)S(1)}, f32[8,1024]{1,0:T(8,128)S(1)}, u32[]{:S(2)}, u32[]{:S(2)}) collective-permute-start(f32[8,1024]{1,0:T(8,128)S(1)} %shard_map.73), channel_id=1, source_target_pairs={{64,32},{32,64},{0,96},{96,0},{65,33},{33,65},{1,97},{97,1},{66,34... | collective-permute-start | bytes 98312 | tf_op jit(solution)/shard_map/ppermute | solution.py:213
  73.1 4.3 %collective-permute-start.26 = (f32[8,1024]{1,0:T(8,128)S(1)}, f32[8,1024]{1,0:T(8,128)S(1)}, u32[]{:S(2)}, u32[]{:S(2)}) collective-permute-start(f32[8,1024]{1,0:T(8,128)S(1)} %shard_map.74), channel_id=1, source_target_pairs={{32,0},{0,32},{64,96},{96,64},{33,1},{1,33},{65,97},{97,65},{34,2}... | collective-permute-start | bytes 98312 | tf_op jit(solution)/shard_map/ppermute | solution.py:213
  (3 other events, 5.7 us)

commit v7 on v5

--- a/solution.py
+++ b/solution.py
@@ -179,8 +179,7 @@
 
 def late_kernel(*refs):
     count = len(LATE)
-    side = refs[count + 4]
-    d_high, d_low, c_high, c_low, source, diag, wanted, flipped = refs[count + 5 :]
+    d_high, d_low, c_high, c_low, side, source, diag, wanted, flipped = refs[count + 5 :]
     size = d_high.shape[0]
     groups = size // LANES
     cols = side.shape[1] - LANES
@@ -334,12 +333,12 @@
         (mat, mat, mat, mat, vmem((size, cols + LANES))),
         *[pieces[number] for number in EARLY],
     )
-    d_high, d_low, c_high, c_low, source, diag, wanted = call(
+    d_high, d_low, c_high, c_low, _, source, diag, wanted = call(
         late_kernel,
-        (mat, mat, mat, mat, vec, vec, vmem((8, LANES))),
+        (mat, mat, mat, mat, vmem((size, cols + LANES)), vec, vec, vmem((8, LANES))),
         *[pieces[number] for number in LATE],
         *filled,
-        aliases={len(LATE) + number: number for number in range(4)},
+        aliases={len(LATE) + number: number for number in range(5)},
         scratch=[pltpu.VMEM((LANES, size), F32)],
     )
     mats = (d_high, d_low, c_high, c_low)

time: 99.2 us -> 99.2 us (level)
  no operation moved by 1% of the time
where the time goes in v7:
time: 99.2 us; the launch traced here: 99.1 us
  starting transfers between devices  44.8 us (45%)
  waiting for transfers between devices  25.2 us (25%)
  blocking collectives  18.9 us (19%)
  Pallas kernels  9.42 us (9%)
    ppermute x10, starting transfers between devices, gathered(): sibling.append(lax.ppermute(piece, 'panel', SIBLINGS))  20.4 us
    all_to_all x1, blocking collectives, per_device(): got = lax.all_to_all(send, 'panel', 0, 0, tiled=True).reshape(cols, LANES)  18.9 us
    ppermute x11, starting transfers between devices, from_partner(): return lax.ppermute(block, 'panel', pairs)  17.1 us
    ppermute x6, waiting for transfers between devices, hop(): return lax.ppermute(block, 'depth', route)  12.5 us
    ppermute x11, waiting for transfers between devices, from_partner(): return lax.ppermute(block, 'panel', pairs)  12.4 us
    pallas_call x17, Pallas kernels, call(): pl.pallas_call(kernel, out_shape=out_shape, in_specs=[space] * len(args),...  8.43 us
    ppermute x6, starting transfers between devices, hop(): return lax.ppermute(block, 'depth', route)  7.28 us
  transfers between devices with their start and end apart: 27, of which 13 were waited for; matrix products, arithmetic and copies ran while one was open for 0% of the time, Pallas kernels for 3%

profile of v7, /device:TPU:1, one launch (start us, length us, event | category | flops | bytes accessed | tf_op | source)
XLA Modules:
  0.0 99.1 jit_solution(17723079953620288718)
XLA Ops:
  1.6 2.2 %collective-permute-start = (f32[32,2048]{1,0:T(8,128)S(1)}, f32[32,2048]{1,0:T(8,128)S(1)}, u32[]{:S(2)}, u32[]{:S(2)}) collective-permute-start(f32[32,2048]{1,0:T(8,128)S(1)} %shard_map.59.first), channel_id=1, source_target_pairs={{0,2},{1,9},{2,0},{3,11},{4,6},{5,13},{6,4},{7,15},{8,10},{9,1},{1... | collective-permute-start | bytes 786440 | tf_op jit(solution)/shard_map/ppermute | solution.py:26
  3.8 4.1 %collective-permute-done.second = f32[32,2048]{1,0:T(8,128)S(1)} collective-permute-done((f32[32,2048]{1,0:T(8,128)S(1)}, f32[32,2048]{1,0:T(8,128)S(1)}, u32[]{:S(2)}, u32[]{:S(2)}) %collective-permute-start) | collective-permute-done | bytes 262176 | tf_op jit(solution)/shard_map/ppermute | solution.py:26
  7.9 1.9 %collective-permute-start.3 = (f32[64,2048]{1,0:T(8,128)S(1)}, f32[64,2048]{1,0:T(8,128)S(1)}, u32[]{:S(2)}, u32[]{:S(2)}) collective-permute-start(f32[64,2048]{1,0:T(8,128)S(1)} %shard_map.60.refs_0_), channel_id=1, source_target_pairs={{0,8},{1,3},{2,10},{3,1},{4,12},{5,7},{6,14},{7,5},{8,0},{9,11},{1... | collective-permute-start | bytes 1572872 | tf_op jit(solution)/shard_map/ppermute | solution.py:26
  9.8 2.9 %collective-permute-start.6 = (f32[32,2048]{1,0:T(8,128)S(1)}, f32[32,2048]{1,0:T(8,128)S(1)}, u32[]{:S(2)}, u32[]{:S(2)}) collective-permute-start(f32[32,2048]{1,0:T(8,128)S(1)} %shard_map.59.first), channel_id=1, source_target_pairs={{0,4},{1,17},{2,6},{3,19},{4,0},{5,21},{6,2},{7,23},{8,12},{9,25},... | collective-permute-start | bytes 786440 | tf_op jit(solution)/shard_map/ppermute | solution.py:26
  13.5 2.2 %collective-permute-start.1 = (f32[64,2048]{1,0:T(8,128)S(1)}, f32[64,2048]{1,0:T(8,128)S(1)}, u32[]{:S(2)}, u32[]{:S(2)}) collective-permute-start(f32[64,2048]{1,0:T(8,128)S(1)} %shard_map.60.refs_0_), channel_id=1, source_target_pairs={{0,24},{1,7},{2,26},{3,5},{4,28},{5,3},{6,30},{7,1},{8,16},{9,15},... | collective-permute-start | bytes 1572872 | tf_op jit(solution)/shard_map/ppermute | solution.py:26
  15.7 3.1 %collective-permute-done.6.second = f32[32,2048]{1,0:T(8,128)S(1)} collective-permute-done((f32[32,2048]{1,0:T(8,128)S(1)}, f32[32,2048]{1,0:T(8,128)S(1)}, u32[]{:S(2)}, u32[]{:S(2)}) %collective-permute-start.6) | collective-permute-done | bytes 262176 | tf_op jit(solution)/shard_map/ppermute | solution.py:26
  18.8 1.5 %collective-permute-done.5.first = f32[32,2048]{1,0:T(8,128)S(1)} collective-permute-done((f32[32,2048]{1,0:T(8,128)S(1)}, f32[32,2048]{1,0:T(8,128)S(1)}, u32[]{:S(2)}, u32[]{:S(2)}) %collective-permute-start.5) | collective-permute-done | bytes 262176 | tf_op jit(solution)/shard_map/ppermute | solution.py:26
  20.4 1.6 %collective-permute-start.9 = (f32[64,2048]{1,0:T(8,128)S(1)}, f32[64,2048]{1,0:T(8,128)S(1)}, u32[]{:S(2)}, u32[]{:S(2)}) collective-permute-start(f32[64,2048]{1,0:T(8,128)S(1)} %shard_map.63.refs_1_), channel_id=1, source_target_pairs={{0,24},{1,7},{2,26},{3,5},{4,28},{5,3},{6,30},{7,1},{8,16},{9,15},... | collective-permute-start | bytes 1572872 | tf_op jit(solution)/shard_map/ppermute | solution.py:26
  22.0 7.0 %collective-permute-start.15 = (f32[64,2048]{1,0:T(8,128)S(1)}, f32[64,2048]{1,0:T(8,128)S(1)}, u32[]{:S(2)}, u32[]{:S(2)}) collective-permute-start(f32[64,2048]{1,0:T(8,128)S(1)} %shard_map.60.refs_0_), channel_id=1, source_target_pairs={{0,1},{1,0},{2,3},{3,2},{4,5},{5,4},{6,7},{7,6},{8,9},{9,8},{10,11... | collective-permute-start | bytes 1572872 | tf_op jit(solution)/shard_map/ppermute | solution.py:77
  29.5 1.6 %collective-permute-start.4 = (f32[32,2048]{1,0:T(8,128)S(1)}, f32[32,2048]{1,0:T(8,128)S(1)}, u32[]{:S(2)}, u32[]{:S(2)}) collective-permute-start(f32[32,2048]{1,0:T(8,128)S(1)} %shard_map.62), channel_id=1, source_target_pairs={{0,24},{1,7},{2,26},{3,5},{4,28},{5,3},{6,30},{7,1},{8,16},{9,15},... | collective-permute-start | bytes 786440 | tf_op jit(solution)/shard_map/ppermute | solution.py:26
  31.1 2.6 %collective-permute-done.9.both.refs_5_ = f32[64,2048]{1,0:T(8,128)S(1)} collective-permute-done((f32[64,2048]{1,0:T(8,128)S(1)}, f32[64,2048]{1,0:T(8,128)S(1)}, u32[]{:S(2)}, u32[]{:S(2)}) %collective-permute-start.9) | collective-permute-done | bytes 524320 | tf_op jit(solution)/shard_map/ppermute | solution.py:26
  35.3 4.1 %collective-permute-start.17 = (f32[64,2048]{1,0:T(8,128)S(1)}, f32[64,2048]{1,0:T(8,128)S(1)}, u32[]{:S(2)}, u32[]{:S(2)}) collective-permute-start(f32[64,2048]{1,0:T(8,128)S(1)} %collective-permute-done.3.both.refs_2_), channel_id=1, source_target_pairs={{0,1},{1,0},{2,3},{3,2},{4,5},{5,4},{6,7},{7,6},{8,9},{9,8},{10,11... | collective-permute-start | bytes 1572872 | tf_op jit(solution)/shard_map/ppermute | solution.py:77
  40.1 2.0 %collective-permute-start.8 = (f32[32,2048]{1,0:T(8,128)S(1)}, f32[32,2048]{1,0:T(8,128)S(1)}, u32[]{:S(2)}, u32[]{:S(2)}) collective-permute-start(f32[32,2048]{1,0:T(8,128)S(1)} %shard_map.64), channel_id=1, source_target_pairs={{0,24},{1,7},{2,26},{3,5},{4,28},{5,3},{6,30},{7,1},{8,16},{9,15},... | collective-permute-start | bytes 786440 | tf_op jit(solution)/shard_map/ppermute | solution.py:26
  43.0 3.4 %collective-permute-start.19 = (f32[64,2048]{1,0:T(8,128)S(1)}, f32[64,2048]{1,0:T(8,128)S(1)}, u32[]{:S(2)}, u32[]{:S(2)}) collective-permute-start(f32[64,2048]{1,0:T(8,128)S(1)} %collective-permute-done.7.both.refs_4_), channel_id=1, source_target_pairs={{0,1},{1,0},{2,3},{3,2},{4,5},{5,4},{6,7},{7,6},{8,9},{9,8},{10,11... | collective-permute-start | bytes 1572872 | tf_op jit(solution)/shard_map/ppermute | solution.py:77
  46.6 4.6 %collective-permute-start.12 = (f32[32,2048]{1,0:T(8,128)S(1)}, f32[32,2048]{1,0:T(8,128)S(1)}, u32[]{:S(2)}, u32[]{:S(2)}) collective-permute-start(f32[32,2048]{1,0:T(8,128)S(1)} %collective-permute-done.4.refs_1_), channel_id=1, source_target_pairs={{0,1},{1,0},{2,3},{3,2},{4,5},{5,4},{6,7},{7,6},{8,9},{9,8},{10,11... | collective-permute-start | bytes 786440 | tf_op jit(solution)/shard_map/ppermute | solution.py:77
  54.6 1.8 %shard_map.69 = f32[8,1024]{1,0:T(8,128)S(1)} custom-call(bf16[1024,1024]{1,0:T(8,128)(2,1)S(1)} %get-tuple-element.25.d_high, bf16[1024,1024]{1,0:T(8,128)(2,1)S(1)} %get-tuple-element.26.d_low, bf16[1024,1024]{1,0:T(8,128)(2,1)S(1)} %get-tuple-element.27.high.c_high, bf16[1024,1024]{1,0:T(8,128)(2,1)S(1)} %get-tuple-element.28.low.c_low, ...), custom_call_target="tpu_custom_call" | custom-call | tf_op jit(solution)/shard_map/pallas_call | solution.py:302
  56.4 2.8 %collective-permute-done.21.refs_0_ = f32[8,1024]{1,0:T(8,128)S(1)} collective-permute-done((f32[8,1024]{1,0:T(8,128)S(1)}, f32[8,1024]{1,0:T(8,128)S(1)}, u32[]{:S(2)}, u32[]{:S(2)}) %collective-permute-start.21) | collective-permute-done | bytes 32800 | tf_op jit(solution)/shard_map/ppermute | solution.py:216
  60.0 3.2 %collective-permute-done.22.refs_0_.refs_1_ = f32[8,1024]{1,0:T(8,128)S(1)} collective-permute-done((f32[8,1024]{1,0:T(8,128)S(1)}, f32[8,1024]{1,0:T(8,128)S(1)}, u32[]{:S(2)}, u32[]{:S(2)}) %collective-permute-start.22) | collective-permute-done | bytes 32800 | tf_op jit(solution)/shard_map/ppermute | solution.py:216
  63.8 2.2 %collective-permute-done.23.refs_2_ = f32[8,1024]{1,0:T(8,128)S(1)} collective-permute-done((f32[8,1024]{1,0:T(8,128)S(1)}, f32[8,1024]{1,0:T(8,128)S(1)}, u32[]{:S(2)}, u32[]{:S(2)}) %collective-permute-start.23) | collective-permute-done | bytes 32800 | tf_op jit(solution)/shard_map/ppermute | solution.py:216
  69.2 2.3 %collective-permute-start.25 = (f32[8,1024]{1,0:T(8,128)S(1)}, f32[8,1024]{1,0:T(8,128)S(1)}, u32[]{:S(2)}, u32[]{:S(2)}) collective-permute-start(f32[8,1024]{1,0:T(8,128)S(1)} %shard_map.73), channel_id=1, source_target_pairs={{64,32},{32,64},{0,96},{96,0},{65,33},{33,65},{1,97},{97,1},{66,34... | collective-permute-start | bytes 98312 | tf_op jit(solution)/shard_map/ppermute | solution.py:216
  71.5 1.7 %collective-permute-done.25.ahead.refs_1_ = f32[8,1024]{1,0:T(8,128)S(1)} collective-permute-done((f32[8,1024]{1,0:T(8,128)S(1)}, f32[8,1024]{1,0:T(8,128)S(1)}, u32[]{:S(2)}, u32[]{:S(2)}) %collective-permute-start.25) | collective-permute-done | bytes 32800 | tf_op jit(solution)/shard_map/ppermute | solution.py:216
  73.2 3.0 %collective-permute-start.26 = (f32[8,1024]{1,0:T(8,128)S(1)}, f32[8,1024]{1,0:T(8,128)S(1)}, u32[]{:S(2)}, u32[]{:S(2)}) collective-permute-start(f32[8,1024]{1,0:T(8,128)S(1)} %shard_map.74), channel_id=1, source_target_pairs={{32,0},{0,32},{64,96},{96,64},{33,1},{1,33},{65,97},{97,65},{34,2}... | collective-permute-start | bytes 98312 | tf_op jit(solution)/shard_map/ppermute | solution.py:216
  77.4 2.1 %shard_map.75 = f32[32,8,128]{2,1,0:T(8,128)S(1)} custom-call(bf16[1024,1024]{1,0:T(8,128)(2,1)S(1)} %get-tuple-element.25.d_high, bf16[1024,1024]{1,0:T(8,128)(2,1)S(1)} %get-tuple-element.26.d_low, bf16[1024,1024]{1,0:T(8,128)(2,1)S(1)} %get-tuple-element.29.c_high, bf16[1024,1024]{1,0:T(8,128)(2,1)S(1)} %get-tuple-element.30.c_low, ...), custom_call_target="tpu_custom_call" | custom-call | tf_op jit(solution)/shard_map/pallas_call | solution.py:302
  79.5 18.9 %all_to_all.5 = f32[32,8,128]{2,1,0:T(8,128)S(1)} all-to-all(f32[32,8,128]{2,1,0:T(8,128)S(1)} %shard_map.75), channel_id=1, replica_groups=mesh['depth'=4,'panel'=32] {'panel'}, dimensions={0} | all-to-all | bytes 262144 | tf_op jit(solution)/shard_map/all_to_all | solution.py:372
  (49 shorter events, 15.6 us)
Async XLA Ops:
  1.6 6.3 %collective-permute-start = (f32[32,2048]{1,0:T(8,128)S(1)}, f32[32,2048]{1,0:T(8,128)S(1)}, u32[]{:S(2)}, u32[]{:S(2)}) collective-permute-start(f32[32,2048]{1,0:T(8,128)S(1)} %shard_map.59.first), channel_id=1, source_target_pairs={{0,2},{1,9},{2,0},{3,11},{4,6},{5,13},{6,4},{7,15},{8,10},{9,1},{1... | collective-permute-start | bytes 786440 | tf_op jit(solution)/shard_map/ppermute | solution.py:26
  7.9 21.1 %collective-permute-start.3 = (f32[64,2048]{1,0:T(8,128)S(1)}, f32[64,2048]{1,0:T(8,128)S(1)}, u32[]{:S(2)}, u32[]{:S(2)}) collective-permute-start(f32[64,2048]{1,0:T(8,128)S(1)} %shard_map.60.refs_0_), channel_id=1, source_target_pairs={{0,8},{1,3},{2,10},{3,1},{4,12},{5,7},{6,14},{7,5},{8,0},{9,11},{1... | collective-permute-start | bytes 1572872 | tf_op jit(solution)/shard_map/ppermute | solution.py:26
  9.8 9.0 %collective-permute-start.6 = (f32[32,2048]{1,0:T(8,128)S(1)}, f32[32,2048]{1,0:T(8,128)S(1)}, u32[]{:S(2)}, u32[]{:S(2)}) collective-permute-start(f32[32,2048]{1,0:T(8,128)S(1)} %shard_map.59.first), channel_id=1, source_target_pairs={{0,4},{1,17},{2,6},{3,19},{4,0},{5,21},{6,2},{7,23},{8,12},{9,25},... | collective-permute-start | bytes 786440 | tf_op jit(solution)/shard_map/ppermute | solution.py:26
  12.7 7.6 %collective-permute-start.5 = (f32[32,2048]{1,0:T(8,128)S(1)}, f32[32,2048]{1,0:T(8,128)S(1)}, u32[]{:S(2)}, u32[]{:S(2)}) collective-permute-start(f32[32,2048]{1,0:T(8,128)S(1)} %shard_map.59.first), channel_id=1, source_target_pairs={{0,6},{1,25},{2,4},{3,27},{4,2},{5,29},{6,0},{7,31},{8,14},{9,17},... | collective-permute-start | bytes 786440 | tf_op jit(solution)/shard_map/ppermute | solution.py:26
  13.5 16.0 %collective-permute-start.1 = (f32[64,2048]{1,0:T(8,128)S(1)}, f32[64,2048]{1,0:T(8,128)S(1)}, u32[]{:S(2)}, u32[]{:S(2)}) collective-permute-start(f32[64,2048]{1,0:T(8,128)S(1)} %shard_map.60.refs_0_), channel_id=1, source_target_pairs={{0,24},{1,7},{2,26},{3,5},{4,28},{5,3},{6,30},{7,1},{8,16},{9,15},... | collective-permute-start | bytes 1572872 | tf_op jit(solution)/shard_map/ppermute | solution.py:26
  20.4 13.3 %collective-permute-start.9 = (f32[64,2048]{1,0:T(8,128)S(1)}, f32[64,2048]{1,0:T(8,128)S(1)}, u32[]{:S(2)}, u32[]{:S(2)}) collective-permute-start(f32[64,2048]{1,0:T(8,128)S(1)} %shard_map.63.refs_1_), channel_id=1, source_target_pairs={{0,24},{1,7},{2,26},{3,5},{4,28},{5,3},{6,30},{7,1},{8,16},{9,15},... | collective-permute-start | bytes 1572872 | tf_op jit(solution)/shard_map/ppermute | solution.py:26
  22.0 12.5 %collective-permute-start.15 = (f32[64,2048]{1,0:T(8,128)S(1)}, f32[64,2048]{1,0:T(8,128)S(1)}, u32[]{:S(2)}, u32[]{:S(2)}) collective-permute-start(f32[64,2048]{1,0:T(8,128)S(1)} %shard_map.60.refs_0_), channel_id=1, source_target_pairs={{0,1},{1,0},{2,3},{3,2},{4,5},{5,4},{6,7},{7,6},{8,9},{9,8},{10,11... | collective-permute-start | bytes 1572872 | tf_op jit(solution)/shard_map/ppermute | solution.py:77
  29.0 6.3 %collective-permute-start.16 = (f32[64,2048]{1,0:T(8,128)S(1)}, f32[64,2048]{1,0:T(8,128)S(1)}, u32[]{:S(2)}, u32[]{:S(2)}) collective-permute-start(f32[64,2048]{1,0:T(8,128)S(1)} %shard_map.63.refs_1_), channel_id=1, source_target_pairs={{0,1},{1,0},{2,3},{3,2},{4,5},{5,4},{6,7},{7,6},{8,9},{9,8},{10,11... | collective-permute-start | bytes 1572872 | tf_op jit(solution)/shard_map/ppermute | solution.py:77
  29.0 10.3 %collective-permute-start.7 = (f32[64,2048]{1,0:T(8,128)S(1)}, f32[64,2048]{1,0:T(8,128)S(1)}, u32[]{:S(2)}, u32[]{:S(2)}) collective-permute-start(f32[64,2048]{1,0:T(8,128)S(1)} %shard_map.63.refs_1_), channel_id=1, source_target_pairs={{0,8},{1,3},{2,10},{3,1},{4,12},{5,7},{6,14},{7,5},{8,0},{9,11},{1... | collective-permute-start | bytes 1572872 | tf_op jit(solution)/shard_map/ppermute | solution.py:26
  29.5 10.0 %collective-permute-start.4 = (f32[32,2048]{1,0:T(8,128)S(1)}, f32[32,2048]{1,0:T(8,128)S(1)}, u32[]{:S(2)}, u32[]{:S(2)}) collective-permute-start(f32[32,2048]{1,0:T(8,128)S(1)} %shard_map.62), channel_id=1, source_target_pairs={{0,24},{1,7},{2,26},{3,5},{4,28},{5,3},{6,30},{7,1},{8,16},{9,15},... | collective-permute-start | bytes 786440 | tf_op jit(solution)/shard_map/ppermute | solution.py:26
  33.7 6.4 %collective-permute-start.2 = (f32[32,2048]{1,0:T(8,128)S(1)}, f32[32,2048]{1,0:T(8,128)S(1)}, u32[]{:S(2)}, u32[]{:S(2)}) collective-permute-start(f32[32,2048]{1,0:T(8,128)S(1)} %shard_map.61), channel_id=1, source_target_pairs={{0,8},{1,3},{2,10},{3,1},{4,12},{5,7},{6,14},{7,5},{8,0},{9,11},{1... | collective-permute-start | bytes 786440 | tf_op jit(solution)/shard_map/ppermute | solution.py:26
  34.5 8.4 %collective-permute-start.10 = (f32[32,2048]{1,0:T(8,128)S(1)}, f32[32,2048]{1,0:T(8,128)S(1)}, u32[]{:S(2)}, u32[]{:S(2)}) collective-permute-start(f32[32,2048]{1,0:T(8,128)S(1)} %shard_map.65), channel_id=1, source_target_pairs={{0,8},{1,3},{2,10},{3,1},{4,12},{5,7},{6,14},{7,5},{8,0},{9,11},{1... | collective-permute-start | bytes 786440 | tf_op jit(solution)/shard_map/ppermute | solution.py:26
  35.3 15.9 %collective-permute-start.17 = (f32[64,2048]{1,0:T(8,128)S(1)}, f32[64,2048]{1,0:T(8,128)S(1)}, u32[]{:S(2)}, u32[]{:S(2)}) collective-permute-start(f32[64,2048]{1,0:T(8,128)S(1)} %collective-permute-done.3.both.refs_2_), channel_id=1, source_target_pairs={{0,1},{1,0},{2,3},{3,2},{4,5},{5,4},{6,7},{7,6},{8,9},{9,8},{10,11... | collective-permute-start | bytes 1572872 | tf_op jit(solution)/shard_map/ppermute | solution.py:77
  39.4 11.8 %collective-permute-start.18 = (f32[64,2048]{1,0:T(8,128)S(1)}, f32[64,2048]{1,0:T(8,128)S(1)}, u32[]{:S(2)}, u32[]{:S(2)}) collective-permute-start(f32[64,2048]{1,0:T(8,128)S(1)} %collective-permute-done.1.both.refs_3_), channel_id=1, source_target_pairs={{0,1},{1,0},{2,3},{3,2},{4,5},{5,4},{6,7},{7,6},{8,9},{9,8},{10,11... | collective-permute-start | bytes 1572872 | tf_op jit(solution)/shard_map/ppermute | solution.py:77
  39.5 12.2 %collective-permute-start.20 = (f32[64,2048]{1,0:T(8,128)S(1)}, f32[64,2048]{1,0:T(8,128)S(1)}, u32[]{:S(2)}, u32[]{:S(2)}) collective-permute-start(f32[64,2048]{1,0:T(8,128)S(1)} %collective-permute-done.9.both.refs_5_), channel_id=1, source_target_pairs={{0,1},{1,0},{2,3},{3,2},{4,5},{5,4},{6,7},{7,6},{8,9},{9,8},{10,11... | collective-permute-start | bytes 1572872 | tf_op jit(solution)/shard_map/ppermute | solution.py:77
  40.1 6.5 %collective-permute-start.8 = (f32[32,2048]{1,0:T(8,128)S(1)}, f32[32,2048]{1,0:T(8,128)S(1)}, u32[]{:S(2)}, u32[]{:S(2)}) collective-permute-start(f32[32,2048]{1,0:T(8,128)S(1)} %shard_map.64), channel_id=1, source_target_pairs={{0,24},{1,7},{2,26},{3,5},{4,28},{5,3},{6,30},{7,1},{8,16},{9,15},... | collective-permute-start | bytes 786440 | tf_op jit(solution)/shard_map/ppermute | solution.py:26
  43.0 8.8 %collective-permute-start.19 = (f32[64,2048]{1,0:T(8,128)S(1)}, f32[64,2048]{1,0:T(8,128)S(1)}, u32[]{:S(2)}, u32[]{:S(2)}) collective-permute-start(f32[64,2048]{1,0:T(8,128)S(1)} %collective-permute-done.7.both.refs_4_), channel_id=1, source_target_pairs={{0,1},{1,0},{2,3},{3,2},{4,5},{5,4},{6,7},{7,6},{8,9},{9,8},{10,11... | collective-permute-start | bytes 1572872 | tf_op jit(solution)/shard_map/ppermute | solution.py:77
  46.6 6.6 %collective-permute-start.12 = (f32[32,2048]{1,0:T(8,128)S(1)}, f32[32,2048]{1,0:T(8,128)S(1)}, u32[]{:S(2)}, u32[]{:S(2)}) collective-permute-start(f32[32,2048]{1,0:T(8,128)S(1)} %collective-permute-done.4.refs_1_), channel_id=1, source_target_pairs={{0,1},{1,0},{2,3},{3,2},{4,5},{5,4},{6,7},{7,6},{8,9},{9,8},{10,11... | collective-permute-start | bytes 786440 | tf_op jit(solution)/shard_map/ppermute | solution.py:77
  56.4 2.8 %collective-permute-start.21 = (f32[8,1024]{1,0:T(8,128)S(1)}, f32[8,1024]{1,0:T(8,128)S(1)}, u32[]{:S(2)}, u32[]{:S(2)}) collective-permute-start(f32[8,1024]{1,0:T(8,128)S(1)} %shard_map.69), channel_id=1, source_target_pairs={{0,32},{32,0},{64,96},{96,64},{1,33},{33,1},{65,97},{97,65},{2,34}... | collective-permute-start | bytes 98312 | tf_op jit(solution)/shard_map/ppermute | solution.py:216
  59.2 4.0 %collective-permute-start.22 = (f32[8,1024]{1,0:T(8,128)S(1)}, f32[8,1024]{1,0:T(8,128)S(1)}, u32[]{:S(2)}, u32[]{:S(2)}) collective-permute-start(f32[8,1024]{1,0:T(8,128)S(1)} %shard_map.70), channel_id=1, source_target_pairs={{32,64},{64,32},{0,96},{96,0},{33,65},{65,33},{1,97},{97,1},{34,66... | collective-permute-start | bytes 98312 | tf_op jit(solution)/shard_map/ppermute | solution.py:216
  63.2 2.8 %collective-permute-start.23 = (f32[8,1024]{1,0:T(8,128)S(1)}, f32[8,1024]{1,0:T(8,128)S(1)}, u32[]{:S(2)}, u32[]{:S(2)}) collective-permute-start(f32[8,1024]{1,0:T(8,128)S(1)} %shard_map.71), channel_id=1, source_target_pairs={{64,96},{96,64},{0,32},{32,0},{65,97},{97,65},{1,33},{33,1},{66,98... | collective-permute-start | bytes 98312 | tf_op jit(solution)/shard_map/ppermute | solution.py:216
  66.0 3.2 %collective-permute-start.24 = (f32[8,1024]{1,0:T(8,128)S(1)}, f32[8,1024]{1,0:T(8,128)S(1)}, u32[]{:S(2)}, u32[]{:S(2)}) collective-permute-start(f32[8,1024]{1,0:T(8,128)S(1)} %get-tuple-element.35), channel_id=1, source_target_pairs={{96,64},{64,96},{0,32},{32,0},{97,65},{65,97},{1,33},{33,1},{98,66... | collective-permute-start | bytes 98312 | tf_op jit(solution)/shard_map/ppermute | solution.py:216
  69.2 4.0 %collective-permute-start.25 = (f32[8,1024]{1,0:T(8,128)S(1)}, f32[8,1024]{1,0:T(8,128)S(1)}, u32[]{:S(2)}, u32[]{:S(2)}) collective-permute-start(f32[8,1024]{1,0:T(8,128)S(1)} %shard_map.73), channel_id=1, source_target_pairs={{64,32},{32,64},{0,96},{96,0},{65,33},{33,65},{1,97},{97,1},{66,34... | collective-permute-start | bytes 98312 | tf_op jit(solution)/shard_map/ppermute | solution.py:216
  73.2 4.3 %collective-permute-start.26 = (f32[8,1024]{1,0:T(8,128)S(1)}, f32[8,1024]{1,0:T(8,128)S(1)}, u32[]{:S(2)}, u32[]{:S(2)}) collective-permute-start(f32[8,1024]{1,0:T(8,128)S(1)} %shard_map.74), channel_id=1, source_target_pairs={{32,0},{0,32},{64,96},{96,64},{33,1},{1,33},{65,97},{97,65},{34,2}... | collective-permute-start | bytes 98312 | tf_op jit(solution)/shard_map/ppermute | solution.py:216
  (3 other events, 5.7 us)
